TPU v7x, 32 devices: a whole 2x2x4 slice. The times are simulated.
32 devices in a mesh: dp: 8 (over z, y), tensor: 4 (over x, core).
Axes of the slice: x: 2, y: 2, z: 4, core: 2. Of those that a mesh axis runs over, the one named last changes fastest.
Arguments:
- inputs: bfloat16 [4096, 768], P(('dp', 'tensor')), may hold values from -6 to 6
- prev_logits: bfloat16 [4096, 12, 4096], P('dp', 'tensor'), may hold values from -6 to 6
- w_query: bfloat16 [768, 768], P('dp', 'tensor'), may hold values from -0.21875 to 0.21875
- w_key: bfloat16 [768, 768], P('dp', 'tensor'), may hold values from -0.21875 to 0.21875
- w_value: bfloat16 [768, 768], P('dp', 'tensor'), may hold values from -0.21875 to 0.21875
- w_attn_out: bfloat16 [768, 768], P('tensor', 'dp'), may hold values from -2.5 to 2.5
- w_ffn_in: bfloat16 [768, 3072], P('dp', 'tensor'), may hold values from -0.21875 to 0.21875
- ffn_bias: bfloat16 [3072], P(('tensor', 'dp')), may hold values from -3 to 3
- w_ffn_out: bfloat16 [3072, 768], P(('tensor', 'dp')), may hold values from -0.109375 to 0.109375
- norm1_gain: float32 [768], replicated, may hold values from 0.5 to 1.5
- norm1_shift: float32 [768], replicated, may hold values from -2 to 2
- norm2_gain: float32 [768], replicated, may hold values from 0.5 to 1.5
- norm2_shift: float32 [768], replicated, may hold values from -2 to 2
- token_segment: int32 [4096], replicated, may hold values from 0 to 12, as said below
- segment_parent: int32 [1, 13], replicated, may hold values from 0 to 4, as said below
- out_grad: bfloat16 [4096, 768], P(('dp', 'tensor')), may hold values from -6 to 6
- logit_grad: bfloat16 [4096, 12, 4096], P('dp', 'tensor'), may hold values from -6 to 6
Outputs:
- output: bfloat16 [4096, 768], P(('dp', 'tensor'))
- logits: bfloat16 [4096, 12, 4096], P('dp', 'tensor')
- input_grad: float32 [4096, 768], P(('dp', 'tensor'))
- prev_grad: bfloat16 [4096, 12, 4096], P('dp', 'tensor')
- w_query_grad: float32 [768, 768], P('dp', 'tensor')
- w_key_grad: float32 [768, 768], P('dp', 'tensor')
- w_value_grad: float32 [768, 768], P('dp', 'tensor')
- w_attn_out_grad: float32 [768, 768], P('tensor', 'dp')
- w_ffn_in_grad: float32 [768, 3072], P('dp', 'tensor')
- ffn_bias_grad: float32 [3072], P(('tensor', 'dp'))
- w_ffn_out_grad: float32 [3072, 768], P(('tensor', 'dp'))
- norm1_gain_grad: float32 [768], replicated
- norm1_shift_grad: float32 [768], replicated
- norm2_gain_grad: float32 [768], replicated
- norm2_shift_grad: float32 [768], replicated
Inputs may be any that keep to these rules, and one draw needn't show every extreme that they name: `token_segment`: in each tree the first 2048 tokens are segment 0, the trunk; the other tokens hold the 4 branches (segments 1 to 4, 256 tokens each) and the 8 leaves (segments 5 to 12, 128 tokens each), each segment one contiguous run, in an order that varies from tree to tree. `segment_parent`: row t lists the parents of tree t's segments: 0 for the trunk and every branch, a branch for every leaf, each branch the parent of exactly two leaves.
All inputs are finite; a program needn't handle non-finite values.
Results may differ from a plain program's by a relative error of at most 0.017.
Values may be sent and summed in bfloat16 or wider, within the bound.
No kernel may reach another device: no remote copies, remote signals or barrier semaphores. Data moves between devices by JAX's collectives and lax.ppermute only.
A program may use at most 256 MiB of HBM per device.

v0:
```python
import functools
import math

import jax
import jax.numpy as jnp
from jax import lax
from jax.experimental import pallas as pl
from jax.experimental.pallas import tpu as pltpu
from jax.sharding import PartitionSpec as P

E = 64
SPARE = 8 << 20
TRUNK = 2048
BLOCK = 128
EPSILON = 1e-12
LOW = -1e30

BF = jnp.bfloat16
F32 = jnp.float32


def layer_norm(values, norm_gain, norm_shift):
    center = values - jnp.mean(values, axis=-1, keepdims=True)
    spread = jnp.mean(center * center, axis=-1, keepdims=True)
    return center * lax.rsqrt(spread + EPSILON) * norm_gain + norm_shift


def size_of(*arrays):
    return sum(math.prod(a.shape) * jnp.dtype(a.dtype).itemsize for a in arrays)


def apart(x):
    return pltpu.with_memory_space_constraint(x, pltpu.HBM)


def contract(a, b, da, db):
    return lax.dot_general(a, b, (((da,), (db,)), ((), ())), preferred_element_type=F32)


def block_mask(shard, rows, act_ref, q_blocks):
    nb = rows // BLOCK
    total_blocks = act_ref.shape[0] // nb
    parts = []
    for qi in q_blocks:
        flags = [act_ref[qi * total_blocks + shard * nb + ki].astype(F32) for ki in range(nb)]
        line = jnp.concatenate([jnp.full((1, BLOCK), f, F32) for f in flags], axis=1)
        parts.append(jnp.broadcast_to(line, (BLOCK, rows)))
    return jnp.concatenate(parts, axis=0)


def in_use(shard, rows, act_ref):
    nb = rows // BLOCK
    total_blocks = act_ref.shape[0] // nb
    flags = [act_ref[qi * total_blocks + shard * nb + ki] for qi in range(nb) for ki in range(nb)]
    return functools.reduce(jnp.maximum, flags) == 1


def tile_of(ref, head, shard, rows):
    return ref.at[head, :, pl.ds(pl.multiple_of(shard * rows, BLOCK), rows)]


def read_pieces(pieces, parted, refs):
    if parted:
        return [(lambda rs: refs[0][0, rs, :], lambda rs: refs[1][0, rs, :])], refs[2:]
    return [
        (lambda rs, ref=ref: ref[0, rs, :], lambda rs, ref=ref: ref[1, rs, :]) for ref in refs[:pieces]
    ], refs[pieces:]


def forward_kernel(first, last, pieces, parted, base, rc, *refs):
    sid_ref, act_ref, q_ref = refs[:3]
    readers, refs = read_pieces(pieces, parted, refs[3:])
    prev_ref, refs = refs[0], refs[1:]
    if not first:
        carry_in, refs = refs[1], refs[2:]
    logit_ref, refs = refs[0], refs[1:]
    if last:
        mix_ref, refs = refs[0], refs[1:]
    out_ref, m_s, acc_s, q_s, kv_s, prev_s, logit_s, in_sem, out_sem = refs
    heads, rows, _ = prev_ref.shape
    count = pieces * heads

    def incoming(i):
        tile = tile_of(prev_ref, i % heads, sid_ref[base + i // heads], rows)
        return pltpu.make_async_copy(tile, prev_s.at[i], in_sem.at[i])

    def outgoing(i):
        tile = tile_of(logit_ref, i % heads, sid_ref[base + i // heads], rows)
        return pltpu.make_async_copy(logit_s.at[i], tile, out_sem.at[i])

    def used(i):
        return in_use(sid_ref[base + i // heads], rows, act_ref)

    @pl.loop(0, count)
    def _(i):
        @pl.when(used(i))
        def _():
            incoming(i).start()

    for h in range(heads):
        feature = slice(h * E, (h + 1) * E)
        q_s[h] = q_ref[feature, :].astype(F32).T.astype(BF)
        for p, (keys, values) in enumerate(readers):
            kv_s[p * heads + h, :E, :] = values(feature)
            kv_s[p * heads + h, E : 2 * E, :] = jnp.ones((E, rows), BF)
            kv_s[p * heads + h, 2 * E :, :] = keys(feature)
        if first:
            m_s[h] = jnp.full((rows, 1), LOW, F32)
            acc_s[h] = jnp.zeros((rows, 2 * E), F32)
        else:
            m_s[h] = carry_in[h, :, 96:97]
            acc_s[h] = carry_in[h]

    @pl.loop(0, count)
    def _(i):
        shard, h, here = sid_ref[base + i // heads], i % heads, used(i)

        @pl.when(here)
        def _():
            incoming(i).wait()

            for r0 in range(0, rows, min(rc, rows)):
                rs = slice(r0, r0 + min(rc, rows))
                on = block_mask(shard, rows, act_ref, range(r0 // BLOCK, rs.stop // BLOCK))
                s = contract(q_s[h, rs, :], kv_s[i, 2 * E :, :], 1, 0) + prev_s[i, rs, :].astype(F32)
                logit_s[i, rs, :] = (s * on).astype(BF)
                s = s + (on - 1.0) * (-LOW)
                m_old = m_s[h, rs, :]
                m_new = jnp.maximum(m_old, jnp.max(s, axis=1, keepdims=True))
                weight = jnp.exp(s - m_new).astype(BF)
                fix = jnp.exp(m_old - m_new)
                m_s[h, rs, :] = m_new
                acc_s[h, rs, :] = acc_s[h, rs, :] * fix + contract(weight, kv_s[i, : 2 * E, :], 1, 1)

        @pl.when(jnp.logical_not(here))
        def _():
            logit_s[i] = jnp.zeros((rows, rows), BF)

        outgoing(i).start()

    for h in range(heads):
        if last:
            total = acc_s[h, :, E : E + 1]
            out = acc_s[h, :, :E] / total
            mix_ref[h * E : (h + 1) * E, :] = out.T.astype(BF)
            out_ref[h, :, :E] = out
            out_ref[h, :, E:] = jnp.broadcast_to(m_s[h] + jnp.log(total), (rows, 128 - E))
        else:
            out_ref[h, :, :96] = acc_s[h, :, :96]
            out_ref[h, :, 96:] = jnp.broadcast_to(m_s[h], (rows, 32))

    @pl.loop(0, count)
    def _(i):
        outgoing(i).wait()


def attend_forward(sid, base, act, q_t, kvs, prev, carry, last, rc=256):
    heads, rows, length = prev.shape
    first, parted = carry is None, kvs[0].shape[0] == 1
    pieces = 1 if parted else len(kvs)
    scalars = pl.BlockSpec(memory_space=pltpu.SMEM)
    whole = pl.BlockSpec(memory_space=pltpu.VMEM)
    left = pl.BlockSpec(memory_space=pltpu.HBM)
    in_specs = [scalars, scalars, whole] + [whole] * len(kvs) + [left]
    args = [sid, act, q_t, *kvs, prev]
    aliases = {}
    if not first:
        aliases = {len(args): 0}
        in_specs += [left, whole]
        args += list(carry)
    out_shape = [jax.ShapeDtypeStruct((heads, rows, length), BF)]
    if last:
        out_shape.append(jax.ShapeDtypeStruct((heads * E, rows), BF))
    out_shape.append(jax.ShapeDtypeStruct((heads, rows, 128), F32))
    work = heads * pieces * rows * rows
    return pl.pallas_call(
        functools.partial(forward_kernel, first, last, pieces, parted, base, rc),
        out_shape=out_shape,
        in_specs=in_specs,
        out_specs=[left] + [whole] * (len(out_shape) - 1),
        scratch_shapes=[
            pltpu.VMEM((heads, rows, 1), F32),
            pltpu.VMEM((heads, rows, 128), F32),
            pltpu.VMEM((heads, rows, E), BF),
            pltpu.VMEM((pieces * heads, 3 * E, rows), BF),
            pltpu.VMEM((pieces * heads, rows, rows), BF),
            pltpu.VMEM((pieces * heads, rows, rows), BF),
            pltpu.SemaphoreType.DMA((pieces * heads,)),
            pltpu.SemaphoreType.DMA((pieces * heads,)),
        ],
        input_output_aliases=aliases,
        cost_estimate=pl.CostEstimate(flops=4 * E * work, transcendentals=work, bytes_accessed=4 * work),
        compiler_params=pltpu.CompilerParams(
            vmem_limit_bytes=6 * work + 16 * heads * rows * 128 * 4 + SPARE
        ),
    )(*args)


def backward_kernel(first, last, pieces, parted, base, rc, *refs):
    sid_ref, act_ref, q_ref, do_ref, aux_ref = refs[:5]
    readers, refs = read_pieces(pieces, parted, refs[5:])
    prev_ref, up_ref, refs = refs[0], refs[1], refs[2:]
    if not first:
        gq_in, refs = refs[1], refs[2:]
    outputs = 2 if parted else pieces
    pg_ref, gkv_refs = refs[0], refs[1 : 1 + outputs]
    gq_ref, q_s, do_s, d_s, lse_s, gq_s, p_s, kv_s, gkv_s, prev_s, up_s, pg_s, prev_sem, up_sem, out_sem = refs[1 + outputs :]
    heads, rows, _ = prev_ref.shape
    count = pieces * heads

    def incoming(i):
        at = i % heads, sid_ref[base + i // heads], rows
        return (
            pltpu.make_async_copy(tile_of(prev_ref, *at), prev_s.at[i], prev_sem.at[i]),
            pltpu.make_async_copy(tile_of(up_ref, *at), up_s.at[i], up_sem.at[i]),
        )

    def outgoing(i):
        tile = tile_of(pg_ref, i % heads, sid_ref[base + i // heads], rows)
        return pltpu.make_async_copy(pg_s.at[i], tile, out_sem.at[i])

    def used(i):
        return in_use(sid_ref[base + i // heads], rows, act_ref)

    @pl.loop(0, count)
    def _(i):
        @pl.when(used(i))
        def _():
            for copy in incoming(i):
                copy.start()

    for h in range(heads):
        feature = slice(h * E, (h + 1) * E)
        q_s[h] = q_ref[feature, :].astype(F32).T.astype(BF)
        do = do_ref[feature, :].astype(F32).T
        do_s[h] = do.astype(BF)
        d_s[h] = jnp.sum(do * aux_ref[h, :, :E], axis=1, keepdims=True)
        lse_s[h] = aux_ref[h, :, E : E + 1]
        gq_s[h] = jnp.zeros((rows, E), F32) if first else gq_in[h]
        for p, (keys, values) in enumerate(readers):
            kv_s[p * heads + h, :E, :] = keys(feature)
            kv_s[p * heads + h, E:, :] = values(feature)

    @pl.loop(0, count)
    def _(i):
        shard, h, here = sid_ref[base + i // heads], i % heads, used(i)
        feature = pl.ds(pl.multiple_of(h * E, E), E)

        @pl.when(here)
        def _():
            for copy in incoming(i):
                copy.wait()
            for r0 in range(0, rows, min(rc, rows)):
                rs = slice(r0, r0 + min(rc, rows))
                on = block_mask(shard, rows, act_ref, range(r0 // BLOCK, rs.stop // BLOCK))
                s = contract(q_s[h, rs, :], kv_s[i, :E, :], 1, 0) + prev_s[i, rs, :].astype(F32)
                weight = jnp.exp(s - lse_s[h, rs, :] + (on - 1.0) * (-LOW))
                dp = contract(do_s[h, rs, :], kv_s[i, E:, :], 1, 0)
                upper = up_s[i, rs, :].astype(F32) * on
                pg_s[i, rs, :] = (weight * (dp - d_s[h, rs, :]) + upper).astype(BF)
                p_s[rs, :] = weight.astype(BF)
            gkv_s[i, :E, :] = contract(q_ref[feature, :], pg_s[i], 1, 0).astype(BF)
            gkv_s[i, E:, :] = contract(do_ref[feature, :], p_s[...], 1, 0).astype(BF)
            gq_s[h] += contract(pg_s[i], kv_s[i, :E, :], 1, 1)

        @pl.when(jnp.logical_not(here))
        def _():
            pg_s[i] = jnp.zeros((rows, rows), BF)
            gkv_s[i] = jnp.zeros((2 * E, rows), BF)

        outgoing(i).start()

    for h in range(heads):
        feature = slice(h * E, (h + 1) * E)
        for p in range(pieces):
            for w in range(2):
                part = gkv_s[p * heads + h, w * E : (w + 1) * E, :]
                if parted:
                    gkv_refs[w][0, feature, :] = part
                else:
                    gkv_refs[p][w, feature, :] = part
        if last:
            gq_ref[feature, :] = (gq_s[h] * (E ** (-0.5))).T.astype(BF)
        else:
            gq_ref[h] = gq_s[h]

    @pl.loop(0, count)
    def _(i):
        outgoing(i).wait()


def attend_backward(sid, base, act, q_t, do_t, aux, kvs, prev, up, carry, last, rc=256):
    heads, rows, length = prev.shape
    first, parted = carry is None, kvs[0].shape[0] == 1
    pieces = 1 if parted else len(kvs)
    scalars = pl.BlockSpec(memory_space=pltpu.SMEM)
    whole = pl.BlockSpec(memory_space=pltpu.VMEM)
    left = pl.BlockSpec(memory_space=pltpu.HBM)
    in_specs = [scalars, scalars, whole, whole, whole] + [whole] * len(kvs) + [left, left]
    args = [sid, act, q_t, do_t, aux, *kvs, prev, up]
    aliases = {}
    if not first:
        aliases = {len(args): 0}
        in_specs += [left, whole]
        args += list(carry)
    out_shape = [jax.ShapeDtypeStruct((heads, rows, length), BF)]
    out_shape += [jax.ShapeDtypeStruct(kv.shape, BF) for kv in kvs]
    if last:
        out_shape.append(jax.ShapeDtypeStruct((heads * E, rows), BF))
    else:
        out_shape.append(jax.ShapeDtypeStruct((heads, rows, E), F32))
    work = heads * pieces * rows * rows
    return pl.pallas_call(
        functools.partial(backward_kernel, first, last, pieces, parted, base, rc),
        out_shape=out_shape,
        in_specs=in_specs,
        out_specs=[left] + [whole] * (len(kvs) + 1),
        scratch_shapes=[
            pltpu.VMEM((heads, rows, E), BF),
            pltpu.VMEM((heads, rows, E), BF),
            pltpu.VMEM((heads, rows, 1), F32),
            pltpu.VMEM((heads, rows, 1), F32),
            pltpu.VMEM((heads, rows, E), F32),
            pltpu.VMEM((rows, rows), BF),
            pltpu.VMEM((pieces * heads, 2 * E, rows), BF),
            pltpu.VMEM((pieces * heads, 2 * E, rows), BF),
            pltpu.VMEM((pieces * heads, rows, rows), BF),
            pltpu.VMEM((pieces * heads, rows, rows), BF),
            pltpu.VMEM((pieces * heads, rows, rows), BF),
            pltpu.SemaphoreType.DMA((pieces * heads,)),
            pltpu.SemaphoreType.DMA((pieces * heads,)),
            pltpu.SemaphoreType.DMA((pieces * heads,)),
        ],
        input_output_aliases=aliases,
        cost_estimate=pl.CostEstimate(flops=10 * E * work, transcendentals=work, bytes_accessed=6 * work),
        compiler_params=pltpu.CompilerParams(
            vmem_limit_bytes=8 * work + 16 * heads * rows * 128 * 4 + SPARE
        ),
    )(*args)


def fused(body, shapes, scalars, *arrays, scratch=(), flops=0):
    shapes = [jax.ShapeDtypeStruct(shape, kind) for shape, kind in shapes]
    scratch = [pltpu.VMEM(shape, kind) for shape, kind in scratch]
    return pl.pallas_call(
        body,
        out_shape=shapes,
        in_specs=[pl.BlockSpec(memory_space=pltpu.SMEM)]
        + [pl.BlockSpec(memory_space=pltpu.VMEM)] * len(arrays),
        out_specs=[pl.BlockSpec(memory_space=pltpu.VMEM)] * len(shapes),
        scratch_shapes=scratch,
        cost_estimate=pl.CostEstimate(flops=flops, transcendentals=0, bytes_accessed=1 << 20),
        compiler_params=pltpu.CompilerParams(vmem_limit_bytes=size_of(*arrays, *shapes, *scratch) + SPARE),
    )(scalars, *arrays)


def rows_at(index, count):
    return pl.ds(pl.multiple_of(index * count, count), count)


def normalize(values):
    center = values - jnp.mean(values, axis=-1, keepdims=True)
    r = lax.rsqrt(jnp.mean(center * center, axis=-1, keepdims=True) + EPSILON)
    return center * r, r


def pull_norm(n, r, gain, cotangent):
    dn = cotangent * gain
    return r * (dn - jnp.mean(dn, axis=-1, keepdims=True) - n * jnp.mean(dn * n, axis=-1, keepdims=True))


def project_kernel(pieces, s_ref, *refs):
    w_refs, x_refs = refs[: pieces + 1], refs[pieces + 1 : pieces + 5]
    rows_ref, turned_ref, q_ref, kv_ref, w_s = refs[pieces + 5 :]
    share, own = w_refs[0].shape[0], x_refs[0].shape[0]
    width = q_ref.shape[0]
    if pieces == 1:
        share *= 2
    for i in range(pieces - 1):
        w_s[rows_at(s_ref[1 + i], share), :] = w_refs[i][...]
    last = s_ref[pieces] * share
    half = share // 2
    w_s[pl.ds(pl.multiple_of(last, half), half), :] = w_refs[pieces - 1][...]
    w_s[pl.ds(pl.multiple_of(last + half, half), half), :] = w_refs[pieces][...]
    for i in range(4):
        rows_ref[rows_at(s_ref[0] ^ i, own), :] = x_refs[i][...]
    turned_ref[...] = w_s[...].astype(F32).T.astype(BF)
    projected = contract(turned_ref[: 3 * width, :], rows_ref[...], 1, 1)
    q_ref[...] = (projected[:width] * (E ** (-0.5))).astype(BF)
    kv_ref[0] = projected[width : 2 * width].astype(BF)
    kv_ref[1] = projected[2 * width :].astype(BF)


def feed_kernel(s_ref, mixed_ref, x_ref, o0, o1, o2, o3, pack_ref, out_ref, gains_ref, low_ref, active_ref, slope_ref, n_ref, r_ref, mine_ref, other_ref, o_s, part_s, n_s, r_s):
    index = s_ref[0]
    near = index % 2
    rows, model = x_ref.shape
    own, width = rows // 4, o0.shape[0]
    for i, ref in enumerate((o0, o1, o2, o3)):
        o_s[rows_at(index ^ i, width), :] = ref[...]
    bias = pack_ref[:, model:].astype(F32).T
    chunk = min(256, rows)
    for r0 in range(0, rows, chunk):
        rs = slice(r0, r0 + chunk)
        attended = contract(mixed_ref[:, rs].astype(F32).T.astype(BF), o_s[...], 1, 0)
        n, r = normalize(x_ref[rs, :].astype(F32) + attended)
        n_s[rs, :] = n
        r_s[rs, :] = jnp.broadcast_to(r, (chunk, 128))
        low = (n * gains_ref[0:1, :] + gains_ref[1:2, :]).astype(BF)
        low_ref[rs, :] = low
        inner = contract(low, pack_ref[:, :model], 1, 0) + bias
        below = 0.5 + 0.5 * lax.erf(inner * (0.5**0.5))
        density = jnp.exp(-0.5 * inner * inner) * 0.3989422804014327
        slope_ref[rs, :] = below + inner * density
        active = (inner * below).astype(BF)
        active_ref[rs, :] = active
        part_s[rs, :] = contract(active, out_ref[...], 1, 0)
    for f in range(2):
        here = slice(f * own, (f + 1) * own)
        n_ref[here, :] = n_s[rows_at(2 * f + near, own), :]
        r_ref[here, :] = r_s[rows_at(2 * f + near, own), :]
        mine_ref[here, :] = part_s[rows_at(2 * f + near, own), :].astype(BF)
        other_ref[here, :] = part_s[rows_at(2 * f + 1 - near, own), :].astype(BF)


def second_kernel(s_ref, a_ref, b_ref, n_ref, cot_own, cot_far, gains_ref, result_ref, second_ref, low_ref, sums_ref):
    far = s_ref[0] // 2
    own = cot_own.shape[0]
    gain1, shift1, gain2, shift2 = (gains_ref[i : i + 1, :] for i in range(4))
    sums = [jnp.zeros(gain2.shape, F32), jnp.zeros(gain2.shape, F32)]
    for f in range(2):
        here = slice(f * own, (f + 1) * own)
        hidden = n_ref[here, :] * gain1 + shift1
        n, r = normalize(hidden + (a_ref[here, :].astype(F32) + b_ref[here, :].astype(F32)))
        cot = jnp.where(far == f, cot_own[...].astype(F32), cot_far[...].astype(F32))

        @pl.when(far == f)
        def _():
            result_ref[...] = (n * gain2 + shift2).astype(BF)

        second = pull_norm(n, r, gain2, cot)
        second_ref[here, :] = second
        low_ref[here, :] = second.astype(BF)
        sums[0] += jnp.sum(cot * n, axis=0, keepdims=True)
        sums[1] += jnp.sum(cot, axis=0, keepdims=True)
    sums_ref[0:1, :] = sums[0]
    sums_ref[1:2, :] = sums[1]


def back_kernel(s_ref, low_ref, near_ref, slope_ref, pack_ref, out_ref, all_ref, inner_ref, bias_ref, mine_ref, other_ref, part_s):
    near = s_ref[0] % 2
    rows, model = slope_ref.shape
    own = rows // 4
    for f in range(2):
        here = slice(f * own, (f + 1) * own)
        all_ref[rows_at(2 * f + near, own), :] = low_ref[here, :]
        all_ref[rows_at(2 * f + 1 - near, own), :] = near_ref[here, :]
    chunk = min(256, rows)
    bias = jnp.zeros((1, model), F32)
    for r0 in range(0, rows, chunk):
        rs = slice(r0, r0 + chunk)
        grad = contract(all_ref[rs, :], out_ref[...], 1, 1).astype(BF).astype(F32)
        inner = (grad * slope_ref[rs, :]).astype(BF)
        inner_ref[rs, :] = inner
        bias += jnp.sum(inner.astype(F32), axis=0, keepdims=True)
        part_s[rs, :] = contract(inner, pack_ref[:, :model], 1, 1)
    bias_ref[...] = bias
    for f in range(2):
        here = slice(f * own, (f + 1) * own)
        mine_ref[here, :] = part_s[rows_at(2 * f + near, own), :].astype(BF)
        other_ref[here, :] = part_s[rows_at(2 * f + 1 - near, own), :].astype(BF)


def first_kernel(s_ref, a_ref, b_ref, second_ref, n_ref, r_ref, sums_ref, gains_ref, sent_ref, grad_ref):
    far = s_ref[0] // 2
    own = grad_ref.shape[0]
    gain = gains_ref[0:1, :]
    sums = [jnp.zeros(gain.shape, F32), jnp.zeros(gain.shape, F32)]
    for f in range(2):
        here = slice(f * own, (f + 1) * own)
        cot = second_ref[here, :] + (a_ref[here, :].astype(F32) + b_ref[here, :].astype(F32))
        n = n_ref[here, :]
        grad = pull_norm(n, r_ref[here, :1], gain, cot)

        @pl.when(far == f)
        def _():
            grad_ref[...] = grad

        sent_ref[here, :] = grad.astype(BF)
        sums[0] += jnp.sum(cot * n, axis=0, keepdims=True)
        sums[1] += jnp.sum(cot, axis=0, keepdims=True)
    sums = jnp.concatenate(sums + [sums_ref[...]], axis=0)
    high = sums.astype(BF).astype(F32)
    tail = jnp.concatenate([high, sums - high, jnp.zeros((8, sums.shape[1]), F32)], axis=0)
    sent_ref[2 * own :, :] = tail.astype(BF)


def mixed_kernel(s_ref, sent_ref, near_ref, mixed_ref, o_ref, do_ref, grad_w_ref, sums_ref, all_s):
    near = s_ref[0] % 2
    rows = all_s.shape[0]
    own = rows // 4
    for f in range(2):
        here = slice(f * own, (f + 1) * own)
        all_s[rows_at(2 * f + near, own), :] = sent_ref[here, :]
        all_s[rows_at(2 * f + 1 - near, own), :] = near_ref[here, :]
    do_ref[...] = contract(o_ref[...], all_s[...], 1, 1).astype(BF)
    grad_w_ref[...] = contract(mixed_ref[...], all_s[...], 1, 0)
    tail = sent_ref[2 * own :, :].astype(F32) + near_ref[2 * own :, :].astype(F32)
    sums = tail[:4] + tail[4:8]
    high = sums.astype(BF).astype(F32)
    sums_ref[...] = jnp.concatenate([high, sums - high, jnp.zeros((8, sums.shape[1]), F32)], axis=0).astype(BF)


def weight_kernel(s_ref, active_ref, second_ref, low_ref, inner_ref, out_ref):
    model = low_ref.shape[1]
    out_ref[:, :model] = contract(active_ref[...].astype(F32).T.astype(BF), second_ref[...], 1, 0).astype(BF)
    out_ref[:, model:] = contract(low_ref[...].astype(F32).T.astype(BF), inner_ref[...], 1, 0).astype(BF)


def join_kernel(half, s_ref, behind_ref, ahead_ref, up_ref, down_ref, up_out, down_out):
    if half:
        middle = up_ref.shape[0]
        up_out[:middle] = add(ahead_ref[:middle], up_ref[...])
        up_out[middle:] = ahead_ref[middle:]
        down_out[:middle] = behind_ref[:middle]
        down_out[middle:] = add(behind_ref[middle:], down_ref[...])
    else:
        up_out[...] = add(ahead_ref[...], up_ref[...])
        down_out[...] = add(behind_ref[...], down_ref[...])


def close_kernel(s_ref, part_ref, up_ref, down_ref, gq_ref, rows_ref, attn_ref, sums_ref, bias_ref, packed_ref, project_ref):
    members, block, _ = packed_ref.shape
    width, model = attn_ref.shape
    share, units = model // members, bias_ref.shape[1] // members
    project_ref[:width] = gq_ref[...]
    for w in range(2):
        total = part_ref[w].astype(F32) + up_ref[w].astype(F32) + down_ref[w].astype(F32)
        project_ref[(1 + w) * width : (2 + w) * width] = total.astype(BF)
    grads = jnp.concatenate([contract(project_ref[...], rows_ref[...], 1, 0), attn_ref[...]], axis=0).T
    high = bias_ref[...].astype(BF).astype(F32)
    low = bias_ref[...] - high
    for i in range(members):
        packed_ref[i, :share] = grads[i * share : (i + 1) * share].astype(BF)
        at = slice(i * units, (i + 1) * units)
        line = jnp.concatenate([high[:, at], low[:, at], jnp.zeros((1, model - 2 * units), F32)], axis=1)
        tail = [sums_ref[:8].astype(F32), line, jnp.zeros((block - share - 9, model), F32)]
        packed_ref[i, share:] = jnp.concatenate(tail, axis=0).astype(BF)


def input_kernel(s_ref, project_ref, turned_ref, mine_ref, other_ref, part_s):
    near = s_ref[0] % 2
    rows = part_s.shape[0]
    own = rows // 4
    cols = project_ref.shape[0]
    part_s[...] = contract(project_ref[...].astype(F32).T.astype(BF), turned_ref[:cols], 1, 0)
    for f in range(2):
        here = slice(f * own, (f + 1) * own)
        mine_ref[here, :] = part_s[rows_at(2 * f + near, own), :].astype(BF)
        other_ref[here, :] = part_s[rows_at(2 * f + 1 - near, own), :].astype(BF)


class Ring:
    def __init__(self, axis, total, size):
        self.axis, self.size = axis, size
        local = list(range(0, size, 2)) + list(range(size - 1 - size % 2, 0, -2))
        self.local = local
        self.up, self.down = [], []
        for base in range(0, total, size):
            for i in range(size):
                a, b = base + local[i], base + local[(i + 1) % size]
                self.up.append((a, b))
                self.down.append((b, a))

    def members(self, index, offsets):
        n = self.size
        mine = jnp.where(index % 2 == 0, index // 2, n - 1 - index // 2)
        place = (mine + jnp.array(offsets, jnp.int32)) % n
        return jnp.where(place < (n + 1) // 2, 2 * place, 2 * (n - 1 - place) + 1)

    def groups(self):
        if self.size == 1:
            return [[0]]
        half = self.size // 2
        return [[0]] + [[-k, k] for k in range(1, half)] + [[half]]

    def gather(self, x):
        pieces = [x]
        up = down = x
        for group in self.groups()[1:-1]:
            up, down = self.send_up(up), self.send_down(down)
            pieces += [up, down]
        return pieces + [self.send_up(halves(up, 0)[0]), self.send_down(halves(down, 0)[1])]

    def send_up(self, x):
        return lax.ppermute(x, self.axis, self.up)

    def send_down(self, x):
        return lax.ppermute(x, self.axis, self.down)


class RingSum:
    def __init__(self, ring):
        self.ring = ring

    def first(self, a, b):
        self.up, self.down, self.half = self.ring.send_up(a), self.ring.send_down(b), True

    def step(self, scalars, behind, ahead):
        kind = (behind.shape, BF)
        up, down = fused(
            functools.partial(join_kernel, self.half), [kind, kind], scalars, behind, ahead, self.up, self.down
        )
        self.up, self.down, self.half = self.ring.send_up(up), self.ring.send_down(down), False
        return up


def halves(x, axis):
    middle = x.shape[axis] // 2
    return lax.slice_in_dim(x, 0, middle, axis=axis), lax.slice_in_dim(x, middle, x.shape[axis], axis=axis)


def add(a, b):
    return (a.astype(F32) + b.astype(F32)).astype(BF)


def after(x, *earlier):
    return lax.optimization_barrier((x, *earlier))[0]


def spread_gather(x, axis, n):
    return lax.all_to_all(jnp.broadcast_to(x[None], (n,) + x.shape), axis, 0, 0, tiled=True)


def group_sum(x, axis, n):
    parts = lax.all_to_all(x.reshape(n, x.shape[0] // n, x.shape[1]), axis, 0, 0, tiled=True)
    return jnp.sum(parts.astype(F32), axis=0)


def high_low(x):
    high = x.astype(BF)
    return high, (x - high.astype(F32)).astype(BF)


class Quad:
    def __init__(self, axis):
        self.axis = axis
        index = lax.axis_index(axis)
        self.near, self.far = index % 2, index // 2
        self.flip_near = [(i, i ^ 1) for i in range(4)]
        self.flip_far = [(i, i ^ 2) for i in range(4)]

    def send_near(self, x):
        return lax.ppermute(x, self.axis, self.flip_near)

    def send_far(self, x):
        return lax.ppermute(x, self.axis, self.flip_far)


def shards(
    inputs,
    prev_logits,
    w_query,
    w_key,
    w_value,
    w_attn_out,
    w_ffn_in,
    ffn_bias,
    w_ffn_out,
    norm1_gain,
    norm1_shift,
    norm2_gain,
    norm2_shift,
    token_segment,
    segment_parent,
    out_grad,
    logit_grad,
):
    rows, heads, length = prev_logits.shape
    width = heads * E
    own, model = inputs.shape
    spread = length // rows
    nd = lax.axis_size("dp")
    share = model // nd
    data_index, tensor_index = lax.axis_index("dp"), lax.axis_index("tensor")
    tree_index, local_index = data_index // spread, data_index % spread
    nb = rows // BLOCK
    quad = Quad("tensor")
    ring, all_ring = Ring("dp", nd, spread), Ring("dp", nd, nd)
    by_ring = share % 32 == 0
    place = tensor_index.astype(jnp.int32).reshape(1)
    gains = jnp.stack([norm1_gain, norm1_shift, norm2_gain, norm2_shift])

    pack_in = jnp.concatenate([w_ffn_in, ffn_bias[:, None]], axis=1)
    pack = jnp.concatenate([w_query, w_key, w_value, w_attn_out.T], axis=1)
    pack, pack_in, gains = lax.optimization_barrier((pack, pack_in, gains))
    pack_in = lax.all_gather(pack_in, "dp", axis=0, tiled=True)
    w_out = lax.all_gather(w_ffn_out, "dp", axis=0, tiled=True)
    if by_ring:
        pieces = all_ring.gather(pack)
        owners = [o for group in all_ring.groups() for o in group]
        owners = all_ring.members(data_index, owners)
    else:
        pieces = list(spread_gather(pack, "dp", nd).reshape(2, model // 2, 4 * width))
        owners = jnp.zeros((1,), jnp.int32)
    place = jnp.concatenate([place, owners])
    near = quad.send_near(inputs)
    rows_of_four = [inputs, near, quad.send_far(inputs), quad.send_far(near)]
    rows_all, turned, q_t, kv_own = fused(
        functools.partial(project_kernel, len(pieces) - 1),
        [((rows, model), BF), ((4 * width, model), BF), ((width, rows), BF), ((2, width, rows), BF)],
        place,
        *map(apart, pieces),
        *map(apart, rows_of_four),
        scratch=[((model, 4 * width), BF)],
    )
    out_own = turned[3 * width :]

    seg = lax.dynamic_slice_in_dim(token_segment, tree_index * length, length, 0)[::BLOCK]
    parents = lax.dynamic_slice_in_dim(segment_parent, tree_index, 1, 0)[0]
    seg_rows = lax.dynamic_slice_in_dim(seg, local_index * nb, nb, 0)
    labels = jnp.arange(parents.shape[0], dtype=jnp.int32)
    one = jnp.sum(jnp.where(seg_rows[:, None] == labels[None, :], parents[None, :], 0), axis=1)
    two = jnp.sum(jnp.where(one[:, None] == labels[None, :], parents[None, :], 0), axis=1)
    act = (
        (seg[None, :] == seg_rows[:, None])
        | (seg[None, :] == one[:, None])
        | (seg[None, :] == two[:, None])
    )
    act = act.astype(jnp.int32).reshape(-1)

    prev = apart(jnp.transpose(prev_logits, (1, 0, 2)))
    up_grad = apart(jnp.transpose(logit_grad, (1, 0, 2)))
    groups = ring.groups()
    order = [o for group in groups for o in group]
    sid = ring.members(local_index, order)
    held = [[kv_own]]
    going_up = going_down = kv_own
    state = None
    for step, group in enumerate(groups):
        last = step + 1 == len(groups)
        if not last:
            if state is not None:
                going_up, going_down = lax.optimization_barrier((going_up, going_down, state[1]))[:2]
            if step + 2 == len(groups):
                held.append([ring.send_up(going_up[:1]), ring.send_down(going_down[1:])])
            else:
                going_up, going_down = ring.send_up(going_up), ring.send_down(going_down)
                held.append([going_up, going_down])
        result = attend_forward(
            sid, order.index(group[0]), act, q_t, held[step], prev, state, last, 512
        )
        state = (result[0], result[-1])
        if step == 0:
            out_grad_far = quad.send_far(after(out_grad, q_t))
            state = (state[0], after(state[1], out_grad_far))
            near = quad.send_near(out_own)
            outs = [out_own, near, quad.send_far(out_own), quad.send_far(near)]
    logits, mixed, aux = result
    pack_in, w_out, *outs = (apart(after(w, mixed)) for w in (pack_in, w_out, *outs))

    pair = (2 * own, model)
    mixed_all = lax.all_gather(mixed, "tensor", axis=0, tiled=True)
    low, active, slope, first_n, first_r, mine, other = fused(
        feed_kernel,
        [((rows, model), BF), ((rows, model), BF), ((rows, model), F32), (pair, F32), ((2 * own, 128), F32)]
        + [(pair, BF)] * 2,
        place,
        mixed_all,
        rows_all,
        *outs,
        pack_in,
        w_out,
        gains,
        scratch=[((4 * width, model), BF), ((rows, model), F32), ((rows, model), F32), ((rows, 128), F32)],
    )
    mine = add(mine, quad.send_near(other))
    output, second, second_low, sums = fused(
        second_kernel,
        [((own, model), BF), (pair, F32), (pair, BF), ((2, model), F32)],
        place,
        mine,
        quad.send_far(mine),
        first_n,
        apart(out_grad),
        apart(out_grad_far),
        gains,
    )
    second_all, inner, grad_bias, mine, other = fused(
        back_kernel,
        [((rows, model), BF), ((rows, model), BF), ((1, model), F32), (pair, BF), (pair, BF)],
        place,
        second_low,
        quad.send_near(second_low),
        slope,
        pack_in,
        w_out,
        scratch=[((rows, model), F32)],
    )
    mine = add(mine, quad.send_near(other))
    far = quad.send_far(mine)
    (weight_grads,) = fused(
        weight_kernel,
        [((model, 2 * model), BF)],
        place,
        active,
        second_all,
        low,
        after(inner, mine),
    )
    far = after(far, weight_grads)
    weight_grads = lax.psum_scatter(weight_grads, "dp", scatter_dimension=0, tiled=True)

    sent, grad_first = fused(
        first_kernel,
        [((2 * own + 16, model), BF), ((own, model), F32)],
        place,
        mine,
        far,
        second,
        first_n,
        first_r,
        sums,
        gains,
    )
    received = quad.send_near(sent)
    grad_mixed, grad_w_attn, sums = fused(
        mixed_kernel,
        [((width, rows), BF), ((width, model), F32), ((16, model), BF)],
        place,
        sent,
        received,
        mixed,
        out_own,
        scratch=[((rows, model), BF)],
    )

    state = None
    total_kv = RingSum(ring)
    for step, group in reversed(list(enumerate(groups))):
        result = attend_backward(
            sid,
            order.index(group[0]),
            act,
            q_t,
            grad_mixed,
            aux,
            [apart(kv) for kv in held[step]],
            prev,
            up_grad,
            state,
            step == 0,
            256,
        )
        state = (result[0], result[-1])
        if step + 1 == len(groups):
            total_kv.first(*result[1:-1])
        elif step > 0:
            total_kv.step(place, *result[1:-1])
    prev_grad, part, grad_query = result

    packed, grad_project = fused(
        close_kernel,
        [((nd, share + 16, model), BF), ((3 * width, rows), BF)],
        place,
        part,
        total_kv.up,
        total_kv.down,
        grad_query,
        rows_all,
        grad_w_attn,
        sums,
        grad_bias,
    )
    mine, other = fused(
        input_kernel,
        [(pair, BF), (pair, BF)],
        place,
        grad_project,
        apart(turned),
        scratch=[((rows, model), F32)],
    )
    mine, packed = lax.optimization_barrier((add(mine, quad.send_near(other)).reshape(2, own, model), packed))
    far = quad.send_far(lax.dynamic_index_in_dim(mine, 1 - quad.far, 0, keepdims=False))
    kept = lax.dynamic_index_in_dim(mine, quad.far, 0, keepdims=False)
    packed = lax.all_to_all(after(packed, far), "dp", 0, 0, tiled=True)
    grad_inputs = grad_first + (kept.astype(F32) + far.astype(F32))
    weight_grads = weight_grads.astype(F32)
    packed = jnp.sum(packed.astype(F32), axis=0)
    norms = packed[share : share + 4] + packed[share + 4 : share + 8]
    units = grad_bias.shape[1] // nd
    grad_bias = packed[share + 8, :units] + packed[share + 8, units : 2 * units]
    return (
        output,
        jnp.transpose(logits, (1, 0, 2)),
        grad_inputs,
        jnp.transpose(prev_grad, (1, 0, 2)),
        packed[:share, :width],
        packed[:share, width : 2 * width],
        packed[:share, 2 * width : 3 * width],
        packed[:share, 3 * width :].T,
        weight_grads[:, model:],
        grad_bias,
        weight_grads[:, :model],
        norms[0],
        norms[1],
        norms[2],
        norms[3],
    )


def solution(mesh):
    placed = (
        P(("dp", "tensor"), None),
        P("dp", "tensor", None),
        P("dp", "tensor"),
        P("dp", "tensor"),
        P("dp", "tensor"),
        P("tensor", "dp"),
        P("dp", "tensor"),
        P(("tensor", "dp")),
        P(("tensor", "dp"), None),
        P(),
        P(),
        P(),
        P(),
        P(),
        P(),
        P(("dp", "tensor"), None),
        P("dp", "tensor", None),
    )
    return jax.shard_map(
        shards,
        mesh=mesh,
        in_specs=placed,
        out_specs=(
            P(("dp", "tensor"), None),
            P("dp", "tensor", None),
            P(("dp", "tensor"), None),
            P("dp", "tensor", None),
            P("dp", "tensor"),
            P("dp", "tensor"),
            P("dp", "tensor"),
            P("tensor", "dp"),
            P("dp", "tensor"),
            P(("tensor", "dp")),
            P(("tensor", "dp"), None),
            P(),
            P(),
            P(),
            P(),
        ),
        check_vma=False,
    )
```

profile of v0, /device:TPU:0, one launch (start us, length us, event | category | flops | bytes accessed | tf_op | source)
XLA Modules:
  0.0 295.6 jit_solution(11477519764227218263)
XLA Ops:
  15.0 3.0 %collective-permute-start.1 = (bf16[96,768]{1,0:T(8,128)(2,1)S(1)}, bf16[96,768]{1,0:T(8,128)(2,1)S(1)}, u32[]{:S(2)}, u32[]{:S(2)}) collective-permute-start(bf16[96,768]{1,0:T(8,128)(2,1)S(1)} %pad_maximum_fusion.1.refs_0_), channel_id=1, source_target_pairs={{8,0},{16,8},{24,16},{28,24},{20,28},{12,20},{4,12},{0,4},{9,1},{1... | collective-permute-start | bytes 442376 | tf_op jit(solution)/shard_map/ppermute | solution.py:599
  18.1 3.8 %collective-permute-done.1.refs_2_ = bf16[96,768]{1,0:T(8,128)(2,1)S(1)} collective-permute-done((bf16[96,768]{1,0:T(8,128)(2,1)S(1)}, bf16[96,768]{1,0:T(8,128)(2,1)S(1)}, u32[]{:S(2)}, u32[]{:S(2)}) %collective-permute-start.1) | collective-permute-done | bytes 147488 | tf_op jit(solution)/shard_map/ppermute | solution.py:599
  26.2 2.8 collective-permute-done.3.refs_4_
  48.9 5.4 %shard_map.299 = (bf16[3,512,4096]{2,1,0:T(8,128)(2,1)}, f32[3,512,128]{2,1,0:T(8,128)S(1)}) custom-call(s32[8]{0:T(128)S(1)} %get-tuple-element.259.refs_0_, s32[128]{0:T(128)S(1)} %reshape.59.refs_1_, bf16[192,512]{1,0:T(8,128)(2,1)S(1)} %get-tuple-element.103.refs_2_, bf16[2,192,512]{2,1,0:T(8,128)(2,1)S(1)} %get-tuple-element.104.refs_3_.refs_5_, ...), custom_call_target="tpu_custom_call" | custom-call | flops 201326592 | bytes 3145728 | tf_op jit(solution)/shard_map/pallas_call | solution.py:176
  54.4 4.7 %collective-permute-done.12.refs_4_.refs_6_ = bf16[2,192,512]{2,1,0:T(8,128)(2,1)S(1)} collective-permute-done((bf16[2,192,512]{2,1,0:T(8,128)(2,1)S(1)}, bf16[2,192,512]{2,1,0:T(8,128)(2,1)S(1)}, u32[]{:S(2)}, u32[]{:S(2)}) %collective-permute-start.12) | collective-permute-done | bytes 393248 | tf_op jit(solution)/shard_map/ppermute | solution.py:599
  61.2 8.5 %shard_map.300 = (bf16[3,512,4096]{2,1,0:T(8,128)(2,1)}, f32[3,512,128]{2,1,0:T(8,128)S(1)}) custom-call(s32[8]{0:T(128)S(1)} %get-tuple-element.259.refs_0_, s32[128]{0:T(128)S(1)} %reshape.59.refs_1_, bf16[192,512]{1,0:T(8,128)(2,1)S(1)} %get-tuple-element.103.refs_2_, ...), custom_call_target="tpu_custom_call", output_to_operand_aliasing={{0}: (6, {})} | custom-call | flops 402653184 | bytes 6291456 | tf_op jit(solution)/shard_map/pallas_call | solution.py:176
  75.5 6.0 %shard_map.301 = (bf16[3,512,4096]{2,1,0:T(8,128)(2,1)}, f32[3,512,128]{2,1,0:T(8,128)S(1)}) custom-call(s32[8]{0:T(128)S(1)} %get-tuple-element.259.refs_0_, s32[128]{0:T(128)S(1)} %reshape.59.refs_1_, bf16[192,512]{1,0:T(8,128)(2,1)S(1)} %get-tuple-element.103.refs_2_, ...), custom_call_target="tpu_custom_call", output_to_operand_aliasing={{0}: (6, {})} | custom-call | flops 402653184 | bytes 6291456 | tf_op jit(solution)/shard_map/pallas_call | solution.py:176
  86.5 3.1 %shard_map.302 = (bf16[3,512,4096]{2,1,0:T(8,128)(2,1)}, f32[3,512,128]{2,1,0:T(8,128)S(1)}) custom-call(s32[8]{0:T(128)S(1)} %get-tuple-element.259.refs_0_, s32[128]{0:T(128)S(1)} %reshape.59.refs_1_, bf16[192,512]{1,0:T(8,128)(2,1)S(1)} %get-tuple-element.103.refs_2_, ...), custom_call_target="tpu_custom_call", output_to_operand_aliasing={{0}: (6, {})} | custom-call | flops 402653184 | bytes 6291456 | tf_op jit(solution)/shard_map/pallas_call | solution.py:176
  89.6 3.4 %collective-permute-done.19.refs_4_.refs_6_ = bf16[1,192,512]{2,1,0:T(8,128)(2,1)S(1)} collective-permute-done((bf16[1,192,512]{2,1,0:T(8,128)(2,1)S(1)}, bf16[1,192,512]{2,1,0:T(8,128)(2,1)S(1)}, u32[]{:S(2)}, u32[]{:S(2)}) %collective-permute-start.19) | collective-permute-done | bytes 196640 | tf_op jit(solution)/shard_map/ppermute | solution.py:599
  100.0 8.7 %all_gather.9.mixed_ref = bf16[768,512]{1,0:T(8,128)(2,1)S(1)} all-gather(bf16[192,512]{1,0:T(8,128)(2,1)S(1)} %get-tuple-element.121.mixed_ref), channel_id=1, replica_groups=mesh['dp'=8,'tensor'=4] {'tensor'}, dimensions={0}, use_global_device_ids=true | all-gather | bytes 983040 | tf_op jit(solution)/shard_map/all_gather | solution.py:763
  108.7 5.7 %shard_map.304 = (bf16[512,768]{1,0:T(8,128)(2,1)S(1)}, bf16[512,768]{1,0:T(8,128)(2,1)S(1)}, f32[512,768]{1,0:T(8,128)S(1)}, f32[256,768]{1,0:T(8,128)S(1)}, f3...) custom-call(s32[9]{0:T(128)S(1)} %pad_add_fusion.s_ref, ...), custom_call_target="tpu_custom_call" | custom-call | bytes 1048576 | tf_op jit(solution)/shard_map/pallas_call | solution.py:345
  116.8 10.9 %collective-permute-done.24.b_ref = bf16[256,768]{1,0:T(8,128)(2,1)S(1)} collective-permute-done((bf16[256,768]{1,0:T(8,128)(2,1)S(1)}, bf16[256,768]{1,0:T(8,128)(2,1)S(1)}, u32[]{:S(2)}, u32[]{:S(2)}) %collective-permute-start.24) | collective-permute-done | bytes 393248 | tf_op jit(solution)/shard_map/ppermute | solution.py:657
  127.8 2.5 shard_map.305
  132.8 3.5 %shard_map.306 = (bf16[512,768]{1,0:T(8,128)(2,1)S(1)}, bf16[512,768]{1,0:T(8,128)(2,1)S(1)}, f32[1,768]{1,0:T(1,128)S(1)}, bf16[256,768]{1,0:T(8,128)(2,1)S(1)}, bf16[256,768]{1,0:T(8,128)(2,1)S(1)}) custom-call(s32[9]{0:T(128)S(1)} %pad_add_fusion.s_ref, bf16[256,768]{1,0:T(8,128)(2,1)S(1)} %get-tuple-element.137.low_ref, ...), custom_call_target="tpu_custom_call" | custom-call | bytes 1048576 | tf_op jit(solution)/shard_map/pallas_call | solution.py:345
  138.7 3.4 %shard_map.307 = bf16[768,1536]{1,0:T(8,128)(2,1)} custom-call(s32[9]{0:T(128)S(1)} %pad_add_fusion.s_ref, bf16[512,768]{1,0:T(8,128)(2,1)S(1)} %get-tuple-element.141.active_ref, bf16[512,768]{1,0:T(8,128)(2,1)S(1)} %get-tuple-element.142.second_ref, bf16[512,768]{1,0:T(8,128)(2,1)S(1)} %get-tuple-element.143.low_ref, ...), custom_call_target="tpu_custom_call" | custom-call | bytes 1048576 | tf_op jit(solution)/shard_map/pallas_call | solution.py:345
  142.2 7.3 %collective-permute-done.27.b_ref = bf16[256,768]{1,0:T(8,128)(2,1)S(1)} collective-permute-done((bf16[256,768]{1,0:T(8,128)(2,1)S(1)}, bf16[256,768]{1,0:T(8,128)(2,1)S(1)}, u32[]{:S(2)}, u32[]{:S(2)}) %collective-permute-start.27) | collective-permute-done | bytes 393248 | tf_op jit(solution)/shard_map/ppermute | solution.py:657
  161.0 3.3 %shard_map.310 = (bf16[3,512,4096]{2,1,0:T(8,128)(2,1)}, bf16[1,192,512]{2,1,0:T(8,128)(2,1)S(1)}, bf16[1,192,512]{2,1,0:T(8,128)(2,1)S(1)}, f32[3,512,64]{2,1,0:T(8,128)S(1)}) custom-call(s32[8]{0:T(128)S(1)} %copy-done.20, s32[128]{0:T(128)S(1)} %copy-done.24, bf16[192,512]{1,0:T(8,128)(2,1)S(1)} %get-tuple-element.103.refs_2_, ...), custom_call_target="tpu_custom_call" | custom-call | flops 503316480 | bytes 4718592 | tf_op jit(solution)/shard_map/pallas_call | solution.py:313
  164.3 2.4 collective-permute-start.29
  166.7 4.1 %shard_map.311 = (bf16[3,512,4096]{2,1,0:T(8,128)(2,1)}, bf16[2,192,512]{2,1,0:T(8,128)(2,1)S(1)}, bf16[2,192,512]{2,1,0:T(8,128)(2,1)S(1)}, f32[3,512,64]{2,1,0:T(8,128)S(1)}) custom-call(s32[8]{0:T(128)S(1)} %copy-done.21, s32[128]{0:T(128)S(1)} %copy-done.24, bf16[192,512]{1,0:T(8,128)(2,1)S(1)} %get-tuple-element.103.refs_2_, ...), custom_call_target="tpu_custom_call", output_to_operand_aliasing={{0}: (9, {})} | custom-call | flops 1006632960 | bytes 9437184 | tf_op jit(solution)/shard_map/pallas_call | solution.py:313
  170.8 4.4 %collective-permute-done.29.up_ref = bf16[1,192,512]{2,1,0:T(8,128)(2,1)S(1)} collective-permute-done((bf16[1,192,512]{2,1,0:T(8,128)(2,1)S(1)}, bf16[1,192,512]{2,1,0:T(8,128)(2,1)S(1)}, u32[]{:S(2)}, u32[]{:S(2)}) %collective-permute-start.29) | collective-permute-done | bytes 196640 | tf_op jit(solution)/shard_map/ppermute | solution.py:596
  175.3 13.5 %collective-permute-done.30.down_ref = bf16[1,192,512]{2,1,0:T(8,128)(2,1)S(1)} collective-permute-done((bf16[1,192,512]{2,1,0:T(8,128)(2,1)S(1)}, bf16[1,192,512]{2,1,0:T(8,128)(2,1)S(1)}, u32[]{:S(2)}, u32[]{:S(2)}) %collective-permute-start.30) | collective-permute-done | bytes 196640 | tf_op jit(solution)/shard_map/ppermute | solution.py:599
  191.5 6.9 %shard_map.312 = (bf16[3,512,4096]{2,1,0:T(8,128)(2,1)}, bf16[2,192,512]{2,1,0:T(8,128)(2,1)S(1)}, bf16[2,192,512]{2,1,0:T(8,128)(2,1)S(1)}, f32[3,512,64]{2,1,0:T(8,128)S(1)}) custom-call(s32[8]{0:T(128)S(1)} %copy-done.21, s32[128]{0:T(128)S(1)} %copy-done.24, bf16[192,512]{1,0:T(8,128)(2,1)S(1)} %get-tuple-element.103.refs_2_, ...), custom_call_target="tpu_custom_call", output_to_operand_aliasing={{0}: (9, {})} | custom-call | flops 1006632960 | bytes 9437184 | tf_op jit(solution)/shard_map/pallas_call | solution.py:313
  198.4 4.5 %collective-permute-done.31.up_ref = bf16[2,192,512]{2,1,0:T(8,128)(2,1)S(1)} collective-permute-done((bf16[2,192,512]{2,1,0:T(8,128)(2,1)S(1)}, bf16[2,192,512]{2,1,0:T(8,128)(2,1)S(1)}, u32[]{:S(2)}, u32[]{:S(2)}) %collective-permute-start.31) | collective-permute-done | bytes 393248 | tf_op jit(solution)/shard_map/ppermute | solution.py:596
  206.7 9.5 %shard_map.313 = (bf16[3,512,4096]{2,1,0:T(8,128)(2,1)}, bf16[2,192,512]{2,1,0:T(8,128)(2,1)S(1)}, bf16[2,192,512]{2,1,0:T(8,128)(2,1)S(1)}, f32[3,512,64]{2,1,0:T(8,128)S(1)}) custom-call(s32[8]{0:T(128)S(1)} %copy-done.21, s32[128]{0:T(128)S(1)} %copy-done.24, bf16[192,512]{1,0:T(8,128)(2,1)S(1)} %get-tuple-element.103.refs_2_, ...), custom_call_target="tpu_custom_call", output_to_operand_aliasing={{0}: (9, {})} | custom-call | flops 1006632960 | bytes 9437184 | tf_op jit(solution)/shard_map/pallas_call | solution.py:313
  218.9 2.5 collective-permute-start.36
  221.4 6.2 %shard_map.314 = (bf16[3,512,4096]{2,1,0:T(8,128)(2,1)}, bf16[2,192,512]{2,1,0:T(8,128)(2,1)S(1)}, bf16[192,512]{1,0:T(8,128)(2,1)S(1)}) custom-call(s32[8]{0:T(128)S(1)} %copy-done.21, s32[128]{0:T(128)S(1)} %copy-done.25, bf16[192,512]{1,0:T(8,128)(2,1)S(1)} %get-tuple-element.103.refs_2_, ...), custom_call_target="tpu_custom_call", output_to_operand_aliasing={{0}: (8, {})} | custom-call | flops 503316480 | bytes 4718592 | tf_op jit(solution)/shard_map/pallas_call | solution.py:313
  227.7 5.1 %collective-permute-done.35.up_ref = bf16[2,192,512]{2,1,0:T(8,128)(2,1)S(1)} collective-permute-done((bf16[2,192,512]{2,1,0:T(8,128)(2,1)S(1)}, bf16[2,192,512]{2,1,0:T(8,128)(2,1)S(1)}, u32[]{:S(2)}, u32[]{:S(2)}) %collective-permute-start.35) | collective-permute-done | bytes 393248 | tf_op jit(solution)/shard_map/ppermute | solution.py:596
  234.9 2.4 shard_map.318
  241.5 3.0 %collective-permute-start.38 = (bf16[128,768]{1,0:T(8,128)(2,1)S(1)}, bf16[128,768]{1,0:T(8,128)(2,1)S(1)}, u32[]{:S(2)}, u32[]{:S(2)}) collective-permute-start(bf16[128,768]{1,0:T(8,128)(2,1)S(1)} %dynamic-slice_bitcast_fusion), channel_id=1, source_target_pairs={{0,2},{1,3},{2,0},{3,1},{4,6},{5,7},{6,4},{7,5},{8,10},{9,11},{10,... | collective-permute-start | bytes 589832 | tf_op jit(solution)/shard_map/ppermute | solution.py:657
  244.6 5.2 %collective-permute-done.38 = bf16[128,768]{1,0:T(8,128)(2,1)S(1)} collective-permute-done((bf16[128,768]{1,0:T(8,128)(2,1)S(1)}, bf16[128,768]{1,0:T(8,128)(2,1)S(1)}, u32[]{:S(2)}, u32[]{:S(2)}) %collective-permute-start.38) | collective-permute-done | bytes 196640 | tf_op jit(solution)/shard_map/ppermute | solution.py:657
  249.8 3.6 %all-to-all-start = ((bf16[8,112,768]{2,1,0:T(8,128)(2,1)}), bf16[8,112,768]{2,1,0:T(8,128)(2,1)S(1)}, u32[]{:S(2)}, u32[]{:S(2)}) async-start(bf16[8,112,768]{2,1,0:T(8,128)(2,1)} %get-tuple-element.188), calls=%async_computation | async-start | bytes 2752512 | tf_op jit(solution)/shard_map/all_to_all | solution.py:886
  256.0 30.1 %all-to-all-done = bf16[8,112,768]{2,1,0:T(8,128)(2,1)S(1)} async-done(((bf16[8,112,768]{2,1,0:T(8,128)(2,1)}), bf16[8,112,768]{2,1,0:T(8,128)(2,1)S(1)}, u32[]{:S(2)}, u32[]{:S(2)}) %all-to-all-start) | async-done | bytes 1376288 | tf_op jit(solution)/shard_map/all_to_all | solution.py:886
  (204 shorter events, 91.6 us)
Async XLA Ops:
  7.2 101.5 %all-gather.5.cloned.1.call-start = ((), (), s32[]{:S(2)}) async-start(), calls=%async_computation.3 | async-start | bytes 1327104 | tf_op jit(solution)/shard_map/all_gather | solution.py:698
  7.9 100.8 %all-gather.3.cloned.1.call-start = ((), (), s32[]{:S(2)}) async-start(), calls=%async_computation.2 | async-start | bytes 1548288 | tf_op jit(solution)/shard_map/all_gather | solution.py:697
  15.0 6.9 %collective-permute-start.1 = (bf16[96,768]{1,0:T(8,128)(2,1)S(1)}, bf16[96,768]{1,0:T(8,128)(2,1)S(1)}, u32[]{:S(2)}, u32[]{:S(2)}) collective-permute-start(bf16[96,768]{1,0:T(8,128)(2,1)S(1)} %pad_maximum_fusion.1.refs_0_), channel_id=1, source_target_pairs={{8,0},{16,8},{24,16},{28,24},{20,28},{12,20},{4,12},{0,4},{9,1},{1... | collective-permute-start | bytes 442376 | tf_op jit(solution)/shard_map/ppermute | solution.py:599
  18.1 7.7 %collective-permute-start.8 = (bf16[128,768]{1,0:T(8,128)(2,1)}, bf16[128,768]{1,0:T(8,128)(2,1)S(1)}, u32[]{:S(2)}, u32[]{:S(2)}) collective-permute-start(bf16[128,768]{1,0:T(8,128)(2,1)} %refs_9_.1), channel_id=1, source_target_pairs={{0,1},{1,0},{2,3},{3,2},{4,5},{5,4},{6,7},{7,6},{8,9},{9,8},{10,11... | collective-permute-start | bytes 589832 | tf_op jit(solution)/shard_map/ppermute | solution.py:654
  21.9 7.1 %collective-permute-start.3 = (bf16[96,768]{1,0:T(8,128)(2,1)S(1)}, bf16[96,768]{1,0:T(8,128)(2,1)S(1)}, u32[]{:S(2)}, u32[]{:S(2)}) collective-permute-start(bf16[96,768]{1,0:T(8,128)(2,1)S(1)} %collective-permute-done.1.refs_2_), channel_id=1, source_target_pairs={{8,0},{16,8},{24,16},{28,24},{20,28},{12,20},{4,12},{0,4},{9,1},{1... | collective-permute-start | bytes 442376 | tf_op jit(solution)/shard_map/ppermute | solution.py:599
  23.9 13.7 %collective-permute-start.9 = (bf16[128,768]{1,0:T(8,128)(2,1)}, bf16[128,768]{1,0:T(8,128)(2,1)S(1)}, u32[]{:S(2)}, u32[]{:S(2)}) collective-permute-start(bf16[128,768]{1,0:T(8,128)(2,1)} %refs_9_.1), channel_id=1, source_target_pairs={{0,2},{1,3},{2,0},{3,1},{4,6},{5,7},{6,4},{7,5},{8,10},{9,11},{10,... | collective-permute-start | bytes 589832 | tf_op jit(solution)/shard_map/ppermute | solution.py:657
  25.6 228.6 %reduce-scatter.2.cloned.1.call-start = ((), (), s32[]{:S(2)}) async-start(), calls=%async_computation.4 | async-start | bytes 2654208 | tf_op jit(solution)/shard_map/reduce_scatter | solution.py:812
  25.8 11.9 %collective-permute-start.10 = (bf16[128,768]{1,0:T(8,128)(2,1)S(1)}, bf16[128,768]{1,0:T(8,128)(2,1)S(1)}, u32[]{:S(2)}, u32[]{:S(2)}) collective-permute-start(bf16[128,768]{1,0:T(8,128)(2,1)S(1)} %collective-permute-done.8.refs_10_), channel_id=1, source_target_pairs={{0,2},{1,3},{2,0},{3,1},{4,6},{5,7},{6,4},{7,5},{8,10},{9,11},{10,... | collective-permute-start | bytes 589832 | tf_op jit(solution)/shard_map/ppermute | solution.py:657
  29.0 6.4 %collective-permute-start.5 = (bf16[96,768]{1,0:T(8,128)(2,1)S(1)}, bf16[96,768]{1,0:T(8,128)(2,1)S(1)}, u32[]{:S(2)}, u32[]{:S(2)}) collective-permute-start(bf16[96,768]{1,0:T(8,128)(2,1)S(1)} %collective-permute-done.3.refs_4_), channel_id=1, source_target_pairs={{8,0},{16,8},{24,16},{28,24},{20,28},{12,20},{4,12},{0,4},{9,1},{1... | collective-permute-start | bytes 442376 | tf_op jit(solution)/shard_map/ppermute | solution.py:599
  43.6 15.5 %collective-permute-start.12 = (bf16[2,192,512]{2,1,0:T(8,128)(2,1)S(1)}, bf16[2,192,512]{2,1,0:T(8,128)(2,1)S(1)}, u32[]{:S(2)}, u32[]{:S(2)}) collective-permute-start(bf16[2,192,512]{2,1,0:T(8,128)(2,1)S(1)} %get-tuple-element.104.refs_3_.refs_5_), channel_id=1, source_target_pairs={{8,0},{16,8},{24,16},{28,24},{20,28},{12,20},{4,12},{0,4},{9,1},{1... | collective-permute-start | bytes 1179656 | tf_op jit(solution)/shard_map/ppermute | solution.py:599
  45.1 14.0 %collective-permute-start.11 = (bf16[2,192,512]{2,1,0:T(8,128)(2,1)S(1)}, bf16[2,192,512]{2,1,0:T(8,128)(2,1)S(1)}, u32[]{:S(2)}, u32[]{:S(2)}) collective-permute-start(bf16[2,192,512]{2,1,0:T(8,128)(2,1)S(1)} %get-tuple-element.104.refs_3_.refs_5_), channel_id=1, source_target_pairs={{0,8},{8,16},{16,24},{24,28},{28,20},{20,12},{12,4},{4,0},{1,9},{9... | collective-permute-start | bytes 1179656 | tf_op jit(solution)/shard_map/ppermute | solution.py:596
  47.9 6.5 %collective-permute-start.13 = (bf16[128,768]{1,0:T(8,128)(2,1)}, bf16[128,768]{1,0:T(8,128)(2,1)}, u32[]{:S(2)}, u32[]{:S(2)}) collective-permute-start(bf16[128,768]{1,0:T(8,128)(2,1)} %cot_own.1), channel_id=1, source_target_pairs={{0,2},{1,3},{2,0},{3,1},{4,6},{5,7},{6,4},{7,5},{8,10},{9,11},{10,... | collective-permute-start | bytes 589832 | tf_op jit(solution)/shard_map/ppermute | solution.py:657
  59.1 10.6 %collective-permute-start.14 = (bf16[2,192,512]{2,1,0:T(8,128)(2,1)S(1)}, bf16[2,192,512]{2,1,0:T(8,128)(2,1)S(1)}, u32[]{:S(2)}, u32[]{:S(2)}) collective-permute-start(bf16[2,192,512]{2,1,0:T(8,128)(2,1)S(1)} %collective-permute-done.11.refs_3_.refs_5_), channel_id=1, source_target_pairs={{0,8},{8,16},{16,24},{24,28},{28,20},{20,12},{12,4},{4,0},{1,9},{9... | collective-permute-start | bytes 1179656 | tf_op jit(solution)/shard_map/ppermute | solution.py:596
  60.7 9.0 %collective-permute-start.15 = (bf16[2,192,512]{2,1,0:T(8,128)(2,1)S(1)}, bf16[2,192,512]{2,1,0:T(8,128)(2,1)S(1)}, u32[]{:S(2)}, u32[]{:S(2)}) collective-permute-start(bf16[2,192,512]{2,1,0:T(8,128)(2,1)S(1)} %collective-permute-done.12.refs_4_.refs_6_), channel_id=1, source_target_pairs={{8,0},{16,8},{24,16},{28,24},{20,28},{12,20},{4,12},{0,4},{9,1},{1... | collective-permute-start | bytes 1179656 | tf_op jit(solution)/shard_map/ppermute | solution.py:599
  69.7 12.3 %collective-permute-start.16 = (bf16[2,192,512]{2,1,0:T(8,128)(2,1)S(1)}, bf16[2,192,512]{2,1,0:T(8,128)(2,1)S(1)}, u32[]{:S(2)}, u32[]{:S(2)}) collective-permute-start(bf16[2,192,512]{2,1,0:T(8,128)(2,1)S(1)} %collective-permute-done.14.refs_3_.refs_5_), channel_id=1, source_target_pairs={{0,8},{8,16},{16,24},{24,28},{28,20},{20,12},{12,4},{4,0},{1,9},{9... | collective-permute-start | bytes 1179656 | tf_op jit(solution)/shard_map/ppermute | solution.py:596
  69.9 14.5 %collective-permute-start.17 = (bf16[2,192,512]{2,1,0:T(8,128)(2,1)S(1)}, bf16[2,192,512]{2,1,0:T(8,128)(2,1)S(1)}, u32[]{:S(2)}, u32[]{:S(2)}) collective-permute-start(bf16[2,192,512]{2,1,0:T(8,128)(2,1)S(1)} %collective-permute-done.15.refs_4_.refs_6_), channel_id=1, source_target_pairs={{8,0},{16,8},{24,16},{28,24},{20,28},{12,20},{4,12},{0,4},{9,1},{1... | collective-permute-start | bytes 1179656 | tf_op jit(solution)/shard_map/ppermute | solution.py:599
  73.5 25.1 %collective-permute-start.22 = (bf16[192,768]{1,0:T(8,128)(2,1)S(1)}, bf16[192,768]{1,0:T(8,128)(2,1)S(1)}, u32[]{:S(2)}, u32[]{:S(2)}) collective-permute-start(bf16[192,768]{1,0:T(8,128)(2,1)S(1)} %collective-permute-done.20.o1), channel_id=1, source_target_pairs={{0,2},{1,3},{2,0},{3,1},{4,6},{5,7},{6,4},{7,5},{8,10},{9,11},{10,... | collective-permute-start | bytes 884744 | tf_op jit(solution)/shard_map/ppermute | solution.py:657
  74.9 23.7 %collective-permute-start.21 = (bf16[192,768]{1,0:T(8,128)(2,1)S(1)}, bf16[192,768]{1,0:T(8,128)(2,1)S(1)}, u32[]{:S(2)}, u32[]{:S(2)}) collective-permute-start(bf16[192,768]{1,0:T(8,128)(2,1)S(1)} %slice.65.o0.o_ref), channel_id=1, source_target_pairs={{0,2},{1,3},{2,0},{3,1},{4,6},{5,7},{6,4},{7,5},{8,10},{9,11},{10,... | collective-permute-start | bytes 884744 | tf_op jit(solution)/shard_map/ppermute | solution.py:657
  84.4 8.6 %collective-permute-start.19 = (bf16[1,192,512]{2,1,0:T(8,128)(2,1)S(1)}, bf16[1,192,512]{2,1,0:T(8,128)(2,1)S(1)}, u32[]{:S(2)}, u32[]{:S(2)}) collective-permute-start(bf16[1,192,512]{2,1,0:T(8,128)(2,1)S(1)} %slice.64), channel_id=1, source_target_pairs={{8,0},{16,8},{24,16},{28,24},{20,28},{12,20},{4,12},{0,4},{9,1},{1... | collective-permute-start | bytes 589832 | tf_op jit(solution)/shard_map/ppermute | solution.py:599
  85.5 9.4 %collective-permute-start.18 = (bf16[1,192,512]{2,1,0:T(8,128)(2,1)S(1)}, bf16[1,192,512]{2,1,0:T(8,128)(2,1)S(1)}, u32[]{:S(2)}, u32[]{:S(2)}) collective-permute-start(bf16[1,192,512]{2,1,0:T(8,128)(2,1)S(1)} %slice.63), channel_id=1, source_target_pairs={{0,8},{8,16},{16,24},{24,28},{28,20},{20,12},{12,4},{4,0},{1,9},{9... | collective-permute-start | bytes 589832 | tf_op jit(solution)/shard_map/ppermute | solution.py:596
  116.3 11.4 %collective-permute-start.24 = (bf16[256,768]{1,0:T(8,128)(2,1)S(1)}, bf16[256,768]{1,0:T(8,128)(2,1)S(1)}, u32[]{:S(2)}, u32[]{:S(2)}) collective-permute-start(bf16[256,768]{1,0:T(8,128)(2,1)S(1)} %add_convert_fusion.2.a_ref), channel_id=1, source_target_pairs={{0,2},{1,3},{2,0},{3,1},{4,6},{5,7},{6,4},{7,5},{8,10},{9,11},{10,... | collective-permute-start | bytes 1179656 | tf_op jit(solution)/shard_map/ppermute | solution.py:657
  138.2 11.2 %collective-permute-start.27 = (bf16[256,768]{1,0:T(8,128)(2,1)S(1)}, bf16[256,768]{1,0:T(8,128)(2,1)S(1)}, u32[]{:S(2)}, u32[]{:S(2)}) collective-permute-start(bf16[256,768]{1,0:T(8,128)(2,1)S(1)} %add_convert_fusion.1.a_ref), channel_id=1, source_target_pairs={{0,2},{1,3},{2,0},{3,1},{4,6},{5,7},{6,4},{7,5},{8,10},{9,11},{10,... | collective-permute-start | bytes 1179656 | tf_op jit(solution)/shard_map/ppermute | solution.py:657
  164.3 11.0 %collective-permute-start.29 = (bf16[1,192,512]{2,1,0:T(8,128)(2,1)S(1)}, bf16[1,192,512]{2,1,0:T(8,128)(2,1)S(1)}, u32[]{:S(2)}, u32[]{:S(2)}) collective-permute-start(bf16[1,192,512]{2,1,0:T(8,128)(2,1)S(1)} %get-tuple-element.169), channel_id=1, source_target_pairs={{0,8},{8,16},{16,24},{24,28},{28,20},{20,12},{12,4},{4,0},{1,9},{9... | collective-permute-start | bytes 589832 | tf_op jit(solution)/shard_map/ppermute | solution.py:596
  166.7 22.0 %collective-permute-start.30 = (bf16[1,192,512]{2,1,0:T(8,128)(2,1)S(1)}, bf16[1,192,512]{2,1,0:T(8,128)(2,1)S(1)}, u32[]{:S(2)}, u32[]{:S(2)}) collective-permute-start(bf16[1,192,512]{2,1,0:T(8,128)(2,1)S(1)} %get-tuple-element.170), channel_id=1, source_target_pairs={{8,0},{16,8},{24,16},{28,24},{20,28},{12,20},{4,12},{0,4},{9,1},{1... | collective-permute-start | bytes 589832 | tf_op jit(solution)/shard_map/ppermute | solution.py:599
  189.4 13.5 %collective-permute-start.31 = (bf16[2,192,512]{2,1,0:T(8,128)(2,1)S(1)}, bf16[2,192,512]{2,1,0:T(8,128)(2,1)S(1)}, u32[]{:S(2)}, u32[]{:S(2)}) collective-permute-start(bf16[2,192,512]{2,1,0:T(8,128)(2,1)S(1)} %get-tuple-element.171), channel_id=1, source_target_pairs={{0,8},{8,16},{16,24},{24,28},{28,20},{20,12},{12,4},{4,0},{1,9},{9... | collective-permute-start | bytes 1179656 | tf_op jit(solution)/shard_map/ppermute | solution.py:596
  190.6 13.3 %collective-permute-start.32 = (bf16[2,192,512]{2,1,0:T(8,128)(2,1)S(1)}, bf16[2,192,512]{2,1,0:T(8,128)(2,1)S(1)}, u32[]{:S(2)}, u32[]{:S(2)}) collective-permute-start(bf16[2,192,512]{2,1,0:T(8,128)(2,1)S(1)} %get-tuple-element.172), channel_id=1, source_target_pairs={{8,0},{16,8},{24,16},{28,24},{20,28},{12,20},{4,12},{0,4},{9,1},{1... | collective-permute-start | bytes 1179656 | tf_op jit(solution)/shard_map/ppermute | solution.py:599
  204.6 13.5 %collective-permute-start.33 = (bf16[2,192,512]{2,1,0:T(8,128)(2,1)S(1)}, bf16[2,192,512]{2,1,0:T(8,128)(2,1)S(1)}, u32[]{:S(2)}, u32[]{:S(2)}) collective-permute-start(bf16[2,192,512]{2,1,0:T(8,128)(2,1)S(1)} %get-tuple-element.173), channel_id=1, source_target_pairs={{0,8},{8,16},{16,24},{24,28},{28,20},{20,12},{12,4},{4,0},{1,9},{9... | collective-permute-start | bytes 1179656 | tf_op jit(solution)/shard_map/ppermute | solution.py:596
  206.0 12.2 %collective-permute-start.34 = (bf16[2,192,512]{2,1,0:T(8,128)(2,1)S(1)}, bf16[2,192,512]{2,1,0:T(8,128)(2,1)S(1)}, u32[]{:S(2)}, u32[]{:S(2)}) collective-permute-start(bf16[2,192,512]{2,1,0:T(8,128)(2,1)S(1)} %get-tuple-element.174), channel_id=1, source_target_pairs={{8,0},{16,8},{24,16},{28,24},{20,28},{12,20},{4,12},{0,4},{9,1},{1... | collective-permute-start | bytes 1179656 | tf_op jit(solution)/shard_map/ppermute | solution.py:599
  218.9 13.9 %collective-permute-start.35 = (bf16[2,192,512]{2,1,0:T(8,128)(2,1)S(1)}, bf16[2,192,512]{2,1,0:T(8,128)(2,1)S(1)}, u32[]{:S(2)}, u32[]{:S(2)}) collective-permute-start(bf16[2,192,512]{2,1,0:T(8,128)(2,1)S(1)} %get-tuple-element.175), channel_id=1, source_target_pairs={{0,8},{8,16},{16,24},{24,28},{28,20},{20,12},{12,4},{4,0},{1,9},{9... | collective-permute-start | bytes 1179656 | tf_op jit(solution)/shard_map/ppermute | solution.py:596
  218.9 15.9 %collective-permute-start.36 = (bf16[2,192,512]{2,1,0:T(8,128)(2,1)S(1)}, bf16[2,192,512]{2,1,0:T(8,128)(2,1)S(1)}, u32[]{:S(2)}, u32[]{:S(2)}) collective-permute-start(bf16[2,192,512]{2,1,0:T(8,128)(2,1)S(1)} %get-tuple-element.176), channel_id=1, source_target_pairs={{8,0},{16,8},{24,16},{28,24},{20,28},{12,20},{4,12},{0,4},{9,1},{1... | collective-permute-start | bytes 1179656 | tf_op jit(solution)/shard_map/ppermute | solution.py:599
  241.5 8.2 %collective-permute-start.38 = (bf16[128,768]{1,0:T(8,128)(2,1)S(1)}, bf16[128,768]{1,0:T(8,128)(2,1)S(1)}, u32[]{:S(2)}, u32[]{:S(2)}) collective-permute-start(bf16[128,768]{1,0:T(8,128)(2,1)S(1)} %dynamic-slice_bitcast_fusion), channel_id=1, source_target_pairs={{0,2},{1,3},{2,0},{3,1},{4,6},{5,7},{6,4},{7,5},{8,10},{9,11},{10,... | collective-permute-start | bytes 589832 | tf_op jit(solution)/shard_map/ppermute | solution.py:657
  249.8 36.4 %all-to-all-start = ((bf16[8,112,768]{2,1,0:T(8,128)(2,1)}), bf16[8,112,768]{2,1,0:T(8,128)(2,1)S(1)}, u32[]{:S(2)}, u32[]{:S(2)}) async-start(bf16[8,112,768]{2,1,0:T(8,128)(2,1)} %get-tuple-element.188), calls=%async_computation | async-start | bytes 2752512 | tf_op jit(solution)/shard_map/all_to_all | solution.py:886
  (56 other events, 467.2 us)
Sparse Core Ops, SparseCore 0:
  10.2 47.9 all-gather.4
  60.4 44.5 all-gather.2
  155.3 86.3 reduce-scatter.1
where the time goes:
time: 297 us; the launch traced here: 296 us
  waiting for transfers between devices  121 us (41%)
  Pallas kernels  83.5 us (28%)
  starting transfers between devices  41 us (14%)
  local copies, waits for them, and re-layouts  19.6 us (7%)
  between operations  14.5 us (5%)
  blocking collectives  8.69 us (3%)
  other arithmetic  6.99 us (2%)
    ppermute x12, waiting for transfers between devices, send_down(): return lax.ppermute(x, self.axis, self.down)  38.2 us
    all_to_all x1, waiting for transfers between devices, shards(): packed = lax.all_to_all(after(packed, far), 'dp', 0, 0, tiled=True)  30.1 us
    pallas_call x5, Pallas kernels, attend_backward(): pl.pallas_call(functools.partial(backward_kernel, first, last, pieces, pa...  30.1 us
    pallas_call x12, Pallas kernels, fused(): pl.pallas_call(body, out_shape=shapes, in_specs=[pl.BlockSpec(memory_spac...  28.1 us
    pallas_call x5, Pallas kernels, attend_forward(): pl.pallas_call(functools.partial(forward_kernel, first, last, pieces, par...  25.4 us
    ppermute x8, waiting for transfers between devices, send_far(): return lax.ppermute(x, self.axis, self.flip_far)  23.4 us
    ppermute x12, waiting for transfers between devices, send_up(): return lax.ppermute(x, self.axis, self.up)  19 us
    ppermute x12, starting transfers between devices, send_down(): return lax.ppermute(x, self.axis, self.down)  14.4 us
  transfers between devices with their start and end apart: 43, of which 27 were waited for; matrix products, arithmetic and copies ran while one was open for 5% of the time, Pallas kernels for 24%

commit v1 on v0

--- a/solution.py
+++ b/solution.py
@@ -9,7 +9,7 @@
 from jax.sharding import PartitionSpec as P
 
 E = 64
-SPARE = 8 << 20
+SPARE = 6 << 20
 TRUNK = 2048
 BLOCK = 128
 EPSILON = 1e-12
@@ -76,7 +76,7 @@
     logit_ref, refs = refs[0], refs[1:]
     if last:
         mix_ref, refs = refs[0], refs[1:]
-    out_ref, m_s, acc_s, q_s, kv_s, prev_s, logit_s, in_sem, out_sem = refs
+    out_ref, m_s, acc_s, kv_s, prev_s, logit_s, in_sem, out_sem = refs
     heads, rows, _ = prev_ref.shape
     count = pieces * heads
 
@@ -99,7 +99,6 @@
 
     for h in range(heads):
         feature = slice(h * E, (h + 1) * E)
-        q_s[h] = q_ref[feature, :].astype(F32).T.astype(BF)
         for p, (keys, values) in enumerate(readers):
             kv_s[p * heads + h, :E, :] = values(feature)
             kv_s[p * heads + h, E : 2 * E, :] = jnp.ones((E, rows), BF)
@@ -122,7 +121,7 @@
             for r0 in range(0, rows, min(rc, rows)):
                 rs = slice(r0, r0 + min(rc, rows))
                 on = block_mask(shard, rows, act_ref, range(r0 // BLOCK, rs.stop // BLOCK))
-                s = contract(q_s[h, rs, :], kv_s[i, 2 * E :, :], 1, 0) + prev_s[i, rs, :].astype(F32)
+                s = contract(q_ref[h, rs, :], kv_s[i, 2 * E :, :], 1, 0) + prev_s[i, rs, :].astype(F32)
                 logit_s[i, rs, :] = (s * on).astype(BF)
                 s = s + (on - 1.0) * (-LOW)
                 m_old = m_s[h, rs, :]
@@ -154,7 +153,7 @@
         outgoing(i).wait()
 
 
-def attend_forward(sid, base, act, q_t, kvs, prev, carry, last, rc=256):
+def attend_forward(sid, base, act, q_n, kvs, prev, carry, last, rc=256):
     heads, rows, length = prev.shape
     first, parted = carry is None, kvs[0].shape[0] == 1
     pieces = 1 if parted else len(kvs)
@@ -162,7 +161,7 @@
     whole = pl.BlockSpec(memory_space=pltpu.VMEM)
     left = pl.BlockSpec(memory_space=pltpu.HBM)
     in_specs = [scalars, scalars, whole] + [whole] * len(kvs) + [left]
-    args = [sid, act, q_t, *kvs, prev]
+    args = [sid, act, q_n, *kvs, prev]
     aliases = {}
     if not first:
         aliases = {len(args): 0}
@@ -181,7 +180,6 @@
         scratch_shapes=[
             pltpu.VMEM((heads, rows, 1), F32),
             pltpu.VMEM((heads, rows, 128), F32),
-            pltpu.VMEM((heads, rows, E), BF),
             pltpu.VMEM((pieces * heads, 3 * E, rows), BF),
             pltpu.VMEM((pieces * heads, rows, rows), BF),
             pltpu.VMEM((pieces * heads, rows, rows), BF),
@@ -197,14 +195,14 @@
 
 
 def backward_kernel(first, last, pieces, parted, base, rc, *refs):
-    sid_ref, act_ref, q_ref, do_ref, aux_ref = refs[:5]
-    readers, refs = read_pieces(pieces, parted, refs[5:])
+    sid_ref, act_ref, q_ref, do_ref, q_s, do_s, aux_ref = refs[:7]
+    readers, refs = read_pieces(pieces, parted, refs[7:])
     prev_ref, up_ref, refs = refs[0], refs[1], refs[2:]
     if not first:
         gq_in, refs = refs[1], refs[2:]
     outputs = 2 if parted else pieces
     pg_ref, gkv_refs = refs[0], refs[1 : 1 + outputs]
-    gq_ref, q_s, do_s, d_s, lse_s, gq_s, p_s, kv_s, gkv_s, prev_s, up_s, pg_s, prev_sem, up_sem, out_sem = refs[1 + outputs :]
+    gq_ref, gq_s, p_s, kv_s, gkv_s, prev_s, up_s, pg_s, prev_sem, up_sem, out_sem = refs[1 + outputs :]
     heads, rows, _ = prev_ref.shape
     count = pieces * heads
 
@@ -231,11 +229,6 @@
 
     for h in range(heads):
         feature = slice(h * E, (h + 1) * E)
-        q_s[h] = q_ref[feature, :].astype(F32).T.astype(BF)
-        do = do_ref[feature, :].astype(F32).T
-        do_s[h] = do.astype(BF)
-        d_s[h] = jnp.sum(do * aux_ref[h, :, :E], axis=1, keepdims=True)
-        lse_s[h] = aux_ref[h, :, E : E + 1]
         gq_s[h] = jnp.zeros((rows, E), F32) if first else gq_in[h]
         for p, (keys, values) in enumerate(readers):
             kv_s[p * heads + h, :E, :] = keys(feature)
@@ -250,15 +243,20 @@
         def _():
             for copy in incoming(i):
                 copy.wait()
-            for r0 in range(0, rows, min(rc, rows)):
-                rs = slice(r0, r0 + min(rc, rows))
-                on = block_mask(shard, rows, act_ref, range(r0 // BLOCK, rs.stop // BLOCK))
+            chunk = min(rc, rows)
+
+            @pl.loop(0, rows // chunk)
+            def _(r):
+                rs = pl.ds(pl.multiple_of(r * chunk, chunk), chunk)
+                blocks = chunk // BLOCK
+                on = block_mask(shard, rows, act_ref, [r * blocks + b for b in range(blocks)])
                 s = contract(q_s[h, rs, :], kv_s[i, :E, :], 1, 0) + prev_s[i, rs, :].astype(F32)
-                weight = jnp.exp(s - lse_s[h, rs, :] + (on - 1.0) * (-LOW))
+                weight = jnp.exp(s - aux_ref[h, rs, E : E + 1] + (on - 1.0) * (-LOW))
                 dp = contract(do_s[h, rs, :], kv_s[i, E:, :], 1, 0)
                 upper = up_s[i, rs, :].astype(F32) * on
-                pg_s[i, rs, :] = (weight * (dp - d_s[h, rs, :]) + upper).astype(BF)
+                pg_s[i, rs, :] = (weight * (dp - aux_ref[h, rs, :1]) + upper).astype(BF)
                 p_s[rs, :] = weight.astype(BF)
+
             gkv_s[i, :E, :] = contract(q_ref[feature, :], pg_s[i], 1, 0).astype(BF)
             gkv_s[i, E:, :] = contract(do_ref[feature, :], p_s[...], 1, 0).astype(BF)
             gq_s[h] += contract(pg_s[i], kv_s[i, :E, :], 1, 1)
@@ -289,15 +287,15 @@
         outgoing(i).wait()
 
 
-def attend_backward(sid, base, act, q_t, do_t, aux, kvs, prev, up, carry, last, rc=256):
+def attend_backward(sid, base, act, q_t, do_t, q_n, do_n, aux, kvs, prev, up, carry, last, rc=256):
     heads, rows, length = prev.shape
     first, parted = carry is None, kvs[0].shape[0] == 1
     pieces = 1 if parted else len(kvs)
     scalars = pl.BlockSpec(memory_space=pltpu.SMEM)
     whole = pl.BlockSpec(memory_space=pltpu.VMEM)
     left = pl.BlockSpec(memory_space=pltpu.HBM)
-    in_specs = [scalars, scalars, whole, whole, whole] + [whole] * len(kvs) + [left, left]
-    args = [sid, act, q_t, do_t, aux, *kvs, prev, up]
+    in_specs = [scalars, scalars] + [whole] * (5 + len(kvs)) + [left, left]
+    args = [sid, act, q_t, do_t, q_n, do_n, aux, *kvs, prev, up]
     aliases = {}
     if not first:
         aliases = {len(args): 0}
@@ -316,10 +314,6 @@
         in_specs=in_specs,
         out_specs=[left] + [whole] * (len(kvs) + 1),
         scratch_shapes=[
-            pltpu.VMEM((heads, rows, E), BF),
-            pltpu.VMEM((heads, rows, E), BF),
-            pltpu.VMEM((heads, rows, 1), F32),
-            pltpu.VMEM((heads, rows, 1), F32),
             pltpu.VMEM((heads, rows, E), F32),
             pltpu.VMEM((rows, rows), BF),
             pltpu.VMEM((pieces * heads, 2 * E, rows), BF),
@@ -371,7 +365,7 @@
 
 def project_kernel(pieces, s_ref, *refs):
     w_refs, x_refs = refs[: pieces + 1], refs[pieces + 1 : pieces + 5]
-    rows_ref, turned_ref, q_ref, kv_ref, w_s = refs[pieces + 5 :]
+    rows_ref, turned_ref, q_ref, natural_ref, kv_ref, w_s = refs[pieces + 5 :]
     share, own = w_refs[0].shape[0], x_refs[0].shape[0]
     width = q_ref.shape[0]
     if pieces == 1:
@@ -387,6 +381,8 @@
     turned_ref[...] = w_s[...].astype(F32).T.astype(BF)
     projected = contract(turned_ref[: 3 * width, :], rows_ref[...], 1, 1)
     q_ref[...] = (projected[:width] * (E ** (-0.5))).astype(BF)
+    for h in range(width // E):
+        natural_ref[h] = (projected[h * E : (h + 1) * E] * (E ** (-0.5))).T.astype(BF)
     kv_ref[0] = projected[width : 2 * width].astype(BF)
     kv_ref[1] = projected[2 * width :].astype(BF)
 
@@ -495,20 +491,25 @@
     sent_ref[2 * own :, :] = tail.astype(BF)
 
 
-def mixed_kernel(s_ref, sent_ref, near_ref, mixed_ref, o_ref, do_ref, grad_w_ref, sums_ref, all_s):
+def mixed_kernel(s_ref, sent_ref, near_ref, mixed_ref, o_ref, bias_ref, aux_ref, do_ref, natural_ref, line_ref, grad_w_ref, sums_ref, all_s):
     near = s_ref[0] % 2
-    rows = all_s.shape[0]
+    rows, model = all_s.shape
     own = rows // 4
     for f in range(2):
         here = slice(f * own, (f + 1) * own)
         all_s[rows_at(2 * f + near, own), :] = sent_ref[here, :]
         all_s[rows_at(2 * f + 1 - near, own), :] = near_ref[here, :]
-    do_ref[...] = contract(o_ref[...], all_s[...], 1, 1).astype(BF)
+    grad = contract(o_ref[...], all_s[...], 1, 1).astype(BF)
+    do_ref[...] = grad
+    for h in range(natural_ref.shape[0]):
+        do = grad[h * E : (h + 1) * E].astype(F32).T
+        natural_ref[h] = do.astype(BF)
+        line_ref[h, :, :E] = jnp.broadcast_to(jnp.sum(do * aux_ref[h, :, :E], axis=1, keepdims=True), (rows, E))
+        line_ref[h, :, E:] = aux_ref[h, :, E:]
     grad_w_ref[...] = contract(mixed_ref[...], all_s[...], 1, 0)
     tail = sent_ref[2 * own :, :].astype(F32) + near_ref[2 * own :, :].astype(F32)
-    sums = tail[:4] + tail[4:8]
-    high = sums.astype(BF).astype(F32)
-    sums_ref[...] = jnp.concatenate([high, sums - high, jnp.zeros((8, sums.shape[1]), F32)], axis=0).astype(BF)
+    rest = jnp.zeros((sums_ref.shape[0] - 5, model), F32)
+    sums_ref[...] = jnp.concatenate([tail[:4] + tail[4:8], bias_ref[...], rest], axis=0)
 
 
 def weight_kernel(s_ref, active_ref, second_ref, low_ref, inner_ref, out_ref):
@@ -529,23 +530,24 @@
         down_out[...] = add(behind_ref[...], down_ref[...])
 
 
-def close_kernel(s_ref, part_ref, up_ref, down_ref, gq_ref, rows_ref, attn_ref, sums_ref, bias_ref, packed_ref, project_ref):
-    members, block, _ = packed_ref.shape
-    width, model = attn_ref.shape
-    share, units = model // members, bias_ref.shape[1] // members
+def close_kernel(s_ref, part_ref, up_ref, down_ref, gq_ref, rows_ref, attn_ref, *refs):
+    outs, project_ref, total_s = refs[:-2], refs[-2], refs[-1]
+    width = gq_ref.shape[0]
     project_ref[:width] = gq_ref[...]
     for w in range(2):
         total = part_ref[w].astype(F32) + up_ref[w].astype(F32) + down_ref[w].astype(F32)
         project_ref[(1 + w) * width : (2 + w) * width] = total.astype(BF)
-    grads = jnp.concatenate([contract(project_ref[...], rows_ref[...], 1, 0), attn_ref[...]], axis=0).T
-    high = bias_ref[...].astype(BF).astype(F32)
-    low = bias_ref[...] - high
-    for i in range(members):
-        packed_ref[i, :share] = grads[i * share : (i + 1) * share].astype(BF)
-        at = slice(i * units, (i + 1) * units)
-        line = jnp.concatenate([high[:, at], low[:, at], jnp.zeros((1, model - 2 * units), F32)], axis=1)
-        tail = [sums_ref[:8].astype(F32), line, jnp.zeros((block - share - 9, model), F32)]
-        packed_ref[i, share:] = jnp.concatenate(tail, axis=0).astype(BF)
+    total_s[...] = jnp.concatenate([contract(project_ref[...], rows_ref[...], 1, 0), attn_ref[...]], axis=0).T
+    count = len(outs) - 1
+    if count == 0:
+        outs[0][...] = total_s[...].astype(BF)
+        return
+    half = outs[0].shape[0]
+    for i in range(2):
+        at = pl.multiple_of(s_ref[count] * 2 * half + i * half, half)
+        outs[i][...] = total_s[pl.ds(at, half), :].astype(BF)
+    for i in range(1, count):
+        outs[1 + i][...] = total_s[rows_at(s_ref[count - i], 2 * half), :].astype(BF)
 
 
 def input_kernel(s_ref, project_ref, turned_ref, mine_ref, other_ref, part_s):
@@ -612,7 +614,7 @@
             functools.partial(join_kernel, self.half), [kind, kind], scalars, behind, ahead, self.up, self.down
         )
         self.up, self.down, self.half = self.ring.send_up(up), self.ring.send_down(down), False
-        return up
+        return up, down
 
 
 def halves(x, axis):
@@ -691,31 +693,6 @@
     place = tensor_index.astype(jnp.int32).reshape(1)
     gains = jnp.stack([norm1_gain, norm1_shift, norm2_gain, norm2_shift])
 
-    pack_in = jnp.concatenate([w_ffn_in, ffn_bias[:, None]], axis=1)
-    pack = jnp.concatenate([w_query, w_key, w_value, w_attn_out.T], axis=1)
-    pack, pack_in, gains = lax.optimization_barrier((pack, pack_in, gains))
-    pack_in = lax.all_gather(pack_in, "dp", axis=0, tiled=True)
-    w_out = lax.all_gather(w_ffn_out, "dp", axis=0, tiled=True)
-    if by_ring:
-        pieces = all_ring.gather(pack)
-        owners = [o for group in all_ring.groups() for o in group]
-        owners = all_ring.members(data_index, owners)
-    else:
-        pieces = list(spread_gather(pack, "dp", nd).reshape(2, model // 2, 4 * width))
-        owners = jnp.zeros((1,), jnp.int32)
-    place = jnp.concatenate([place, owners])
-    near = quad.send_near(inputs)
-    rows_of_four = [inputs, near, quad.send_far(inputs), quad.send_far(near)]
-    rows_all, turned, q_t, kv_own = fused(
-        functools.partial(project_kernel, len(pieces) - 1),
-        [((rows, model), BF), ((4 * width, model), BF), ((width, rows), BF), ((2, width, rows), BF)],
-        place,
-        *map(apart, pieces),
-        *map(apart, rows_of_four),
-        scratch=[((model, 4 * width), BF)],
-    )
-    out_own = turned[3 * width :]
-
     seg = lax.dynamic_slice_in_dim(token_segment, tree_index * length, length, 0)[::BLOCK]
     parents = lax.dynamic_slice_in_dim(segment_parent, tree_index, 1, 0)[0]
     seg_rows = lax.dynamic_slice_in_dim(seg, local_index * nb, nb, 0)
@@ -728,12 +705,39 @@
         | (seg[None, :] == two[:, None])
     )
     act = act.astype(jnp.int32).reshape(-1)
-
-    prev = apart(jnp.transpose(prev_logits, (1, 0, 2)))
-    up_grad = apart(jnp.transpose(logit_grad, (1, 0, 2)))
     groups = ring.groups()
     order = [o for group in groups for o in group]
     sid = ring.members(local_index, order)
+
+    pack_in = jnp.concatenate([w_ffn_in, ffn_bias[:, None]], axis=1)
+    w_out = lax.all_gather(w_ffn_out, "dp", axis=0, tiled=True)
+    pack = jnp.concatenate([w_query, w_key, w_value, w_attn_out.T], axis=1)
+    if by_ring:
+        pieces = all_ring.gather(pack)
+        pieces[2], pack_in = lax.optimization_barrier((pieces[2], pack_in))
+        owners = [o for group in all_ring.groups() for o in group]
+        owners = all_ring.members(data_index, owners)
+    else:
+        pieces = list(spread_gather(pack, "dp", nd).reshape(2, model // 2, 4 * width))
+        owners = jnp.zeros((1,), jnp.int32)
+    hidden_units = w_ffn_in.shape[1]
+    pack_in = lax.all_gather(pack_in, "dp", axis=0, tiled=True)
+    place = jnp.concatenate([place, owners])
+    place, act, sid, gains = lax.optimization_barrier((place, act, sid, gains))
+    near = quad.send_near(inputs)
+    rows_of_four = [inputs, near, quad.send_far(inputs), quad.send_far(near)]
+    rows_all, turned, q_t, q_n, kv_own = fused(
+        functools.partial(project_kernel, len(pieces) - 1),
+        [((rows, model), BF), ((4 * width, model), BF), ((width, rows), BF), ((heads, rows, E), BF), ((2, width, rows), BF)],
+        place,
+        *map(apart, pieces),
+        *map(apart, rows_of_four),
+        scratch=[((model, 4 * width), BF)],
+    )
+    out_own = turned[3 * width :]
+
+    prev = apart(jnp.transpose(prev_logits, (1, 0, 2)))
+    up_grad = apart(jnp.transpose(logit_grad, (1, 0, 2)))
     held = [[kv_own]]
     going_up = going_down = kv_own
     state = None
@@ -748,7 +752,7 @@
                 going_up, going_down = ring.send_up(going_up), ring.send_down(going_down)
                 held.append([going_up, going_down])
         result = attend_forward(
-            sid, order.index(group[0]), act, q_t, held[step], prev, state, last, 512
+            sid, order.index(group[0]), act, q_n, held[step], prev, state, last, 512
         )
         state = (result[0], result[-1])
         if step == 0:
@@ -781,7 +785,7 @@
         place,
         mine,
         quad.send_far(mine),
-        first_n,
+        apart(first_n),
         apart(out_grad),
         apart(out_grad_far),
         gains,
@@ -806,7 +810,7 @@
         active,
         second_all,
         low,
-        after(inner, mine),
+        inner,
     )
     far = after(far, weight_grads)
     weight_grads = lax.psum_scatter(weight_grads, "dp", scatter_dimension=0, tiled=True)
@@ -818,60 +822,93 @@
         mine,
         far,
         second,
-        first_n,
-        first_r,
+        apart(first_n),
+        apart(first_r),
         sums,
         gains,
     )
     received = quad.send_near(sent)
-    grad_mixed, grad_w_attn, sums = fused(
+    grad_mixed, grad_mixed_n, aux, grad_w_attn, sums = fused(
         mixed_kernel,
-        [((width, rows), BF), ((width, model), F32), ((16, model), BF)],
+        [
+            ((width, rows), BF),
+            ((heads, rows, E), BF),
+            ((heads, rows, 128), F32),
+            ((width, model), F32),
+            ((8, model), F32),
+        ],
         place,
         sent,
         received,
-        mixed,
-        out_own,
+        apart(mixed),
+        apart(out_own),
+        grad_bias,
+        apart(aux),
         scratch=[((rows, model), BF)],
     )
+
+    doublings = iter([1 << i for i in range((nd - 1).bit_length())])
+
+    def sums_step(sums):
+        bit = next(doublings, None)
+        if bit is None:
+            return sums
+        return sums + lax.ppermute(sums, "dp", [(i, i ^ bit) for i in range(nd)])
 
     state = None
     total_kv = RingSum(ring)
-    for step, group in reversed(list(enumerate(groups))):
+    steps = list(reversed(range(1, len(groups))))
+    steps.append(0)
+    for turn, step in enumerate(steps):
         result = attend_backward(
             sid,
-            order.index(group[0]),
+            order.index(groups[step][0]),
             act,
             q_t,
             grad_mixed,
+            q_n,
+            grad_mixed_n,
             aux,
             [apart(kv) for kv in held[step]],
             prev,
             up_grad,
             state,
-            step == 0,
-            256,
+            turn + 1 == len(steps),
+            512,
         )
         state = (result[0], result[-1])
-        if step + 1 == len(groups):
+        if step == 0:
+            part = result[1]
+        elif step + 1 == len(groups):
             total_kv.first(*result[1:-1])
-        elif step > 0:
-            total_kv.step(place, *result[1:-1])
-    prev_grad, part, grad_query = result
-
-    packed, grad_project = fused(
+        else:
+            sums = sums_step(sums)
+            total_kv.step(after(place, sums), *result[1:-1])
+    prev_grad, grad_query = result[0], result[-1]
+    for _ in range(nd):
+        sums = sums_step(sums)
+    grad_w_out, grad_w_in = weight_grads[:, :model].astype(F32), weight_grads[:, model:].astype(F32)
+
+    if by_ring:
+        shapes = [((share // 2, 4 * width), BF)] * 2 + [((share, 4 * width), BF)] * (nd - 1)
+    else:
+        shapes = [((model, 4 * width), BF)]
+    *parts, grad_project = fused(
         close_kernel,
-        [((nd, share + 16, model), BF), ((3 * width, rows), BF)],
+        shapes + [((3 * width, rows), BF)],
         place,
         part,
         total_kv.up,
         total_kv.down,
         grad_query,
         rows_all,
-        grad_w_attn,
-        sums,
-        grad_bias,
-    )
+        apart(grad_w_attn),
+        scratch=[((model, 4 * width), F32)],
+    )
+    if by_ring:
+        last_sum = RingSum(all_ring)
+        last_sum.first(parts[0], parts[1])
+        grad_project = after(grad_project, last_sum.up, last_sum.down)
     mine, other = fused(
         input_kernel,
         [(pair, BF), (pair, BF)],
@@ -880,32 +917,36 @@
         apart(turned),
         scratch=[((rows, model), F32)],
     )
-    mine, packed = lax.optimization_barrier((add(mine, quad.send_near(other)).reshape(2, own, model), packed))
+    mine = add(mine, quad.send_near(other)).reshape(2, own, model)
     far = quad.send_far(lax.dynamic_index_in_dim(mine, 1 - quad.far, 0, keepdims=False))
     kept = lax.dynamic_index_in_dim(mine, quad.far, 0, keepdims=False)
-    packed = lax.all_to_all(after(packed, far), "dp", 0, 0, tiled=True)
     grad_inputs = grad_first + (kept.astype(F32) + far.astype(F32))
-    weight_grads = weight_grads.astype(F32)
-    packed = jnp.sum(packed.astype(F32), axis=0)
-    norms = packed[share : share + 4] + packed[share + 4 : share + 8]
-    units = grad_bias.shape[1] // nd
-    grad_bias = packed[share + 8, :units] + packed[share + 8, units : 2 * units]
+    if by_ring:
+        parts[3] = after(parts[3], grad_w_out, grad_w_in)
+        for i in range(2, nd, 2):
+            if i == 4:
+                parts = lax.optimization_barrier((*parts, far))[:-1]
+            last_sum.step(place, apart(parts[i + 1]), apart(parts[i]))
+        grads = parts[-1].astype(F32) + (last_sum.up.astype(F32) + last_sum.down.astype(F32))
+    else:
+        grads = group_sum(parts[0], "dp", nd)
+    grad_bias = lax.dynamic_slice_in_dim(sums[4], data_index * (hidden_units // nd), hidden_units // nd, 0)
     return (
         output,
         jnp.transpose(logits, (1, 0, 2)),
         grad_inputs,
         jnp.transpose(prev_grad, (1, 0, 2)),
-        packed[:share, :width],
-        packed[:share, width : 2 * width],
-        packed[:share, 2 * width : 3 * width],
-        packed[:share, 3 * width :].T,
-        weight_grads[:, model:],
+        grads[:, :width],
+        grads[:, width : 2 * width],
+        grads[:, 2 * width : 3 * width],
+        grads[:, 3 * width :].T,
+        grad_w_in,
         grad_bias,
-        weight_grads[:, :model],
-        norms[0],
-        norms[1],
-        norms[2],
-        norms[3],
+        grad_w_out,
+        sums[0],
+        sums[1],
+        sums[2],
+        sums[3],
     )
 
 

time: 297 us -> 275 us (0.926)
  waiting for transfers between devices: 121 us -> 90.9 us
  starting transfers between devices: 41 us -> 55.8 us
  local copies, waits for them, and re-layouts: 19.6 us -> 12.2 us
    all_to_all x1 -> x0, waiting for transfers between devices: 30.1 us -> none  [shards(): packed = lax.all_to_all(after(packed, far), 'dp', 0, 0, tiled=True)]
    ppermute x0 -> x3, waiting for transfers between devices: none -> 11.8 us  [sums_step(): return sums + lax.ppermute(sums, 'dp', [(i, i ^ bit) for i in range(nd)])]
    ppermute x12 -> x16, waiting for transfers between devices: 38.2 us -> 29.9 us  [send_down(): return lax.ppermute(x, self.axis, self.down)]
    ppermute x12 -> x16, starting transfers between devices: 14.4 us -> 22.2 us  [send_down(): return lax.ppermute(x, self.axis, self.down)]
    unnamed x92 -> x78, local copies, waits for them, and re-layouts: 11.7 us -> 5.61 us
    ppermute x12 -> x16, starting transfers between devices: 13.1 us -> 17.5 us  [send_up(): return lax.ppermute(x, self.axis, self.up)]
    ppermute x0 -> x3, starting transfers between devices: none -> 4.35 us  [sums_step(): return sums + lax.ppermute(sums, 'dp', [(i, i ^ bit) for i in range(nd)])]
    all_to_all x1 -> x0, starting transfers between devices: 3.57 us -> none  [shards(): packed = lax.all_to_all(after(packed, far), 'dp', 0, 0, tiled=True)]
  transfers between devices with their start and end apart: 43 -> 53, of which waited for: 27 -> 33; matrix products, arithmetic and copies ran while one was open for 5% -> 5% of each run, Pallas kernels for 24% -> 25%
where the time goes in v1:
time: 275 us; the launch traced here: 274 us
  waiting for transfers between devices  90.9 us (33%)
  Pallas kernels  85.3 us (31%)
  starting transfers between devices  55.8 us (20%)
  between operations  14.5 us (5%)
  local copies, waits for them, and re-layouts  12.2 us (4%)
  other arithmetic  8.08 us (3%)
  blocking collectives  7.4 us (3%)
    pallas_call x15, Pallas kernels, fused(): pl.pallas_call(body, out_shape=shapes, in_specs=[pl.BlockSpec(memory_spac...  31.6 us
    ppermute x16, waiting for transfers between devices, send_down(): return lax.ppermute(x, self.axis, self.down)  29.9 us
    pallas_call x5, Pallas kernels, attend_backward(): pl.pallas_call(functools.partial(backward_kernel, first, last, pieces, pa...  28.5 us
    pallas_call x5, Pallas kernels, attend_forward(): pl.pallas_call(functools.partial(forward_kernel, first, last, pieces, par...  25.2 us
    ppermute x16, starting transfers between devices, send_down(): return lax.ppermute(x, self.axis, self.down)  22.2 us
    ppermute x8, waiting for transfers between devices, send_far(): return lax.ppermute(x, self.axis, self.flip_far)  21.9 us
    ppermute x16, starting transfers between devices, send_up(): return lax.ppermute(x, self.axis, self.up)  17.5 us
    ppermute x16, waiting for transfers between devices, send_up(): return lax.ppermute(x, self.axis, self.up)  16.9 us
  transfers between devices with their start and end apart: 53, of which 33 were waited for; matrix products, arithmetic and copies ran while one was open for 5% of the time, Pallas kernels for 25%

profile of v1, /device:TPU:0, one launch (start us, length us, event | category | flops | bytes accessed | tf_op | source)
XLA Modules:
  0.0 274.2 jit_solution(1626757549312916921)
XLA Ops:
  9.8 3.0 %collective-permute-start.1 = (bf16[96,768]{1,0:T(8,128)(2,1)S(1)}, bf16[96,768]{1,0:T(8,128)(2,1)S(1)}, u32[]{:S(2)}, u32[]{:S(2)}) collective-permute-start(bf16[96,768]{1,0:T(8,128)(2,1)S(1)} %pad_maximum_fusion.1.refs_0_), channel_id=1, source_target_pairs={{8,0},{16,8},{24,16},{28,24},{20,28},{12,20},{4,12},{0,4},{9,1},{1... | collective-permute-start | bytes 442376 | tf_op jit(solution)/shard_map/ppermute | solution.py:601
  24.1 2.5 collective-permute-start.5
  33.4 2.6 collective-permute-done.10.refs_12_
  38.0 2.6 shard_map.298
  44.0 5.4 %shard_map.299 = (bf16[3,512,4096]{2,1,0:T(8,128)(2,1)}, f32[3,512,128]{2,1,0:T(8,128)S(1)}) custom-call(s32[8]{0:T(128)S(1)} %get-tuple-element.129.refs_0_, s32[128]{0:T(128)S(1)} %reshape.59.refs_1_, bf16[3,512,64]{2,1,0:T(8,128)(2,1)S(1)} %get-tuple-element.132.refs_2_.refs_4_, bf16[2,192,512]{2,1,0:T(8,128)(2,1)S(1)} %get-tuple-element.133.refs_3_.refs_7_, ...), custom_call_target="tpu_custom_call" | custom-call | flops 201326592 | bytes 3145728 | tf_op jit(solution)/shard_map/pallas_call | solution.py:175
  49.4 7.6 %collective-permute-done.12.refs_4_.refs_8_ = bf16[2,192,512]{2,1,0:T(8,128)(2,1)S(1)} collective-permute-done((bf16[2,192,512]{2,1,0:T(8,128)(2,1)S(1)}, bf16[2,192,512]{2,1,0:T(8,128)(2,1)S(1)}, u32[]{:S(2)}, u32[]{:S(2)}) %collective-permute-start.12) | collective-permute-done | bytes 393248 | tf_op jit(solution)/shard_map/ppermute | solution.py:601
  60.6 8.5 %shard_map.300 = (bf16[3,512,4096]{2,1,0:T(8,128)(2,1)}, f32[3,512,128]{2,1,0:T(8,128)S(1)}) custom-call(s32[8]{0:T(128)S(1)} %get-tuple-element.129.refs_0_, s32[128]{0:T(128)S(1)} %reshape.59.refs_1_, bf16[3,512,64]{2,1,0:T(8,128)(2,1)S(1)} %get-tuple-element.132.refs_2_.refs_4_, ...), custom_call_target="tpu_custom_call", output_to_operand_aliasing={{0}: (6, {})} | custom-call | flops 402653184 | bytes 6291456 | tf_op jit(solution)/shard_map/pallas_call | solution.py:175
  75.0 6.0 %shard_map.301 = (bf16[3,512,4096]{2,1,0:T(8,128)(2,1)}, f32[3,512,128]{2,1,0:T(8,128)S(1)}) custom-call(s32[8]{0:T(128)S(1)} %get-tuple-element.129.refs_0_, s32[128]{0:T(128)S(1)} %reshape.59.refs_1_, bf16[3,512,64]{2,1,0:T(8,128)(2,1)S(1)} %get-tuple-element.132.refs_2_.refs_4_, ...), custom_call_target="tpu_custom_call", output_to_operand_aliasing={{0}: (6, {})} | custom-call | flops 402653184 | bytes 6291456 | tf_op jit(solution)/shard_map/pallas_call | solution.py:175
  81.1 2.4 collective-permute-done.16.refs_3_.refs_7_
  87.8 3.0 %shard_map.302 = (bf16[3,512,4096]{2,1,0:T(8,128)(2,1)}, f32[3,512,128]{2,1,0:T(8,128)S(1)}) custom-call(s32[8]{0:T(128)S(1)} %get-tuple-element.129.refs_0_, s32[128]{0:T(128)S(1)} %reshape.59.refs_1_, bf16[3,512,64]{2,1,0:T(8,128)(2,1)S(1)} %get-tuple-element.132.refs_2_.refs_4_, ...), custom_call_target="tpu_custom_call", output_to_operand_aliasing={{0}: (6, {})} | custom-call | flops 402653184 | bytes 6291456 | tf_op jit(solution)/shard_map/pallas_call | solution.py:175
  90.8 3.6 %collective-permute-done.19.refs_4_.refs_8_ = bf16[1,192,512]{2,1,0:T(8,128)(2,1)S(1)} collective-permute-done((bf16[1,192,512]{2,1,0:T(8,128)(2,1)S(1)}, bf16[1,192,512]{2,1,0:T(8,128)(2,1)S(1)}, u32[]{:S(2)}, u32[]{:S(2)}) %collective-permute-start.19) | collective-permute-done | bytes 196640 | tf_op jit(solution)/shard_map/ppermute | solution.py:601
  94.9 2.2 shard_map.303
  99.6 7.4 %all_gather.9.mixed_ref = bf16[768,512]{1,0:T(8,128)(2,1)S(1)} all-gather(bf16[192,512]{1,0:T(8,128)(2,1)S(1)} %get-tuple-element.151.mixed_ref), channel_id=1, replica_groups=mesh['dp'=8,'tensor'=4] {'tensor'}, dimensions={0}, use_global_device_ids=true | all-gather | bytes 983040 | tf_op jit(solution)/shard_map/all_gather | solution.py:767
  107.0 5.7 %shard_map.304 = (bf16[512,768]{1,0:T(8,128)(2,1)S(1)}, bf16[512,768]{1,0:T(8,128)(2,1)S(1)}, f32[512,768]{1,0:T(8,128)S(1)}, f32[256,768]{1,0:T(8,128)S(1)}, f3...) custom-call(s32[9]{0:T(128)S(1)} %pad_add_fusion.s_ref, ...), custom_call_target="tpu_custom_call" | custom-call | bytes 1048576 | tf_op jit(solution)/shard_map/pallas_call | solution.py:339
  116.7 9.6 %collective-permute-done.24.b_ref = bf16[256,768]{1,0:T(8,128)(2,1)S(1)} collective-permute-done((bf16[256,768]{1,0:T(8,128)(2,1)S(1)}, bf16[256,768]{1,0:T(8,128)(2,1)S(1)}, u32[]{:S(2)}, u32[]{:S(2)}) %collective-permute-start.24) | collective-permute-done | bytes 393248 | tf_op jit(solution)/shard_map/ppermute | solution.py:659
  126.3 2.7 shard_map.305
  130.7 3.5 %shard_map.306 = (bf16[512,768]{1,0:T(8,128)(2,1)S(1)}, bf16[512,768]{1,0:T(8,128)(2,1)S(1)}, f32[1,768]{1,0:T(1,128)S(1)}, bf16[256,768]{1,0:T(8,128)(2,1)S(1)}, bf16[256,768]{1,0:T(8,128)(2,1)S(1)}) custom-call(s32[9]{0:T(128)S(1)} %pad_add_fusion.s_ref, bf16[256,768]{1,0:T(8,128)(2,1)S(1)} %get-tuple-element.167.low_ref, ...), custom_call_target="tpu_custom_call" | custom-call | bytes 1048576 | tf_op jit(solution)/shard_map/pallas_call | solution.py:339
  134.2 3.4 %shard_map.307 = bf16[768,1536]{1,0:T(8,128)(2,1)} custom-call(s32[9]{0:T(128)S(1)} %pad_add_fusion.s_ref, bf16[512,768]{1,0:T(8,128)(2,1)S(1)} %get-tuple-element.171.active_ref, bf16[512,768]{1,0:T(8,128)(2,1)S(1)} %get-tuple-element.172.second_ref, bf16[512,768]{1,0:T(8,128)(2,1)S(1)} %get-tuple-element.173.low_ref, ...), custom_call_target="tpu_custom_call" | custom-call | bytes 1048576 | tf_op jit(solution)/shard_map/pallas_call | solution.py:339
  141.4 9.4 %collective-permute-done.27.b_ref = bf16[256,768]{1,0:T(8,128)(2,1)S(1)} collective-permute-done((bf16[256,768]{1,0:T(8,128)(2,1)S(1)}, bf16[256,768]{1,0:T(8,128)(2,1)S(1)}, u32[]{:S(2)}, u32[]{:S(2)}) %collective-permute-start.27) | collective-permute-done | bytes 393248 | tf_op jit(solution)/shard_map/ppermute | solution.py:659
  157.5 2.6 shard_map.310
  160.1 4.3 %collective-permute-start.32 = (bf16[1,192,512]{2,1,0:T(8,128)(2,1)S(1)}, bf16[1,192,512]{2,1,0:T(8,128)(2,1)S(1)}, u32[]{:S(2)}, u32[]{:S(2)}) collective-permute-start(bf16[1,192,512]{2,1,0:T(8,128)(2,1)S(1)} %get-tuple-element.205), channel_id=1, source_target_pairs={{0,8},{8,16},{16,24},{24,28},{28,20},{20,12},{12,4},{4,0},{1,9},{9... | collective-permute-start | bytes 589832 | tf_op jit(solution)/shard_map/ppermute | solution.py:598
  165.5 3.4 %shard_map.311 = (bf16[3,512,4096]{2,1,0:T(8,128)(2,1)}, bf16[2,192,512]{2,1,0:T(8,128)(2,1)S(1)}, bf16[2,192,512]{2,1,0:T(8,128)(2,1)S(1)}, f32[3,512,64]{2,1,0:T(8,128)S(1)}) custom-call(s32[8]{0:T(128)S(1)} %get-tuple-element.129.refs_0_, s32[128]{0:T(128)S(1)} %reshape.59.refs_1_, ...), custom_call_target="tpu_custom_call", output_to_operand_aliasing={{0}: (11, {})} | custom-call | flops 1006632960 | bytes 9437184 | tf_op jit(solution)/shard_map/pallas_call | solution.py:311
  169.0 3.4 %collective-permute-done.29 = f32[8,768]{1,0:T(8,128)S(1)} collective-permute-done((f32[8,768]{1,0:T(8,128)S(1)}, f32[8,768]{1,0:T(8,128)S(1)}, u32[]{:S(2)}, u32[]{:S(2)}) %collective-permute-start.29) | collective-permute-done | bytes 24608 | tf_op jit(solution)/shard_map/ppermute | solution.py:856
  173.3 9.5 %collective-permute-done.33.down_ref = bf16[1,192,512]{2,1,0:T(8,128)(2,1)S(1)} collective-permute-done((bf16[1,192,512]{2,1,0:T(8,128)(2,1)S(1)}, bf16[1,192,512]{2,1,0:T(8,128)(2,1)S(1)}, u32[]{:S(2)}, u32[]{:S(2)}) %collective-permute-start.33) | collective-permute-done | bytes 196640 | tf_op jit(solution)/shard_map/ppermute | solution.py:601
  186.9 6.9 %shard_map.312 = (bf16[3,512,4096]{2,1,0:T(8,128)(2,1)}, bf16[2,192,512]{2,1,0:T(8,128)(2,1)S(1)}, bf16[2,192,512]{2,1,0:T(8,128)(2,1)S(1)}, f32[3,512,64]{2,1,0:T(8,128)S(1)}) custom-call(s32[8]{0:T(128)S(1)} %get-tuple-element.129.refs_0_, s32[128]{0:T(128)S(1)} %reshape.59.refs_1_, ...), custom_call_target="tpu_custom_call", output_to_operand_aliasing={{0}: (11, {})} | custom-call | flops 1006632960 | bytes 9437184 | tf_op jit(solution)/shard_map/pallas_call | solution.py:311
  202.8 9.4 %shard_map.313 = (bf16[3,512,4096]{2,1,0:T(8,128)(2,1)}, bf16[2,192,512]{2,1,0:T(8,128)(2,1)S(1)}, bf16[2,192,512]{2,1,0:T(8,128)(2,1)S(1)}, f32[3,512,64]{2,1,0:T(8,128)S(1)}) custom-call(s32[8]{0:T(128)S(1)} %get-tuple-element.129.refs_0_, s32[128]{0:T(128)S(1)} %reshape.59.refs_1_, ...), custom_call_target="tpu_custom_call", output_to_operand_aliasing={{0}: (11, {})} | custom-call | flops 1006632960 | bytes 9437184 | tf_op jit(solution)/shard_map/pallas_call | solution.py:311
  212.3 6.2 %collective-permute-done.31 = f32[8,768]{1,0:T(8,128)S(1)} collective-permute-done((f32[8,768]{1,0:T(8,128)S(1)}, f32[8,768]{1,0:T(8,128)S(1)}, u32[]{:S(2)}, u32[]{:S(2)}) %collective-permute-start.31) | collective-permute-done | bytes 24608 | tf_op jit(solution)/shard_map/ppermute | solution.py:856
  221.3 6.2 %shard_map.314 = (bf16[3,512,4096]{2,1,0:T(8,128)(2,1)}, bf16[2,192,512]{2,1,0:T(8,128)(2,1)S(1)}, bf16[192,512]{1,0:T(8,128)(2,1)S(1)}) custom-call(s32[8]{0:T(128)S(1)} %get-tuple-element.129.refs_0_, s32[128]{0:T(128)S(1)} %reshape.59.refs_1_, bf16[192,512]{1,0:T(8,128)(2,1)S(1)} %get-tuple-element.135.refs_2_, ...), custom_call_target="tpu_custom_call", output_to_operand_aliasing={{0}: (10, {})} | custom-call | flops 503316480 | bytes 4718592 | tf_op jit(solution)/shard_map/pallas_call | solution.py:311
  232.7 2.3 collective-permute-done.40.up_ref
  237.0 2.3 shard_map.319
  248.4 3.3 %collective-permute-done.44.up_ref = bf16[96,768]{1,0:T(8,128)(2,1)S(1)} collective-permute-done((bf16[96,768]{1,0:T(8,128)(2,1)S(1)}, bf16[96,768]{1,0:T(8,128)(2,1)S(1)}, u32[]{:S(2)}, u32[]{:S(2)}) %collective-permute-start.44) | collective-permute-done | bytes 147488 | tf_op jit(solution)/shard_map/ppermute | solution.py:598
  263.4 2.3 collective-permute-done.48
  (215 shorter events, 106.4 us)
Async XLA Ops:
  7.2 99.8 %all-gather.5.cloned.1.call-start = ((), (), s32[]{:S(2)}) async-start(), calls=%async_computation.2 | async-start | bytes 1327104 | tf_op jit(solution)/shard_map/all_gather | solution.py:713
  7.9 99.1 %all-gather.3.cloned.1.call-start = ((), (), s32[]{:S(2)}) async-start(), calls=%async_computation.1 | async-start | bytes 1548288 | tf_op jit(solution)/shard_map/all_gather | solution.py:724
  9.8 7.6 %collective-permute-start.1 = (bf16[96,768]{1,0:T(8,128)(2,1)S(1)}, bf16[96,768]{1,0:T(8,128)(2,1)S(1)}, u32[]{:S(2)}, u32[]{:S(2)}) collective-permute-start(bf16[96,768]{1,0:T(8,128)(2,1)S(1)} %pad_maximum_fusion.1.refs_0_), channel_id=1, source_target_pairs={{8,0},{16,8},{24,16},{28,24},{20,28},{12,20},{4,12},{0,4},{9,1},{1... | collective-permute-start | bytes 442376 | tf_op jit(solution)/shard_map/ppermute | solution.py:601
  13.0 17.4 %collective-permute-start.8 = (bf16[128,768]{1,0:T(8,128)(2,1)}, bf16[128,768]{1,0:T(8,128)(2,1)S(1)}, u32[]{:S(2)}, u32[]{:S(2)}) collective-permute-start(bf16[128,768]{1,0:T(8,128)(2,1)} %refs_9_.1), channel_id=1, source_target_pairs={{0,1},{1,0},{2,3},{3,2},{4,5},{5,4},{6,7},{7,6},{8,9},{9,8},{10,11... | collective-permute-start | bytes 589832 | tf_op jit(solution)/shard_map/ppermute | solution.py:656
  13.0 20.5 %collective-permute-start.9 = (bf16[128,768]{1,0:T(8,128)(2,1)}, bf16[128,768]{1,0:T(8,128)(2,1)S(1)}, u32[]{:S(2)}, u32[]{:S(2)}) collective-permute-start(bf16[128,768]{1,0:T(8,128)(2,1)} %refs_9_.1), channel_id=1, source_target_pairs={{0,2},{1,3},{2,0},{3,1},{4,6},{5,7},{6,4},{7,5},{8,10},{9,11},{10,... | collective-permute-start | bytes 589832 | tf_op jit(solution)/shard_map/ppermute | solution.py:659
  19.0 7.6 %collective-permute-start.2 = (bf16[96,768]{1,0:T(8,128)(2,1)S(1)}, bf16[96,768]{1,0:T(8,128)(2,1)S(1)}, u32[]{:S(2)}, u32[]{:S(2)}) collective-permute-start(bf16[96,768]{1,0:T(8,128)(2,1)S(1)} %collective-permute-done.refs_1_), channel_id=1, source_target_pairs={{0,8},{8,16},{16,24},{24,28},{28,20},{20,12},{12,4},{4,0},{1,9},{9... | collective-permute-start | bytes 442376 | tf_op jit(solution)/shard_map/ppermute | solution.py:598
  22.0 221.2 %reduce-scatter.2.cloned.1.call-start = ((), (), s32[]{:S(2)}) async-start(), calls=%async_computation.3 | async-start | bytes 2654208 | tf_op jit(solution)/shard_map/reduce_scatter | solution.py:816
  40.7 16.4 %collective-permute-start.12 = (bf16[2,192,512]{2,1,0:T(8,128)(2,1)S(1)}, bf16[2,192,512]{2,1,0:T(8,128)(2,1)S(1)}, u32[]{:S(2)}, u32[]{:S(2)}) collective-permute-start(bf16[2,192,512]{2,1,0:T(8,128)(2,1)S(1)} %get-tuple-element.133.refs_3_.refs_7_), channel_id=1, source_target_pairs={{8,0},{16,8},{24,16},{28,24},{20,28},{12,20},{4,12},{0,4},{9,1},{1... | collective-permute-start | bytes 1179656 | tf_op jit(solution)/shard_map/ppermute | solution.py:601
  42.7 14.3 %collective-permute-start.11 = (bf16[2,192,512]{2,1,0:T(8,128)(2,1)S(1)}, bf16[2,192,512]{2,1,0:T(8,128)(2,1)S(1)}, u32[]{:S(2)}, u32[]{:S(2)}) collective-permute-start(bf16[2,192,512]{2,1,0:T(8,128)(2,1)S(1)} %get-tuple-element.133.refs_3_.refs_7_), channel_id=1, source_target_pairs={{0,8},{8,16},{16,24},{24,28},{28,20},{20,12},{12,4},{4,0},{1,9},{9... | collective-permute-start | bytes 1179656 | tf_op jit(solution)/shard_map/ppermute | solution.py:598
  42.7 6.7 %collective-permute-start.13 = (bf16[128,768]{1,0:T(8,128)(2,1)}, bf16[128,768]{1,0:T(8,128)(2,1)S(1)}, u32[]{:S(2)}, u32[]{:S(2)}) collective-permute-start(bf16[128,768]{1,0:T(8,128)(2,1)} %cot_own.1), channel_id=1, source_target_pairs={{0,2},{1,3},{2,0},{3,1},{4,6},{5,7},{6,4},{7,5},{8,10},{9,11},{10,... | collective-permute-start | bytes 589832 | tf_op jit(solution)/shard_map/ppermute | solution.py:659
  57.0 12.1 %collective-permute-start.14 = (bf16[2,192,512]{2,1,0:T(8,128)(2,1)S(1)}, bf16[2,192,512]{2,1,0:T(8,128)(2,1)S(1)}, u32[]{:S(2)}, u32[]{:S(2)}) collective-permute-start(bf16[2,192,512]{2,1,0:T(8,128)(2,1)S(1)} %collective-permute-done.11.refs_3_.refs_7_), channel_id=1, source_target_pairs={{0,8},{8,16},{16,24},{24,28},{28,20},{20,12},{12,4},{4,0},{1,9},{9... | collective-permute-start | bytes 1179656 | tf_op jit(solution)/shard_map/ppermute | solution.py:598
  59.2 10.0 %collective-permute-start.15 = (bf16[2,192,512]{2,1,0:T(8,128)(2,1)S(1)}, bf16[2,192,512]{2,1,0:T(8,128)(2,1)S(1)}, u32[]{:S(2)}, u32[]{:S(2)}) collective-permute-start(bf16[2,192,512]{2,1,0:T(8,128)(2,1)S(1)} %collective-permute-done.12.refs_4_.refs_8_), channel_id=1, source_target_pairs={{8,0},{16,8},{24,16},{28,24},{20,28},{12,20},{4,12},{0,4},{9,1},{1... | collective-permute-start | bytes 1179656 | tf_op jit(solution)/shard_map/ppermute | solution.py:601
  69.2 14.3 %collective-permute-start.16 = (bf16[2,192,512]{2,1,0:T(8,128)(2,1)S(1)}, bf16[2,192,512]{2,1,0:T(8,128)(2,1)S(1)}, u32[]{:S(2)}, u32[]{:S(2)}) collective-permute-start(bf16[2,192,512]{2,1,0:T(8,128)(2,1)S(1)} %collective-permute-done.14.refs_3_.refs_7_), channel_id=1, source_target_pairs={{0,8},{8,16},{16,24},{24,28},{28,20},{20,12},{12,4},{4,0},{1,9},{9... | collective-permute-start | bytes 1179656 | tf_op jit(solution)/shard_map/ppermute | solution.py:598
  71.1 14.5 %collective-permute-start.17 = (bf16[2,192,512]{2,1,0:T(8,128)(2,1)S(1)}, bf16[2,192,512]{2,1,0:T(8,128)(2,1)S(1)}, u32[]{:S(2)}, u32[]{:S(2)}) collective-permute-start(bf16[2,192,512]{2,1,0:T(8,128)(2,1)S(1)} %collective-permute-done.15.refs_4_.refs_8_), channel_id=1, source_target_pairs={{8,0},{16,8},{24,16},{28,24},{20,28},{12,20},{4,12},{0,4},{9,1},{1... | collective-permute-start | bytes 1179656 | tf_op jit(solution)/shard_map/ppermute | solution.py:601
  73.0 25.1 %collective-permute-start.22 = (bf16[192,768]{1,0:T(8,128)(2,1)S(1)}, bf16[192,768]{1,0:T(8,128)(2,1)S(1)}, u32[]{:S(2)}, u32[]{:S(2)}) collective-permute-start(bf16[192,768]{1,0:T(8,128)(2,1)S(1)} %collective-permute-done.20.o1), channel_id=1, source_target_pairs={{0,2},{1,3},{2,0},{3,1},{4,6},{5,7},{6,4},{7,5},{8,10},{9,11},{10,... | collective-permute-start | bytes 884744 | tf_op jit(solution)/shard_map/ppermute | solution.py:659
  74.4 23.7 %collective-permute-start.21 = (bf16[192,768]{1,0:T(8,128)(2,1)S(1)}, bf16[192,768]{1,0:T(8,128)(2,1)S(1)}, u32[]{:S(2)}, u32[]{:S(2)}) collective-permute-start(bf16[192,768]{1,0:T(8,128)(2,1)S(1)} %slice.56.o0.o_ref), channel_id=1, source_target_pairs={{0,2},{1,3},{2,0},{3,1},{4,6},{5,7},{6,4},{7,5},{8,10},{9,11},{10,... | collective-permute-start | bytes 884744 | tf_op jit(solution)/shard_map/ppermute | solution.py:659
  85.7 8.7 %collective-permute-start.19 = (bf16[1,192,512]{2,1,0:T(8,128)(2,1)S(1)}, bf16[1,192,512]{2,1,0:T(8,128)(2,1)S(1)}, u32[]{:S(2)}, u32[]{:S(2)}) collective-permute-start(bf16[1,192,512]{2,1,0:T(8,128)(2,1)S(1)} %slice.55), channel_id=1, source_target_pairs={{8,0},{16,8},{24,16},{28,24},{20,28},{12,20},{4,12},{0,4},{9,1},{1... | collective-permute-start | bytes 589832 | tf_op jit(solution)/shard_map/ppermute | solution.py:601
  86.3 8.6 %collective-permute-start.18 = (bf16[1,192,512]{2,1,0:T(8,128)(2,1)S(1)}, bf16[1,192,512]{2,1,0:T(8,128)(2,1)S(1)}, u32[]{:S(2)}, u32[]{:S(2)}) collective-permute-start(bf16[1,192,512]{2,1,0:T(8,128)(2,1)S(1)} %slice.54), channel_id=1, source_target_pairs={{0,8},{8,16},{16,24},{24,28},{28,20},{20,12},{12,4},{4,0},{1,9},{9... | collective-permute-start | bytes 589832 | tf_op jit(solution)/shard_map/ppermute | solution.py:598
  114.7 11.6 %collective-permute-start.24 = (bf16[256,768]{1,0:T(8,128)(2,1)S(1)}, bf16[256,768]{1,0:T(8,128)(2,1)S(1)}, u32[]{:S(2)}, u32[]{:S(2)}) collective-permute-start(bf16[256,768]{1,0:T(8,128)(2,1)S(1)} %add_convert_fusion.2.a_ref), channel_id=1, source_target_pairs={{0,2},{1,3},{2,0},{3,1},{4,6},{5,7},{6,4},{7,5},{8,10},{9,11},{10,... | collective-permute-start | bytes 1179656 | tf_op jit(solution)/shard_map/ppermute | solution.py:659
  139.6 11.2 %collective-permute-start.27 = (bf16[256,768]{1,0:T(8,128)(2,1)S(1)}, bf16[256,768]{1,0:T(8,128)(2,1)S(1)}, u32[]{:S(2)}, u32[]{:S(2)}) collective-permute-start(bf16[256,768]{1,0:T(8,128)(2,1)S(1)} %add_convert_fusion.1.a_ref), channel_id=1, source_target_pairs={{0,2},{1,3},{2,0},{3,1},{4,6},{5,7},{6,4},{7,5},{8,10},{9,11},{10,... | collective-permute-start | bytes 1179656 | tf_op jit(solution)/shard_map/ppermute | solution.py:659
  160.1 13.2 %collective-permute-start.32 = (bf16[1,192,512]{2,1,0:T(8,128)(2,1)S(1)}, bf16[1,192,512]{2,1,0:T(8,128)(2,1)S(1)}, u32[]{:S(2)}, u32[]{:S(2)}) collective-permute-start(bf16[1,192,512]{2,1,0:T(8,128)(2,1)S(1)} %get-tuple-element.205), channel_id=1, source_target_pairs={{0,8},{8,16},{16,24},{24,28},{28,20},{20,12},{12,4},{4,0},{1,9},{9... | collective-permute-start | bytes 589832 | tf_op jit(solution)/shard_map/ppermute | solution.py:598
  164.4 18.4 %collective-permute-start.33 = (bf16[1,192,512]{2,1,0:T(8,128)(2,1)S(1)}, bf16[1,192,512]{2,1,0:T(8,128)(2,1)S(1)}, u32[]{:S(2)}, u32[]{:S(2)}) collective-permute-start(bf16[1,192,512]{2,1,0:T(8,128)(2,1)S(1)} %get-tuple-element.206), channel_id=1, source_target_pairs={{8,0},{16,8},{24,16},{28,24},{20,28},{12,20},{4,12},{0,4},{9,1},{1... | collective-permute-start | bytes 589832 | tf_op jit(solution)/shard_map/ppermute | solution.py:601
  164.4 8.0 %collective-permute-start.29 = (f32[8,768]{1,0:T(8,128)S(1)}, f32[8,768]{1,0:T(8,128)S(1)}, u32[]{:S(2)}, u32[]{:S(2)}) collective-permute-start(f32[8,768]{1,0:T(8,128)S(1)} %get-tuple-element.195), channel_id=1, source_target_pairs={{0,4},{4,0},{8,12},{12,8},{16,20},{20,16},{24,28},{28,24},{1,5},{5... | collective-permute-start | bytes 73736 | tf_op jit(solution)/shard_map/ppermute | solution.py:856
  183.4 14.5 %collective-permute-start.34 = (bf16[2,192,512]{2,1,0:T(8,128)(2,1)S(1)}, bf16[2,192,512]{2,1,0:T(8,128)(2,1)S(1)}, u32[]{:S(2)}, u32[]{:S(2)}) collective-permute-start(bf16[2,192,512]{2,1,0:T(8,128)(2,1)S(1)} %get-tuple-element.207), channel_id=1, source_target_pairs={{0,8},{8,16},{16,24},{24,28},{28,20},{20,12},{12,4},{4,0},{1,9},{9... | collective-permute-start | bytes 1179656 | tf_op jit(solution)/shard_map/ppermute | solution.py:598
  184.3 13.7 %collective-permute-start.35 = (bf16[2,192,512]{2,1,0:T(8,128)(2,1)S(1)}, bf16[2,192,512]{2,1,0:T(8,128)(2,1)S(1)}, u32[]{:S(2)}, u32[]{:S(2)}) collective-permute-start(bf16[2,192,512]{2,1,0:T(8,128)(2,1)S(1)} %get-tuple-element.208), channel_id=1, source_target_pairs={{8,0},{16,8},{24,16},{28,24},{20,28},{12,20},{4,12},{0,4},{9,1},{1... | collective-permute-start | bytes 1179656 | tf_op jit(solution)/shard_map/ppermute | solution.py:601
  185.7 10.3 %collective-permute-start.30 = (f32[8,768]{1,0:T(8,128)S(1)}, f32[8,768]{1,0:T(8,128)S(1)}, u32[]{:S(2)}, u32[]{:S(2)}) collective-permute-start(f32[8,768]{1,0:T(8,128)S(1)} %add.104), channel_id=1, source_target_pairs={{0,8},{4,12},{8,0},{12,4},{16,24},{20,28},{24,16},{28,20},{1,9},{5... | collective-permute-start | bytes 73736 | tf_op jit(solution)/shard_map/ppermute | solution.py:856
  198.7 19.8 %collective-permute-start.36 = (bf16[2,192,512]{2,1,0:T(8,128)(2,1)S(1)}, bf16[2,192,512]{2,1,0:T(8,128)(2,1)S(1)}, u32[]{:S(2)}, u32[]{:S(2)}) collective-permute-start(bf16[2,192,512]{2,1,0:T(8,128)(2,1)S(1)} %get-tuple-element.209), channel_id=1, source_target_pairs={{0,8},{8,16},{16,24},{24,28},{28,20},{20,12},{12,4},{4,0},{1,9},{9... | collective-permute-start | bytes 1179656 | tf_op jit(solution)/shard_map/ppermute | solution.py:598
  198.8 19.7 %collective-permute-start.37 = (bf16[2,192,512]{2,1,0:T(8,128)(2,1)S(1)}, bf16[2,192,512]{2,1,0:T(8,128)(2,1)S(1)}, u32[]{:S(2)}, u32[]{:S(2)}) collective-permute-start(bf16[2,192,512]{2,1,0:T(8,128)(2,1)S(1)} %get-tuple-element.210), channel_id=1, source_target_pairs={{8,0},{16,8},{24,16},{28,24},{20,28},{12,20},{4,12},{0,4},{9,1},{1... | collective-permute-start | bytes 1179656 | tf_op jit(solution)/shard_map/ppermute | solution.py:601
  200.8 17.7 %collective-permute-start.31 = (f32[8,768]{1,0:T(8,128)S(1)}, f32[8,768]{1,0:T(8,128)S(1)}, u32[]{:S(2)}, u32[]{:S(2)}) collective-permute-start(f32[8,768]{1,0:T(8,128)S(1)} %add.105), channel_id=1, source_target_pairs={{0,16},{4,20},{8,24},{12,28},{16,0},{20,4},{24,8},{28,12},{1,17},{... | collective-permute-start | bytes 73736 | tf_op jit(solution)/shard_map/ppermute | solution.py:856
  219.2 8.3 %collective-permute-start.38 = (bf16[2,192,512]{2,1,0:T(8,128)(2,1)S(1)}, bf16[2,192,512]{2,1,0:T(8,128)(2,1)S(1)}, u32[]{:S(2)}, u32[]{:S(2)}) collective-permute-start(bf16[2,192,512]{2,1,0:T(8,128)(2,1)S(1)} %get-tuple-element.211), channel_id=1, source_target_pairs={{0,8},{8,16},{16,24},{24,28},{28,20},{20,12},{12,4},{4,0},{1,9},{9... | collective-permute-start | bytes 1179656 | tf_op jit(solution)/shard_map/ppermute | solution.py:598
  219.6 8.7 %collective-permute-start.39 = (bf16[2,192,512]{2,1,0:T(8,128)(2,1)S(1)}, bf16[2,192,512]{2,1,0:T(8,128)(2,1)S(1)}, u32[]{:S(2)}, u32[]{:S(2)}) collective-permute-start(bf16[2,192,512]{2,1,0:T(8,128)(2,1)S(1)} %get-tuple-element.212), channel_id=1, source_target_pairs={{8,0},{16,8},{24,16},{28,24},{20,28},{12,20},{4,12},{0,4},{9,1},{1... | collective-permute-start | bytes 1179656 | tf_op jit(solution)/shard_map/ppermute | solution.py:601
  241.2 7.1 %collective-permute-start.43 = (bf16[128,768]{1,0:T(8,128)(2,1)S(1)}, bf16[128,768]{1,0:T(8,128)(2,1)S(1)}, u32[]{:S(2)}, u32[]{:S(2)}) collective-permute-start(bf16[128,768]{1,0:T(8,128)(2,1)S(1)} %dynamic-slice_bitcast_fusion), channel_id=1, source_target_pairs={{0,2},{1,3},{2,0},{3,1},{4,6},{5,7},{6,4},{7,5},{8,10},{9,11},{10,... | collective-permute-start | bytes 589832 | tf_op jit(solution)/shard_map/ppermute | solution.py:659
  (59 other events, 535.7 us)
Sparse Core Ops, SparseCore 0:
  10.2 48.9 all-gather.4
  61.4 44.2 all-gather.2
  137.8 86.1 reduce-scatter.1

commit v2 on v1

--- a/solution.py
+++ b/solution.py
@@ -530,8 +530,11 @@
         down_out[...] = add(behind_ref[...], down_ref[...])
 
 
-def close_kernel(s_ref, part_ref, up_ref, down_ref, gq_ref, rows_ref, attn_ref, *refs):
-    outs, project_ref, total_s = refs[:-2], refs[-2], refs[-1]
+def close_kernel(s_ref, part_ref, up_ref, down_ref, gq_ref, rows_ref, attn_ref, turned_ref, *refs):
+    outs, (mine_ref, other_ref, project_ref, total_s, part_s) = refs[:-5], refs[-5:]
+    near = s_ref[0] % 2
+    rows, cols = part_s.shape[0], project_ref.shape[0]
+    own = rows // 4
     width = gq_ref.shape[0]
     project_ref[:width] = gq_ref[...]
     for w in range(2):
@@ -541,20 +544,13 @@
     count = len(outs) - 1
     if count == 0:
         outs[0][...] = total_s[...].astype(BF)
-        return
-    half = outs[0].shape[0]
-    for i in range(2):
-        at = pl.multiple_of(s_ref[count] * 2 * half + i * half, half)
-        outs[i][...] = total_s[pl.ds(at, half), :].astype(BF)
-    for i in range(1, count):
-        outs[1 + i][...] = total_s[rows_at(s_ref[count - i], 2 * half), :].astype(BF)
-
-
-def input_kernel(s_ref, project_ref, turned_ref, mine_ref, other_ref, part_s):
-    near = s_ref[0] % 2
-    rows = part_s.shape[0]
-    own = rows // 4
-    cols = project_ref.shape[0]
+    else:
+        half = outs[0].shape[0]
+        for i in range(2):
+            at = pl.multiple_of(s_ref[count] * 2 * half + i * half, half)
+            outs[i][...] = total_s[pl.ds(at, half), :].astype(BF)
+        for i in range(1, count):
+            outs[1 + i][...] = total_s[rows_at(s_ref[count - i], 2 * half), :].astype(BF)
     part_s[...] = contract(project_ref[...].astype(F32).T.astype(BF), turned_ref[:cols], 1, 0)
     for f in range(2):
         here = slice(f * own, (f + 1) * own)
@@ -893,9 +889,9 @@
         shapes = [((share // 2, 4 * width), BF)] * 2 + [((share, 4 * width), BF)] * (nd - 1)
     else:
         shapes = [((model, 4 * width), BF)]
-    *parts, grad_project = fused(
+    *parts, mine, other = fused(
         close_kernel,
-        shapes + [((3 * width, rows), BF)],
+        shapes + [(pair, BF), (pair, BF)],
         place,
         part,
         total_kv.up,
@@ -903,30 +899,20 @@
         grad_query,
         rows_all,
         apart(grad_w_attn),
-        scratch=[((model, 4 * width), F32)],
+        apart(turned),
+        scratch=[((3 * width, rows), BF), ((model, 4 * width), F32), ((rows, model), F32)],
     )
     if by_ring:
         last_sum = RingSum(all_ring)
         last_sum.first(parts[0], parts[1])
-        grad_project = after(grad_project, last_sum.up, last_sum.down)
-    mine, other = fused(
-        input_kernel,
-        [(pair, BF), (pair, BF)],
-        place,
-        grad_project,
-        apart(turned),
-        scratch=[((rows, model), F32)],
-    )
     mine = add(mine, quad.send_near(other)).reshape(2, own, model)
     far = quad.send_far(lax.dynamic_index_in_dim(mine, 1 - quad.far, 0, keepdims=False))
     kept = lax.dynamic_index_in_dim(mine, quad.far, 0, keepdims=False)
     grad_inputs = grad_first + (kept.astype(F32) + far.astype(F32))
     if by_ring:
-        parts[3] = after(parts[3], grad_w_out, grad_w_in)
         for i in range(2, nd, 2):
-            if i == 4:
-                parts = lax.optimization_barrier((*parts, far))[:-1]
-            last_sum.step(place, apart(parts[i + 1]), apart(parts[i]))
+            scalars = after(place, *((far,) if i == 4 else (grad_w_out, grad_w_in) if i == 6 else ()))
+            last_sum.step(scalars, parts[i + 1], parts[i])
         grads = parts[-1].astype(F32) + (last_sum.up.astype(F32) + last_sum.down.astype(F32))
     else:
         grads = group_sum(parts[0], "dp", nd)

time: 275 us -> 268 us (0.975)
  starting transfers between devices: 55.8 us -> 53 us
    ppermute x8, waiting for transfers between devices: 21.9 us -> 24.6 us  [send_far(): return lax.ppermute(x, self.axis, self.flip_far)]
    pallas_call x15 -> x14, Pallas kernels: 31.6 us -> 28.9 us  [fused(): pl.pallas_call(body, out_shape=shapes, in_specs=[pl.BlockSpec(memory_spac...]
    unnamed x78 -> x64, local copies, waits for them, and re-layouts: 5.61 us -> 4.07 us
  transfers between devices with their start and end apart: 53 -> 53, of which waited for: 33 -> 31; matrix products, arithmetic and copies ran while one was open for 5% -> 5% of each run, Pallas kernels for 25% -> 25%
where the time goes in v2:
time: 268 us; the launch traced here: 267 us
  waiting for transfers between devices  90.6 us (34%)
  Pallas kernels  82.6 us (31%)
  starting transfers between devices  53 us (20%)
  between operations  14.4 us (5%)
  local copies, waits for them, and re-layouts  10.7 us (4%)
  other arithmetic  8.09 us (3%)
  blocking collectives  7.41 us (3%)
    pallas_call x14, Pallas kernels, fused(): pl.pallas_call(body, out_shape=shapes, in_specs=[pl.BlockSpec(memory_spac...  28.9 us
    pallas_call x5, Pallas kernels, attend_backward(): pl.pallas_call(functools.partial(backward_kernel, first, last, pieces, pa...  28.5 us
    ppermute x16, waiting for transfers between devices, send_down(): return lax.ppermute(x, self.axis, self.down)  28.3 us
    pallas_call x5, Pallas kernels, attend_forward(): pl.pallas_call(functools.partial(forward_kernel, first, last, pieces, par...  25.2 us
    ppermute x8, waiting for transfers between devices, send_far(): return lax.ppermute(x, self.axis, self.flip_far)  24.6 us
    ppermute x16, starting transfers between devices, send_down(): return lax.ppermute(x, self.axis, self.down)  21.3 us
    ppermute x16, starting transfers between devices, send_up(): return lax.ppermute(x, self.axis, self.up)  17.2 us
    ppermute x16, waiting for transfers between devices, send_up(): return lax.ppermute(x, self.axis, self.up)  15.4 us
  transfers between devices with their start and end apart: 53, of which 31 were waited for; matrix products, arithmetic and copies ran while one was open for 5% of the time, Pallas kernels for 25%

profile of v2, /device:TPU:0, one launch (start us, length us, event | category | flops | bytes accessed | tf_op | source)
XLA Modules:
  0.0 266.8 jit_solution(924227300702196255)
XLA Ops:
  9.8 3.0 %collective-permute-start.1 = (bf16[96,768]{1,0:T(8,128)(2,1)S(1)}, bf16[96,768]{1,0:T(8,128)(2,1)S(1)}, u32[]{:S(2)}, u32[]{:S(2)}) collective-permute-start(bf16[96,768]{1,0:T(8,128)(2,1)S(1)} %pad_maximum_fusion.1.refs_0_), channel_id=1, source_target_pairs={{8,0},{16,8},{24,16},{28,24},{20,28},{12,20},{4,12},{0,4},{9,1},{1... | collective-permute-start | bytes 442376 | tf_op jit(solution)/shard_map/ppermute | solution.py:597
  24.1 2.5 collective-permute-start.5
  33.4 2.6 collective-permute-done.10.refs_12_
  38.0 2.6 shard_map.298
  44.0 5.4 %shard_map.299 = (bf16[3,512,4096]{2,1,0:T(8,128)(2,1)}, f32[3,512,128]{2,1,0:T(8,128)S(1)}) custom-call(s32[8]{0:T(128)S(1)} %get-tuple-element.123.refs_0_, s32[128]{0:T(128)S(1)} %reshape.59.refs_1_, bf16[3,512,64]{2,1,0:T(8,128)(2,1)S(1)} %get-tuple-element.126.refs_2_.refs_4_, bf16[2,192,512]{2,1,0:T(8,128)(2,1)S(1)} %get-tuple-element.127.refs_3_.refs_7_, ...), custom_call_target="tpu_custom_call" | custom-call | flops 201326592 | bytes 3145728 | tf_op jit(solution)/shard_map/pallas_call | solution.py:175
  49.4 7.6 %collective-permute-done.12.refs_4_.refs_8_ = bf16[2,192,512]{2,1,0:T(8,128)(2,1)S(1)} collective-permute-done((bf16[2,192,512]{2,1,0:T(8,128)(2,1)S(1)}, bf16[2,192,512]{2,1,0:T(8,128)(2,1)S(1)}, u32[]{:S(2)}, u32[]{:S(2)}) %collective-permute-start.12) | collective-permute-done | bytes 393248 | tf_op jit(solution)/shard_map/ppermute | solution.py:597
  60.6 8.5 %shard_map.300 = (bf16[3,512,4096]{2,1,0:T(8,128)(2,1)}, f32[3,512,128]{2,1,0:T(8,128)S(1)}) custom-call(s32[8]{0:T(128)S(1)} %get-tuple-element.123.refs_0_, s32[128]{0:T(128)S(1)} %reshape.59.refs_1_, bf16[3,512,64]{2,1,0:T(8,128)(2,1)S(1)} %get-tuple-element.126.refs_2_.refs_4_, ...), custom_call_target="tpu_custom_call", output_to_operand_aliasing={{0}: (6, {})} | custom-call | flops 402653184 | bytes 6291456 | tf_op jit(solution)/shard_map/pallas_call | solution.py:175
  75.0 6.0 %shard_map.301 = (bf16[3,512,4096]{2,1,0:T(8,128)(2,1)}, f32[3,512,128]{2,1,0:T(8,128)S(1)}) custom-call(s32[8]{0:T(128)S(1)} %get-tuple-element.123.refs_0_, s32[128]{0:T(128)S(1)} %reshape.59.refs_1_, bf16[3,512,64]{2,1,0:T(8,128)(2,1)S(1)} %get-tuple-element.126.refs_2_.refs_4_, ...), custom_call_target="tpu_custom_call", output_to_operand_aliasing={{0}: (6, {})} | custom-call | flops 402653184 | bytes 6291456 | tf_op jit(solution)/shard_map/pallas_call | solution.py:175
  81.1 2.4 collective-permute-done.16.refs_3_.refs_7_
  87.8 3.0 %shard_map.302 = (bf16[3,512,4096]{2,1,0:T(8,128)(2,1)}, f32[3,512,128]{2,1,0:T(8,128)S(1)}) custom-call(s32[8]{0:T(128)S(1)} %get-tuple-element.123.refs_0_, s32[128]{0:T(128)S(1)} %reshape.59.refs_1_, bf16[3,512,64]{2,1,0:T(8,128)(2,1)S(1)} %get-tuple-element.126.refs_2_.refs_4_, ...), custom_call_target="tpu_custom_call", output_to_operand_aliasing={{0}: (6, {})} | custom-call | flops 402653184 | bytes 6291456 | tf_op jit(solution)/shard_map/pallas_call | solution.py:175
  92.5 2.5 collective-permute-done.18.refs_3_.refs_7_
  98.2 7.4 %all_gather.9.mixed_ref = bf16[768,512]{1,0:T(8,128)(2,1)S(1)} all-gather(bf16[192,512]{1,0:T(8,128)(2,1)S(1)} %get-tuple-element.145.mixed_ref), channel_id=1, replica_groups=mesh['dp'=8,'tensor'=4] {'tensor'}, dimensions={0}, use_global_device_ids=true | all-gather | bytes 983040 | tf_op jit(solution)/shard_map/all_gather | solution.py:763
  106.1 5.8 %shard_map.304 = (bf16[512,768]{1,0:T(8,128)(2,1)S(1)}, bf16[512,768]{1,0:T(8,128)(2,1)S(1)}, f32[512,768]{1,0:T(8,128)S(1)}, f32[256,768]{1,0:T(8,128)S(1)}, f3...) custom-call(s32[9]{0:T(128)S(1)} %pad_add_fusion.s_ref, ...), custom_call_target="tpu_custom_call" | custom-call | bytes 1048576 | tf_op jit(solution)/shard_map/pallas_call | solution.py:339
  115.2 9.7 %collective-permute-done.24.b_ref = bf16[256,768]{1,0:T(8,128)(2,1)S(1)} collective-permute-done((bf16[256,768]{1,0:T(8,128)(2,1)S(1)}, bf16[256,768]{1,0:T(8,128)(2,1)S(1)}, u32[]{:S(2)}, u32[]{:S(2)}) %collective-permute-start.24) | collective-permute-done | bytes 393248 | tf_op jit(solution)/shard_map/ppermute | solution.py:655
  125.0 2.7 %shard_map.305 = (bf16[128,768]{1,0:T(8,128)(2,1)}, f32[256,768]{1,0:T(8,128)S(1)}, bf16[256,768]{1,0:T(8,128)(2,1)S(1)}, f32[2,768]{1,0:T(2,128)S(1)}) custom-call(s32[9]{0:T(128)S(1)} %pad_add_fusion.s_ref, bf16[256,768]{1,0:T(8,128)(2,1)S(1)} %add_convert_fusion.2.a_ref, bf16[256,768]{1,0:T(8,128)(2,1)S(1)} %collective-permute-done.24.b_ref, ...), custom_call_target="tpu_custom_call" | custom-call | bytes 1048576 | tf_op jit(solution)/shard_map/pallas_call | solution.py:339
  129.4 3.5 %shard_map.306 = (bf16[512,768]{1,0:T(8,128)(2,1)S(1)}, bf16[512,768]{1,0:T(8,128)(2,1)S(1)}, f32[1,768]{1,0:T(1,128)S(1)}, bf16[256,768]{1,0:T(8,128)(2,1)S(1)}, bf16[256,768]{1,0:T(8,128)(2,1)S(1)}) custom-call(s32[9]{0:T(128)S(1)} %pad_add_fusion.s_ref, bf16[256,768]{1,0:T(8,128)(2,1)S(1)} %get-tuple-element.161.low_ref, ...), custom_call_target="tpu_custom_call" | custom-call | bytes 1048576 | tf_op jit(solution)/shard_map/pallas_call | solution.py:339
  132.9 3.4 %shard_map.307 = bf16[768,1536]{1,0:T(8,128)(2,1)} custom-call(s32[9]{0:T(128)S(1)} %pad_add_fusion.s_ref, bf16[512,768]{1,0:T(8,128)(2,1)S(1)} %get-tuple-element.165.active_ref, bf16[512,768]{1,0:T(8,128)(2,1)S(1)} %get-tuple-element.166.second_ref, bf16[512,768]{1,0:T(8,128)(2,1)S(1)} %get-tuple-element.167.low_ref, ...), custom_call_target="tpu_custom_call" | custom-call | bytes 1048576 | tf_op jit(solution)/shard_map/pallas_call | solution.py:339
  139.9 9.6 %collective-permute-done.27.b_ref = bf16[256,768]{1,0:T(8,128)(2,1)S(1)} collective-permute-done((bf16[256,768]{1,0:T(8,128)(2,1)S(1)}, bf16[256,768]{1,0:T(8,128)(2,1)S(1)}, u32[]{:S(2)}, u32[]{:S(2)}) %collective-permute-start.27) | collective-permute-done | bytes 393248 | tf_op jit(solution)/shard_map/ppermute | solution.py:655
  156.2 2.6 shard_map.310
  158.8 3.3 %collective-permute-start.32 = (bf16[1,192,512]{2,1,0:T(8,128)(2,1)S(1)}, bf16[1,192,512]{2,1,0:T(8,128)(2,1)S(1)}, u32[]{:S(2)}, u32[]{:S(2)}) collective-permute-start(bf16[1,192,512]{2,1,0:T(8,128)(2,1)S(1)} %get-tuple-element.199), channel_id=1, source_target_pairs={{0,8},{8,16},{16,24},{24,28},{28,20},{20,12},{12,4},{4,0},{1,9},{9... | collective-permute-start | bytes 589832 | tf_op jit(solution)/shard_map/ppermute | solution.py:594
  162.9 3.4 %shard_map.311 = (bf16[3,512,4096]{2,1,0:T(8,128)(2,1)}, bf16[2,192,512]{2,1,0:T(8,128)(2,1)S(1)}, bf16[2,192,512]{2,1,0:T(8,128)(2,1)S(1)}, f32[3,512,64]{2,1,0:T(8,128)S(1)}) custom-call(s32[8]{0:T(128)S(1)} %get-tuple-element.123.refs_0_, s32[128]{0:T(128)S(1)} %reshape.59.refs_1_, ...), custom_call_target="tpu_custom_call", output_to_operand_aliasing={{0}: (11, {})} | custom-call | flops 1006632960 | bytes 9437184 | tf_op jit(solution)/shard_map/pallas_call | solution.py:311
  166.3 3.7 %collective-permute-done.29 = f32[8,768]{1,0:T(8,128)S(1)} collective-permute-done((f32[8,768]{1,0:T(8,128)S(1)}, f32[8,768]{1,0:T(8,128)S(1)}, u32[]{:S(2)}, u32[]{:S(2)}) %collective-permute-start.29) | collective-permute-done | bytes 24608 | tf_op jit(solution)/shard_map/ppermute | solution.py:852
  170.8 10.4 %collective-permute-done.33.down_ref = bf16[1,192,512]{2,1,0:T(8,128)(2,1)S(1)} collective-permute-done((bf16[1,192,512]{2,1,0:T(8,128)(2,1)S(1)}, bf16[1,192,512]{2,1,0:T(8,128)(2,1)S(1)}, u32[]{:S(2)}, u32[]{:S(2)}) %collective-permute-start.33) | collective-permute-done | bytes 196640 | tf_op jit(solution)/shard_map/ppermute | solution.py:597
  184.7 6.9 %shard_map.312 = (bf16[3,512,4096]{2,1,0:T(8,128)(2,1)}, bf16[2,192,512]{2,1,0:T(8,128)(2,1)S(1)}, bf16[2,192,512]{2,1,0:T(8,128)(2,1)S(1)}, f32[3,512,64]{2,1,0:T(8,128)S(1)}) custom-call(s32[8]{0:T(128)S(1)} %get-tuple-element.123.refs_0_, s32[128]{0:T(128)S(1)} %reshape.59.refs_1_, ...), custom_call_target="tpu_custom_call", output_to_operand_aliasing={{0}: (11, {})} | custom-call | flops 1006632960 | bytes 9437184 | tf_op jit(solution)/shard_map/pallas_call | solution.py:311
  191.6 2.5 collective-permute-done.30
  199.2 2.4 collective-permute-start.31
  201.6 9.4 %shard_map.313 = (bf16[3,512,4096]{2,1,0:T(8,128)(2,1)}, bf16[2,192,512]{2,1,0:T(8,128)(2,1)S(1)}, bf16[2,192,512]{2,1,0:T(8,128)(2,1)S(1)}, f32[3,512,64]{2,1,0:T(8,128)S(1)}) custom-call(s32[8]{0:T(128)S(1)} %get-tuple-element.123.refs_0_, s32[128]{0:T(128)S(1)} %reshape.59.refs_1_, ...), custom_call_target="tpu_custom_call", output_to_operand_aliasing={{0}: (11, {})} | custom-call | flops 1006632960 | bytes 9437184 | tf_op jit(solution)/shard_map/pallas_call | solution.py:311
  211.0 6.6 %collective-permute-done.31 = f32[8,768]{1,0:T(8,128)S(1)} collective-permute-done((f32[8,768]{1,0:T(8,128)S(1)}, f32[8,768]{1,0:T(8,128)S(1)}, u32[]{:S(2)}, u32[]{:S(2)}) %collective-permute-start.31) | collective-permute-done | bytes 24608 | tf_op jit(solution)/shard_map/ppermute | solution.py:852
  220.5 6.2 %shard_map.314 = (bf16[3,512,4096]{2,1,0:T(8,128)(2,1)}, bf16[2,192,512]{2,1,0:T(8,128)(2,1)S(1)}, bf16[192,512]{1,0:T(8,128)(2,1)S(1)}) custom-call(s32[8]{0:T(128)S(1)} %get-tuple-element.123.refs_0_, s32[128]{0:T(128)S(1)} %reshape.59.refs_1_, bf16[192,512]{1,0:T(8,128)(2,1)S(1)} %get-tuple-element.129.refs_2_, ...), custom_call_target="tpu_custom_call", output_to_operand_aliasing={{0}: (10, {})} | custom-call | flops 503316480 | bytes 4718592 | tf_op jit(solution)/shard_map/pallas_call | solution.py:311
  227.2 3.0 %shard_map.318 = (bf16[48,768]{1,0:T(8,128)(2,1)S(1)}, bf16[48,768]{1,0:T(8,128)(2,1)S(1)}, bf16[96,768]{1,0:T(8,128)(2,1)S(1)}, bf16[96,768]{1,0:T(8,128)(2,1)S...) custom-call(s32[9]{0:T(128)S(1)} %pad_add_fusion.s_ref, ...), custom_call_target="tpu_custom_call" | custom-call | bytes 1048576 | tf_op jit(solution)/shard_map/pallas_call | solution.py:339
  232.4 2.6 collective-permute-done.42.up_ref
  242.5 2.7 %collective-permute-done.41 = bf16[128,768]{1,0:T(8,128)(2,1)S(1)} collective-permute-done((bf16[128,768]{1,0:T(8,128)(2,1)S(1)}, bf16[128,768]{1,0:T(8,128)(2,1)S(1)}, u32[]{:S(2)}, u32[]{:S(2)}) %collective-permute-start.41) | collective-permute-done | bytes 196640 | tf_op jit(solution)/shard_map/ppermute | solution.py:655
  (200 shorter events, 98.6 us)
Async XLA Ops:
  7.2 98.4 %all-gather.5.cloned.1.call-start = ((), (), s32[]{:S(2)}) async-start(), calls=%async_computation.2 | async-start | bytes 1327104 | tf_op jit(solution)/shard_map/all_gather | solution.py:709
  7.9 98.2 %all-gather.3.cloned.1.call-start = ((), (), s32[]{:S(2)}) async-start(), calls=%async_computation.1 | async-start | bytes 1548288 | tf_op jit(solution)/shard_map/all_gather | solution.py:720
  9.8 7.6 %collective-permute-start.1 = (bf16[96,768]{1,0:T(8,128)(2,1)S(1)}, bf16[96,768]{1,0:T(8,128)(2,1)S(1)}, u32[]{:S(2)}, u32[]{:S(2)}) collective-permute-start(bf16[96,768]{1,0:T(8,128)(2,1)S(1)} %pad_maximum_fusion.1.refs_0_), channel_id=1, source_target_pairs={{8,0},{16,8},{24,16},{28,24},{20,28},{12,20},{4,12},{0,4},{9,1},{1... | collective-permute-start | bytes 442376 | tf_op jit(solution)/shard_map/ppermute | solution.py:597
  13.0 17.4 %collective-permute-start.8 = (bf16[128,768]{1,0:T(8,128)(2,1)}, bf16[128,768]{1,0:T(8,128)(2,1)S(1)}, u32[]{:S(2)}, u32[]{:S(2)}) collective-permute-start(bf16[128,768]{1,0:T(8,128)(2,1)} %refs_9_.1), channel_id=1, source_target_pairs={{0,1},{1,0},{2,3},{3,2},{4,5},{5,4},{6,7},{7,6},{8,9},{9,8},{10,11... | collective-permute-start | bytes 589832 | tf_op jit(solution)/shard_map/ppermute | solution.py:652
  13.0 20.5 %collective-permute-start.9 = (bf16[128,768]{1,0:T(8,128)(2,1)}, bf16[128,768]{1,0:T(8,128)(2,1)S(1)}, u32[]{:S(2)}, u32[]{:S(2)}) collective-permute-start(bf16[128,768]{1,0:T(8,128)(2,1)} %refs_9_.1), channel_id=1, source_target_pairs={{0,2},{1,3},{2,0},{3,1},{4,6},{5,7},{6,4},{7,5},{8,10},{9,11},{10,... | collective-permute-start | bytes 589832 | tf_op jit(solution)/shard_map/ppermute | solution.py:655
  19.0 7.6 %collective-permute-start.2 = (bf16[96,768]{1,0:T(8,128)(2,1)S(1)}, bf16[96,768]{1,0:T(8,128)(2,1)S(1)}, u32[]{:S(2)}, u32[]{:S(2)}) collective-permute-start(bf16[96,768]{1,0:T(8,128)(2,1)S(1)} %collective-permute-done.refs_1_), channel_id=1, source_target_pairs={{0,8},{8,16},{16,24},{24,28},{28,20},{20,12},{12,4},{4,0},{1,9},{9... | collective-permute-start | bytes 442376 | tf_op jit(solution)/shard_map/ppermute | solution.py:594
  22.0 225.9 %reduce-scatter.2.cloned.1.call-start = ((), (), s32[]{:S(2)}) async-start(), calls=%async_computation.3 | async-start | bytes 2654208 | tf_op jit(solution)/shard_map/reduce_scatter | solution.py:812
  40.7 16.4 %collective-permute-start.12 = (bf16[2,192,512]{2,1,0:T(8,128)(2,1)S(1)}, bf16[2,192,512]{2,1,0:T(8,128)(2,1)S(1)}, u32[]{:S(2)}, u32[]{:S(2)}) collective-permute-start(bf16[2,192,512]{2,1,0:T(8,128)(2,1)S(1)} %get-tuple-element.127.refs_3_.refs_7_), channel_id=1, source_target_pairs={{8,0},{16,8},{24,16},{28,24},{20,28},{12,20},{4,12},{0,4},{9,1},{1... | collective-permute-start | bytes 1179656 | tf_op jit(solution)/shard_map/ppermute | solution.py:597
  42.7 14.3 %collective-permute-start.11 = (bf16[2,192,512]{2,1,0:T(8,128)(2,1)S(1)}, bf16[2,192,512]{2,1,0:T(8,128)(2,1)S(1)}, u32[]{:S(2)}, u32[]{:S(2)}) collective-permute-start(bf16[2,192,512]{2,1,0:T(8,128)(2,1)S(1)} %get-tuple-element.127.refs_3_.refs_7_), channel_id=1, source_target_pairs={{0,8},{8,16},{16,24},{24,28},{28,20},{20,12},{12,4},{4,0},{1,9},{9... | collective-permute-start | bytes 1179656 | tf_op jit(solution)/shard_map/ppermute | solution.py:594
  57.0 12.1 %collective-permute-start.14 = (bf16[2,192,512]{2,1,0:T(8,128)(2,1)S(1)}, bf16[2,192,512]{2,1,0:T(8,128)(2,1)S(1)}, u32[]{:S(2)}, u32[]{:S(2)}) collective-permute-start(bf16[2,192,512]{2,1,0:T(8,128)(2,1)S(1)} %collective-permute-done.11.refs_3_.refs_7_), channel_id=1, source_target_pairs={{0,8},{8,16},{16,24},{24,28},{28,20},{20,12},{12,4},{4,0},{1,9},{9... | collective-permute-start | bytes 1179656 | tf_op jit(solution)/shard_map/ppermute | solution.py:594
  59.2 10.0 %collective-permute-start.15 = (bf16[2,192,512]{2,1,0:T(8,128)(2,1)S(1)}, bf16[2,192,512]{2,1,0:T(8,128)(2,1)S(1)}, u32[]{:S(2)}, u32[]{:S(2)}) collective-permute-start(bf16[2,192,512]{2,1,0:T(8,128)(2,1)S(1)} %collective-permute-done.12.refs_4_.refs_8_), channel_id=1, source_target_pairs={{8,0},{16,8},{24,16},{28,24},{20,28},{12,20},{4,12},{0,4},{9,1},{1... | collective-permute-start | bytes 1179656 | tf_op jit(solution)/shard_map/ppermute | solution.py:597
  69.2 14.3 %collective-permute-start.16 = (bf16[2,192,512]{2,1,0:T(8,128)(2,1)S(1)}, bf16[2,192,512]{2,1,0:T(8,128)(2,1)S(1)}, u32[]{:S(2)}, u32[]{:S(2)}) collective-permute-start(bf16[2,192,512]{2,1,0:T(8,128)(2,1)S(1)} %collective-permute-done.14.refs_3_.refs_7_), channel_id=1, source_target_pairs={{0,8},{8,16},{16,24},{24,28},{28,20},{20,12},{12,4},{4,0},{1,9},{9... | collective-permute-start | bytes 1179656 | tf_op jit(solution)/shard_map/ppermute | solution.py:594
  71.1 14.5 %collective-permute-start.17 = (bf16[2,192,512]{2,1,0:T(8,128)(2,1)S(1)}, bf16[2,192,512]{2,1,0:T(8,128)(2,1)S(1)}, u32[]{:S(2)}, u32[]{:S(2)}) collective-permute-start(bf16[2,192,512]{2,1,0:T(8,128)(2,1)S(1)} %collective-permute-done.15.refs_4_.refs_8_), channel_id=1, source_target_pairs={{8,0},{16,8},{24,16},{28,24},{20,28},{12,20},{4,12},{0,4},{9,1},{1... | collective-permute-start | bytes 1179656 | tf_op jit(solution)/shard_map/ppermute | solution.py:597
  73.0 25.2 %collective-permute-start.22 = (bf16[192,768]{1,0:T(8,128)(2,1)S(1)}, bf16[192,768]{1,0:T(8,128)(2,1)S(1)}, u32[]{:S(2)}, u32[]{:S(2)}) collective-permute-start(bf16[192,768]{1,0:T(8,128)(2,1)S(1)} %collective-permute-done.20.o1), channel_id=1, source_target_pairs={{0,2},{1,3},{2,0},{3,1},{4,6},{5,7},{6,4},{7,5},{8,10},{9,11},{10,... | collective-permute-start | bytes 884744 | tf_op jit(solution)/shard_map/ppermute | solution.py:655
  74.4 23.8 %collective-permute-start.21 = (bf16[192,768]{1,0:T(8,128)(2,1)S(1)}, bf16[192,768]{1,0:T(8,128)(2,1)}, u32[]{:S(2)}, u32[]{:S(2)}) collective-permute-start(bf16[192,768]{1,0:T(8,128)(2,1)S(1)} %slice.56.o0.o_ref), channel_id=1, source_target_pairs={{0,2},{1,3},{2,0},{3,1},{4,6},{5,7},{6,4},{7,5},{8,10},{9,11},{10,... | collective-permute-start | bytes 884744 | tf_op jit(solution)/shard_map/ppermute | solution.py:655
  85.7 6.8 %collective-permute-start.19 = (bf16[1,192,512]{2,1,0:T(8,128)(2,1)S(1)}, bf16[1,192,512]{2,1,0:T(8,128)(2,1)S(1)}, u32[]{:S(2)}, u32[]{:S(2)}) collective-permute-start(bf16[1,192,512]{2,1,0:T(8,128)(2,1)S(1)} %slice.55), channel_id=1, source_target_pairs={{8,0},{16,8},{24,16},{28,24},{20,28},{12,20},{4,12},{0,4},{9,1},{1... | collective-permute-start | bytes 589832 | tf_op jit(solution)/shard_map/ppermute | solution.py:597
  86.3 8.6 %collective-permute-start.18 = (bf16[1,192,512]{2,1,0:T(8,128)(2,1)S(1)}, bf16[1,192,512]{2,1,0:T(8,128)(2,1)S(1)}, u32[]{:S(2)}, u32[]{:S(2)}) collective-permute-start(bf16[1,192,512]{2,1,0:T(8,128)(2,1)S(1)} %slice.54), channel_id=1, source_target_pairs={{0,8},{8,16},{16,24},{24,28},{28,20},{20,12},{12,4},{4,0},{1,9},{9... | collective-permute-start | bytes 589832 | tf_op jit(solution)/shard_map/ppermute | solution.py:594
  113.8 11.2 %collective-permute-start.24 = (bf16[256,768]{1,0:T(8,128)(2,1)S(1)}, bf16[256,768]{1,0:T(8,128)(2,1)S(1)}, u32[]{:S(2)}, u32[]{:S(2)}) collective-permute-start(bf16[256,768]{1,0:T(8,128)(2,1)S(1)} %add_convert_fusion.2.a_ref), channel_id=1, source_target_pairs={{0,2},{1,3},{2,0},{3,1},{4,6},{5,7},{6,4},{7,5},{8,10},{9,11},{10,... | collective-permute-start | bytes 1179656 | tf_op jit(solution)/shard_map/ppermute | solution.py:655
  138.3 11.2 %collective-permute-start.27 = (bf16[256,768]{1,0:T(8,128)(2,1)S(1)}, bf16[256,768]{1,0:T(8,128)(2,1)S(1)}, u32[]{:S(2)}, u32[]{:S(2)}) collective-permute-start(bf16[256,768]{1,0:T(8,128)(2,1)S(1)} %add_convert_fusion.1.a_ref), channel_id=1, source_target_pairs={{0,2},{1,3},{2,0},{3,1},{4,6},{5,7},{6,4},{7,5},{8,10},{9,11},{10,... | collective-permute-start | bytes 1179656 | tf_op jit(solution)/shard_map/ppermute | solution.py:655
  158.8 12.1 %collective-permute-start.32 = (bf16[1,192,512]{2,1,0:T(8,128)(2,1)S(1)}, bf16[1,192,512]{2,1,0:T(8,128)(2,1)S(1)}, u32[]{:S(2)}, u32[]{:S(2)}) collective-permute-start(bf16[1,192,512]{2,1,0:T(8,128)(2,1)S(1)} %get-tuple-element.199), channel_id=1, source_target_pairs={{0,8},{8,16},{16,24},{24,28},{28,20},{20,12},{12,4},{4,0},{1,9},{9... | collective-permute-start | bytes 589832 | tf_op jit(solution)/shard_map/ppermute | solution.py:594
  162.1 19.2 %collective-permute-start.33 = (bf16[1,192,512]{2,1,0:T(8,128)(2,1)S(1)}, bf16[1,192,512]{2,1,0:T(8,128)(2,1)S(1)}, u32[]{:S(2)}, u32[]{:S(2)}) collective-permute-start(bf16[1,192,512]{2,1,0:T(8,128)(2,1)S(1)} %get-tuple-element.200), channel_id=1, source_target_pairs={{8,0},{16,8},{24,16},{28,24},{20,28},{12,20},{4,12},{0,4},{9,1},{1... | collective-permute-start | bytes 589832 | tf_op jit(solution)/shard_map/ppermute | solution.py:597
  162.1 7.9 %collective-permute-start.29 = (f32[8,768]{1,0:T(8,128)S(1)}, f32[8,768]{1,0:T(8,128)S(1)}, u32[]{:S(2)}, u32[]{:S(2)}) collective-permute-start(f32[8,768]{1,0:T(8,128)S(1)} %get-tuple-element.189), channel_id=1, source_target_pairs={{0,4},{4,0},{8,12},{12,8},{16,20},{20,16},{24,28},{28,24},{1,5},{5... | collective-permute-start | bytes 73736 | tf_op jit(solution)/shard_map/ppermute | solution.py:852
  181.9 14.5 %collective-permute-start.34 = (bf16[2,192,512]{2,1,0:T(8,128)(2,1)S(1)}, bf16[2,192,512]{2,1,0:T(8,128)(2,1)S(1)}, u32[]{:S(2)}, u32[]{:S(2)}) collective-permute-start(bf16[2,192,512]{2,1,0:T(8,128)(2,1)S(1)} %get-tuple-element.201), channel_id=1, source_target_pairs={{0,8},{8,16},{16,24},{24,28},{28,20},{20,12},{12,4},{4,0},{1,9},{9... | collective-permute-start | bytes 1179656 | tf_op jit(solution)/shard_map/ppermute | solution.py:594
  182.7 13.7 %collective-permute-start.35 = (bf16[2,192,512]{2,1,0:T(8,128)(2,1)S(1)}, bf16[2,192,512]{2,1,0:T(8,128)(2,1)S(1)}, u32[]{:S(2)}, u32[]{:S(2)}) collective-permute-start(bf16[2,192,512]{2,1,0:T(8,128)(2,1)S(1)} %get-tuple-element.202), channel_id=1, source_target_pairs={{8,0},{16,8},{24,16},{28,24},{20,28},{12,20},{4,12},{0,4},{9,1},{1... | collective-permute-start | bytes 1179656 | tf_op jit(solution)/shard_map/ppermute | solution.py:597
  184.2 10.0 %collective-permute-start.30 = (f32[8,768]{1,0:T(8,128)S(1)}, f32[8,768]{1,0:T(8,128)S(1)}, u32[]{:S(2)}, u32[]{:S(2)}) collective-permute-start(f32[8,768]{1,0:T(8,128)S(1)} %add.104), channel_id=1, source_target_pairs={{0,8},{4,12},{8,0},{12,4},{16,24},{20,28},{24,16},{28,20},{1,9},{5... | collective-permute-start | bytes 73736 | tf_op jit(solution)/shard_map/ppermute | solution.py:852
  197.1 20.5 %collective-permute-start.36 = (bf16[2,192,512]{2,1,0:T(8,128)(2,1)S(1)}, bf16[2,192,512]{2,1,0:T(8,128)(2,1)S(1)}, u32[]{:S(2)}, u32[]{:S(2)}) collective-permute-start(bf16[2,192,512]{2,1,0:T(8,128)(2,1)S(1)} %get-tuple-element.203), channel_id=1, source_target_pairs={{0,8},{8,16},{16,24},{24,28},{28,20},{20,12},{12,4},{4,0},{1,9},{9... | collective-permute-start | bytes 1179656 | tf_op jit(solution)/shard_map/ppermute | solution.py:594
  197.2 20.5 %collective-permute-start.37 = (bf16[2,192,512]{2,1,0:T(8,128)(2,1)S(1)}, bf16[2,192,512]{2,1,0:T(8,128)(2,1)S(1)}, u32[]{:S(2)}, u32[]{:S(2)}) collective-permute-start(bf16[2,192,512]{2,1,0:T(8,128)(2,1)S(1)} %get-tuple-element.204), channel_id=1, source_target_pairs={{8,0},{16,8},{24,16},{28,24},{20,28},{12,20},{4,12},{0,4},{9,1},{1... | collective-permute-start | bytes 1179656 | tf_op jit(solution)/shard_map/ppermute | solution.py:597
  199.2 18.5 %collective-permute-start.31 = (f32[8,768]{1,0:T(8,128)S(1)}, f32[8,768]{1,0:T(8,128)S(1)}, u32[]{:S(2)}, u32[]{:S(2)}) collective-permute-start(f32[8,768]{1,0:T(8,128)S(1)} %add.105), channel_id=1, source_target_pairs={{0,16},{4,20},{8,24},{12,28},{16,0},{20,4},{24,8},{28,12},{1,17},{... | collective-permute-start | bytes 73736 | tf_op jit(solution)/shard_map/ppermute | solution.py:852
  218.4 8.3 %collective-permute-start.38 = (bf16[2,192,512]{2,1,0:T(8,128)(2,1)S(1)}, bf16[2,192,512]{2,1,0:T(8,128)(2,1)S(1)}, u32[]{:S(2)}, u32[]{:S(2)}) collective-permute-start(bf16[2,192,512]{2,1,0:T(8,128)(2,1)S(1)} %get-tuple-element.205), channel_id=1, source_target_pairs={{0,8},{8,16},{16,24},{24,28},{28,20},{20,12},{12,4},{4,0},{1,9},{9... | collective-permute-start | bytes 1179656 | tf_op jit(solution)/shard_map/ppermute | solution.py:594
  218.7 8.5 %collective-permute-start.39 = (bf16[2,192,512]{2,1,0:T(8,128)(2,1)S(1)}, bf16[2,192,512]{2,1,0:T(8,128)(2,1)S(1)}, u32[]{:S(2)}, u32[]{:S(2)}) collective-permute-start(bf16[2,192,512]{2,1,0:T(8,128)(2,1)S(1)} %get-tuple-element.206), channel_id=1, source_target_pairs={{8,0},{16,8},{24,16},{28,24},{20,28},{12,20},{4,12},{0,4},{9,1},{1... | collective-permute-start | bytes 1179656 | tf_op jit(solution)/shard_map/ppermute | solution.py:597
  230.2 9.1 %collective-permute-start.40 = (bf16[256,768]{1,0:T(8,128)(2,1)S(1)}, bf16[256,768]{1,0:T(8,128)(2,1)S(1)}, u32[]{:S(2)}, u32[]{:S(2)}) collective-permute-start(bf16[256,768]{1,0:T(8,128)(2,1)S(1)} %get-tuple-element.210), channel_id=1, source_target_pairs={{0,1},{1,0},{2,3},{3,2},{4,5},{5,4},{6,7},{7,6},{8,9},{9,8},{10,11... | collective-permute-start | bytes 1179656 | tf_op jit(solution)/shard_map/ppermute | solution.py:652
  237.3 8.0 %collective-permute-start.44 = (bf16[96,768]{1,0:T(8,128)(2,1)S(1)}, bf16[96,768]{1,0:T(8,128)(2,1)S(1)}, u32[]{:S(2)}, u32[]{:S(2)}) collective-permute-start(bf16[96,768]{1,0:T(8,128)(2,1)S(1)} %get-tuple-element.223), channel_id=1, source_target_pairs={{0,8},{8,16},{16,24},{24,28},{28,20},{20,12},{12,4},{4,0},{1,9},{9... | collective-permute-start | bytes 442376 | tf_op jit(solution)/shard_map/ppermute | solution.py:594
  (52 other events, 475.5 us)
Sparse Core Ops, SparseCore 0:
  10.2 48.9 all-gather.4
  61.4 44.6 all-gather.2
  136.5 86.7 reduce-scatter.1

commit v3 on v2

--- a/solution.py
+++ b/solution.py
@@ -363,6 +363,20 @@
     return r * (dn - jnp.mean(dn, axis=-1, keepdims=True) - n * jnp.mean(dn * n, axis=-1, keepdims=True))
 
 
+def pack_kernel(s_ref, query_ref, key_ref, value_ref, out_ref, pack_ref):
+    turned = out_ref[...].astype(F32).T
+    parts = [ref[...].astype(F32) for ref in (query_ref, key_ref, value_ref)]
+    pack_ref[...] = jnp.concatenate([*parts, turned], axis=1).astype(BF)
+
+
+def finish_kernel(s_ref, part_ref, up_ref, down_ref, query_ref, key_ref, value_ref, out_ref):
+    width = query_ref.shape[1]
+    total = part_ref[...].astype(F32) + (up_ref[...].astype(F32) + down_ref[...].astype(F32))
+    for i, ref in enumerate((query_ref, key_ref, value_ref)):
+        ref[...] = total[:, i * width : (i + 1) * width]
+    out_ref[...] = total[:, 3 * width :].T
+
+
 def project_kernel(pieces, s_ref, *refs):
     w_refs, x_refs = refs[: pieces + 1], refs[pieces + 1 : pieces + 5]
     rows_ref, turned_ref, q_ref, natural_ref, kv_ref, w_s = refs[pieces + 5 :]
@@ -707,13 +721,16 @@
 
     pack_in = jnp.concatenate([w_ffn_in, ffn_bias[:, None]], axis=1)
     w_out = lax.all_gather(w_ffn_out, "dp", axis=0, tiled=True)
-    pack = jnp.concatenate([w_query, w_key, w_value, w_attn_out.T], axis=1)
     if by_ring:
+        (pack,) = fused(
+            pack_kernel, [((share, 4 * width), BF)], place, *map(apart, (w_query, w_key, w_value, w_attn_out))
+        )
         pieces = all_ring.gather(pack)
         pieces[2], pack_in = lax.optimization_barrier((pieces[2], pack_in))
         owners = [o for group in all_ring.groups() for o in group]
         owners = all_ring.members(data_index, owners)
     else:
+        pack = jnp.concatenate([w_query, w_key, w_value, w_attn_out.T], axis=1)
         pieces = list(spread_gather(pack, "dp", nd).reshape(2, model // 2, 4 * width))
         owners = jnp.zeros((1,), jnp.int32)
     hidden_units = w_ffn_in.shape[1]
@@ -743,7 +760,7 @@
             if state is not None:
                 going_up, going_down = lax.optimization_barrier((going_up, going_down, state[1]))[:2]
             if step + 2 == len(groups):
-                held.append([ring.send_up(going_up[:1]), ring.send_down(going_down[1:])])
+                held.append([apart(ring.send_up(going_up[:1])), apart(ring.send_down(going_down[1:]))])
             else:
                 going_up, going_down = ring.send_up(going_up), ring.send_down(going_down)
                 held.append([going_up, going_down])
@@ -865,7 +882,7 @@
             q_n,
             grad_mixed_n,
             aux,
-            [apart(kv) for kv in held[step]],
+            held[step] if step + 1 == len(groups) else [apart(kv) for kv in held[step]],
             prev,
             up_grad,
             state,
@@ -898,7 +915,7 @@
         total_kv.down,
         grad_query,
         rows_all,
-        apart(grad_w_attn),
+        grad_w_attn,
         apart(turned),
         scratch=[((3 * width, rows), BF), ((model, 4 * width), F32), ((rows, model), F32)],
     )
@@ -913,19 +930,25 @@
         for i in range(2, nd, 2):
             scalars = after(place, *((far,) if i == 4 else (grad_w_out, grad_w_in) if i == 6 else ()))
             last_sum.step(scalars, parts[i + 1], parts[i])
-        grads = parts[-1].astype(F32) + (last_sum.up.astype(F32) + last_sum.down.astype(F32))
+        grads = fused(
+            finish_kernel,
+            [((share, width), F32)] * 3 + [((width, share), F32)],
+            place,
+            parts[-1],
+            last_sum.up,
+            last_sum.down,
+        )
     else:
         grads = group_sum(parts[0], "dp", nd)
+        grads = [grads[:, i * width : (i + 1) * width] for i in range(4)]
+        grads[3] = grads[3].T
     grad_bias = lax.dynamic_slice_in_dim(sums[4], data_index * (hidden_units // nd), hidden_units // nd, 0)
     return (
         output,
         jnp.transpose(logits, (1, 0, 2)),
         grad_inputs,
         jnp.transpose(prev_grad, (1, 0, 2)),
-        grads[:, :width],
-        grads[:, width : 2 * width],
-        grads[:, 2 * width : 3 * width],
-        grads[:, 3 * width :].T,
+        *grads,
         grad_w_in,
         grad_bias,
         grad_w_out,

time: 268 us -> 262 us (0.978)
  waiting for transfers between devices: 90.6 us -> 78 us
  starting transfers between devices: 53 us -> 60.5 us
    ppermute x16, starting transfers between devices: 21.3 us -> 31.4 us  [send_down(): return lax.ppermute(x, self.axis, self.down)]
    ppermute x3, waiting for transfers between devices: 12.8 us -> 5.33 us  [sums_step(): return sums + lax.ppermute(sums, 'dp', [(i, i ^ bit) for i in range(nd)])]
    ppermute x16, starting transfers between devices: 17.2 us -> 11.2 us  [send_up(): return lax.ppermute(x, self.axis, self.up)]
    ppermute x3, starting transfers between devices: 3.74 us -> 6.6 us  [sums_step(): return sums + lax.ppermute(sums, 'dp', [(i, i ^ bit) for i in range(nd)])]
    pallas_call x14 -> x16, Pallas kernels: 28.9 us -> 31 us  [fused(): pl.pallas_call(body, out_shape=shapes, in_specs=[pl.BlockSpec(memory_spac...]
  transfers between devices with their start and end apart: 53 -> 53, of which waited for: 31 -> 30; matrix products, arithmetic and copies ran while one was open for 5% -> 5% of each run, Pallas kernels for 25% -> 26%
where the time goes in v3:
time: 262 us; the launch traced here: 261 us
  Pallas kernels  85.2 us (33%)
  waiting for transfers between devices  78 us (30%)
  starting transfers between devices  60.5 us (23%)
  between operations  14.4 us (5%)
  local copies, waits for them, and re-layouts  8.91 us (3%)
  blocking collectives  7.4 us (3%)
  other arithmetic  7.09 us (3%)
    ppermute x16, starting transfers between devices, send_down(): return lax.ppermute(x, self.axis, self.down)  31.4 us
    pallas_call x16, Pallas kernels, fused(): pl.pallas_call(body, out_shape=shapes, in_specs=[pl.BlockSpec(memory_spac...  31 us
    pallas_call x5, Pallas kernels, attend_backward(): pl.pallas_call(functools.partial(backward_kernel, first, last, pieces, pa...  28.5 us
    ppermute x16, waiting for transfers between devices, send_down(): return lax.ppermute(x, self.axis, self.down)  25.9 us
    pallas_call x5, Pallas kernels, attend_forward(): pl.pallas_call(functools.partial(forward_kernel, first, last, pieces, par...  25.6 us
    ppermute x8, waiting for transfers between devices, send_far(): return lax.ppermute(x, self.axis, self.flip_far)  23.7 us
    ppermute x16, waiting for transfers between devices, send_up(): return lax.ppermute(x, self.axis, self.up)  14.3 us
    ppermute x16, starting transfers between devices, send_up(): return lax.ppermute(x, self.axis, self.up)  11.2 us
  transfers between devices with their start and end apart: 53, of which 30 were waited for; matrix products, arithmetic and copies ran while one was open for 5% of the time, Pallas kernels for 26%

profile of v3, /device:TPU:0, one launch (start us, length us, event | category | flops | bytes accessed | tf_op | source)
XLA Modules:
  0.0 261.4 jit_solution(14865965902681754107)
XLA Ops:
  9.0 3.0 %collective-permute-start.1 = (bf16[96,768]{1,0:T(8,128)(2,1)S(1)}, bf16[96,768]{1,0:T(8,128)(2,1)S(1)}, u32[]{:S(2)}, u32[]{:S(2)}) collective-permute-start(bf16[96,768]{1,0:T(8,128)(2,1)S(1)} %shard_map.298.refs_0_), channel_id=1, source_target_pairs={{8,0},{16,8},{24,16},{28,24},{20,28},{12,20},{4,12},{0,4},{9,1},{1... | collective-permute-start | bytes 442376 | tf_op jit(solution)/shard_map/ppermute | solution.py:611
  36.9 2.5 shard_map.299
  42.1 5.4 %shard_map.300 = (bf16[3,512,4096]{2,1,0:T(8,128)(2,1)}, f32[3,512,128]{2,1,0:T(8,128)S(1)}) custom-call(s32[8]{0:T(128)S(1)} %get-tuple-element.127.refs_0_, s32[128]{0:T(128)S(1)} %reshape.59.refs_1_, bf16[3,512,64]{2,1,0:T(8,128)(2,1)S(1)} %get-tuple-element.130.refs_2_.refs_4_, bf16[2,192,512]{2,1,0:T(8,128)(2,1)S(1)} %get-tuple-element.131.refs_3_.refs_7_, ...), custom_call_target="tpu_custom_call" | custom-call | flops 201326592 | bytes 3145728 | tf_op jit(solution)/shard_map/pallas_call | solution.py:175
  47.6 8.7 %collective-permute-done.12.refs_4_.refs_8_ = bf16[2,192,512]{2,1,0:T(8,128)(2,1)S(1)} collective-permute-done((bf16[2,192,512]{2,1,0:T(8,128)(2,1)S(1)}, bf16[2,192,512]{2,1,0:T(8,128)(2,1)S(1)}, u32[]{:S(2)}, u32[]{:S(2)}) %collective-permute-start.12) | collective-permute-done | bytes 393248 | tf_op jit(solution)/shard_map/ppermute | solution.py:611
  57.4 2.8 %collective-permute-start.15 = (bf16[2,192,512]{2,1,0:T(8,128)(2,1)S(1)}, bf16[2,192,512]{2,1,0:T(8,128)(2,1)S(1)}, u32[]{:S(2)}, u32[]{:S(2)}) collective-permute-start(bf16[2,192,512]{2,1,0:T(8,128)(2,1)S(1)} %collective-permute-done.12.refs_4_.refs_8_), channel_id=1, source_target_pairs={{8,0},{16,8},{24,16},{28,24},{20,28},{12,20},{4,12},{0,4},{9,1},{1... | collective-permute-start | bytes 1179656 | tf_op jit(solution)/shard_map/ppermute | solution.py:611
  60.2 8.5 %shard_map.301 = (bf16[3,512,4096]{2,1,0:T(8,128)(2,1)}, f32[3,512,128]{2,1,0:T(8,128)S(1)}) custom-call(s32[8]{0:T(128)S(1)} %get-tuple-element.127.refs_0_, s32[128]{0:T(128)S(1)} %reshape.59.refs_1_, bf16[3,512,64]{2,1,0:T(8,128)(2,1)S(1)} %get-tuple-element.130.refs_2_.refs_4_, ...), custom_call_target="tpu_custom_call", output_to_operand_aliasing={{0}: (6, {})} | custom-call | flops 402653184 | bytes 6291456 | tf_op jit(solution)/shard_map/pallas_call | solution.py:175
  74.7 6.0 %shard_map.302 = (bf16[3,512,4096]{2,1,0:T(8,128)(2,1)}, f32[3,512,128]{2,1,0:T(8,128)S(1)}) custom-call(s32[8]{0:T(128)S(1)} %get-tuple-element.127.refs_0_, s32[128]{0:T(128)S(1)} %reshape.59.refs_1_, bf16[3,512,64]{2,1,0:T(8,128)(2,1)S(1)} %get-tuple-element.130.refs_2_.refs_4_, ...), custom_call_target="tpu_custom_call", output_to_operand_aliasing={{0}: (6, {})} | custom-call | flops 402653184 | bytes 6291456 | tf_op jit(solution)/shard_map/pallas_call | solution.py:175
  82.2 3.2 %collective-permute-start.19 = (bf16[1,192,512]{2,1,0:T(8,128)(2,1)S(1)}, bf16[1,192,512]{2,1,0:T(8,128)(2,1)S(1)}, u32[]{:S(2)}, u32[]{:S(2)}) collective-permute-start(bf16[1,192,512]{2,1,0:T(8,128)(2,1)S(1)} %slice.43), channel_id=1, source_target_pairs={{8,0},{16,8},{24,16},{28,24},{20,28},{12,20},{4,12},{0,4},{9,1},{1... | collective-permute-start | bytes 589832 | tf_op jit(solution)/shard_map/ppermute | solution.py:611
  85.4 3.0 %shard_map.303 = (bf16[3,512,4096]{2,1,0:T(8,128)(2,1)}, f32[3,512,128]{2,1,0:T(8,128)S(1)}) custom-call(s32[8]{0:T(128)S(1)} %get-tuple-element.127.refs_0_, s32[128]{0:T(128)S(1)} %reshape.59.refs_1_, bf16[3,512,64]{2,1,0:T(8,128)(2,1)S(1)} %get-tuple-element.130.refs_2_.refs_4_, ...), custom_call_target="tpu_custom_call", output_to_operand_aliasing={{0}: (6, {})} | custom-call | flops 402653184 | bytes 6291456 | tf_op jit(solution)/shard_map/pallas_call | solution.py:175
  88.9 4.6 %collective-permute-done.18.refs_3_.refs_7_ = bf16[1,192,512]{2,1,0:T(8,128)(2,1)S(1)} collective-permute-done((bf16[1,192,512]{2,1,0:T(8,128)(2,1)S(1)}, bf16[1,192,512]{2,1,0:T(8,128)(2,1)S(1)}, u32[]{:S(2)}, u32[]{:S(2)}) %collective-permute-start.18) | collective-permute-done | bytes 196640 | tf_op jit(solution)/shard_map/ppermute | solution.py:608
  94.1 2.7 %shard_map.304 = (bf16[3,512,4096]{2,1,0:T(8,128)(2,1)}, bf16[192,512]{1,0:T(8,128)(2,1)S(1)}, f32[3,512,128]{2,1,0:T(8,128)S(1)}) custom-call(s32[8]{0:T(128)S(1)} %get-tuple-element.127.refs_0_, s32[128]{0:T(128)S(1)} %reshape.59.refs_1_, bf16[3,512,64]{2,1,0:T(8,128)(2,1)S(1)} %get-tuple-element.130.refs_2_.refs_4_, ...), custom_call_target="tpu_custom_call", output_to_operand_aliasing={{0}: (6, {})} | custom-call | flops 201326592 | bytes 3145728 | tf_op jit(solution)/shard_map/pallas_call | solution.py:175
  98.6 7.4 %all_gather.9.mixed_ref = bf16[768,512]{1,0:T(8,128)(2,1)S(1)} all-gather(bf16[192,512]{1,0:T(8,128)(2,1)S(1)} %get-tuple-element.149.mixed_ref), channel_id=1, replica_groups=mesh['dp'=8,'tensor'=4] {'tensor'}, dimensions={0}, use_global_device_ids=true | all-gather | bytes 983040 | tf_op jit(solution)/shard_map/all_gather | solution.py:780
  106.0 5.7 %shard_map.305 = (bf16[512,768]{1,0:T(8,128)(2,1)S(1)}, bf16[512,768]{1,0:T(8,128)(2,1)S(1)}, f32[512,768]{1,0:T(8,128)S(1)}, f32[256,768]{1,0:T(8,128)S(1)}, f3...) custom-call(s32[9]{0:T(128)S(1)} %pad_add_fusion.s_ref, ...), custom_call_target="tpu_custom_call" | custom-call | bytes 1048576 | tf_op jit(solution)/shard_map/pallas_call | solution.py:339
  115.6 9.6 %collective-permute-done.24.b_ref = bf16[256,768]{1,0:T(8,128)(2,1)S(1)} collective-permute-done((bf16[256,768]{1,0:T(8,128)(2,1)S(1)}, bf16[256,768]{1,0:T(8,128)(2,1)S(1)}, u32[]{:S(2)}, u32[]{:S(2)}) %collective-permute-start.24) | collective-permute-done | bytes 393248 | tf_op jit(solution)/shard_map/ppermute | solution.py:669
  125.3 2.7 %shard_map.306 = (bf16[128,768]{1,0:T(8,128)(2,1)}, f32[256,768]{1,0:T(8,128)S(1)}, bf16[256,768]{1,0:T(8,128)(2,1)S(1)}, f32[2,768]{1,0:T(2,128)S(1)}) custom-call(s32[9]{0:T(128)S(1)} %pad_add_fusion.s_ref, bf16[256,768]{1,0:T(8,128)(2,1)S(1)} %add_convert_fusion.2.a_ref, bf16[256,768]{1,0:T(8,128)(2,1)S(1)} %collective-permute-done.24.b_ref, ...), custom_call_target="tpu_custom_call" | custom-call | bytes 1048576 | tf_op jit(solution)/shard_map/pallas_call | solution.py:339
  129.7 3.5 %shard_map.307 = (bf16[512,768]{1,0:T(8,128)(2,1)S(1)}, bf16[512,768]{1,0:T(8,128)(2,1)S(1)}, f32[1,768]{1,0:T(1,128)S(1)}, bf16[256,768]{1,0:T(8,128)(2,1)S(1)}, bf16[256,768]{1,0:T(8,128)(2,1)S(1)}) custom-call(s32[9]{0:T(128)S(1)} %pad_add_fusion.s_ref, bf16[256,768]{1,0:T(8,128)(2,1)S(1)} %get-tuple-element.165.low_ref, ...), custom_call_target="tpu_custom_call" | custom-call | bytes 1048576 | tf_op jit(solution)/shard_map/pallas_call | solution.py:339
  133.2 3.5 %shard_map.308 = bf16[768,1536]{1,0:T(8,128)(2,1)} custom-call(s32[9]{0:T(128)S(1)} %pad_add_fusion.s_ref, bf16[512,768]{1,0:T(8,128)(2,1)S(1)} %get-tuple-element.169.active_ref, bf16[512,768]{1,0:T(8,128)(2,1)S(1)} %get-tuple-element.170.second_ref, bf16[512,768]{1,0:T(8,128)(2,1)S(1)} %get-tuple-element.171.low_ref, ...), custom_call_target="tpu_custom_call" | custom-call | bytes 1048576 | tf_op jit(solution)/shard_map/pallas_call | solution.py:339
  140.4 9.4 %collective-permute-done.27.b_ref = bf16[256,768]{1,0:T(8,128)(2,1)S(1)} collective-permute-done((bf16[256,768]{1,0:T(8,128)(2,1)S(1)}, bf16[256,768]{1,0:T(8,128)(2,1)S(1)}, u32[]{:S(2)}, u32[]{:S(2)}) %collective-permute-start.27) | collective-permute-done | bytes 393248 | tf_op jit(solution)/shard_map/ppermute | solution.py:669
  155.7 2.6 shard_map.311
  158.9 5.9 %collective-permute-start.33 = (bf16[1,192,512]{2,1,0:T(8,128)(2,1)S(1)}, bf16[1,192,512]{2,1,0:T(8,128)(2,1)S(1)}, u32[]{:S(2)}, u32[]{:S(2)}) collective-permute-start(bf16[1,192,512]{2,1,0:T(8,128)(2,1)S(1)} %get-tuple-element.204), channel_id=1, source_target_pairs={{8,0},{16,8},{24,16},{28,24},{20,28},{12,20},{4,12},{0,4},{9,1},{1... | collective-permute-start | bytes 589832 | tf_op jit(solution)/shard_map/ppermute | solution.py:611
  166.8 3.4 %shard_map.312 = (bf16[3,512,4096]{2,1,0:T(8,128)(2,1)}, bf16[2,192,512]{2,1,0:T(8,128)(2,1)S(1)}, bf16[2,192,512]{2,1,0:T(8,128)(2,1)S(1)}, f32[3,512,64]{2,1,0:T(8,128)S(1)}) custom-call(s32[8]{0:T(128)S(1)} %get-tuple-element.127.refs_0_, s32[128]{0:T(128)S(1)} %reshape.59.refs_1_, ...), custom_call_target="tpu_custom_call", output_to_operand_aliasing={{0}: (11, {})} | custom-call | flops 1006632960 | bytes 9437184 | tf_op jit(solution)/shard_map/pallas_call | solution.py:311
  170.6 7.2 %collective-permute-done.33.down_ref = bf16[1,192,512]{2,1,0:T(8,128)(2,1)S(1)} collective-permute-done((bf16[1,192,512]{2,1,0:T(8,128)(2,1)S(1)}, bf16[1,192,512]{2,1,0:T(8,128)(2,1)S(1)}, u32[]{:S(2)}, u32[]{:S(2)}) %collective-permute-start.33) | collective-permute-done | bytes 196640 | tf_op jit(solution)/shard_map/ppermute | solution.py:611
  182.9 6.9 %shard_map.313 = (bf16[3,512,4096]{2,1,0:T(8,128)(2,1)}, bf16[2,192,512]{2,1,0:T(8,128)(2,1)S(1)}, bf16[2,192,512]{2,1,0:T(8,128)(2,1)S(1)}, f32[3,512,64]{2,1,0:T(8,128)S(1)}) custom-call(s32[8]{0:T(128)S(1)} %get-tuple-element.127.refs_0_, s32[128]{0:T(128)S(1)} %reshape.59.refs_1_, ...), custom_call_target="tpu_custom_call", output_to_operand_aliasing={{0}: (11, {})} | custom-call | flops 1006632960 | bytes 9437184 | tf_op jit(solution)/shard_map/pallas_call | solution.py:311
  195.0 2.4 collective-permute-start.31
  197.3 9.4 %shard_map.314 = (bf16[3,512,4096]{2,1,0:T(8,128)(2,1)}, bf16[2,192,512]{2,1,0:T(8,128)(2,1)S(1)}, bf16[2,192,512]{2,1,0:T(8,128)(2,1)S(1)}, f32[3,512,64]{2,1,0:T(8,128)S(1)}) custom-call(s32[8]{0:T(128)S(1)} %get-tuple-element.127.refs_0_, s32[128]{0:T(128)S(1)} %reshape.59.refs_1_, ...), custom_call_target="tpu_custom_call", output_to_operand_aliasing={{0}: (11, {})} | custom-call | flops 1006632960 | bytes 9437184 | tf_op jit(solution)/shard_map/pallas_call | solution.py:311
  206.8 3.1 %collective-permute-done.31 = f32[8,768]{1,0:T(8,128)S(1)} collective-permute-done((f32[8,768]{1,0:T(8,128)S(1)}, f32[8,768]{1,0:T(8,128)S(1)}, u32[]{:S(2)}, u32[]{:S(2)}) %collective-permute-start.31) | collective-permute-done | bytes 24608 | tf_op jit(solution)/shard_map/ppermute | solution.py:869
  212.7 6.2 %shard_map.315 = (bf16[3,512,4096]{2,1,0:T(8,128)(2,1)}, bf16[2,192,512]{2,1,0:T(8,128)(2,1)S(1)}, bf16[192,512]{1,0:T(8,128)(2,1)S(1)}) custom-call(s32[8]{0:T(128)S(1)} %get-tuple-element.127.refs_0_, s32[128]{0:T(128)S(1)} %reshape.59.refs_1_, bf16[192,512]{1,0:T(8,128)(2,1)S(1)} %get-tuple-element.133.refs_2_, ...), custom_call_target="tpu_custom_call", output_to_operand_aliasing={{0}: (10, {})} | custom-call | flops 503316480 | bytes 4718592 | tf_op jit(solution)/shard_map/pallas_call | solution.py:311
  220.5 2.3 collective-permute-done.39.down_ref
  222.9 2.8 %shard_map.319 = (bf16[48,768]{1,0:T(8,128)(2,1)S(1)}, bf16[48,768]{1,0:T(8,128)(2,1)S(1)}, bf16[96,768]{1,0:T(8,128)(2,1)S(1)}, bf16[96,768]{1,0:T(8,128)(2,1)S...) custom-call(s32[9]{0:T(128)S(1)} %pad_add_fusion.s_ref, ...), custom_call_target="tpu_custom_call" | custom-call | bytes 1048576 | tf_op jit(solution)/shard_map/pallas_call | solution.py:339
  227.9 2.6 collective-permute-done.42.up_ref
  237.4 2.6 %collective-permute-done.41 = bf16[128,768]{1,0:T(8,128)(2,1)S(1)} collective-permute-done((bf16[128,768]{1,0:T(8,128)(2,1)S(1)}, bf16[128,768]{1,0:T(8,128)(2,1)S(1)}, u32[]{:S(2)}, u32[]{:S(2)}) %collective-permute-start.41) | collective-permute-done | bytes 196640 | tf_op jit(solution)/shard_map/ppermute | solution.py:669
  250.6 2.3 collective-permute-done.48.up_ref
  (195 shorter events, 95.0 us)
Async XLA Ops:
  7.2 98.8 %all-gather.5.cloned.1.call-start = ((), (), s32[]{:S(2)}) async-start(), calls=%async_computation.2 | async-start | bytes 1327104 | tf_op jit(solution)/shard_map/all_gather | solution.py:723
  7.9 98.1 %all-gather.3.cloned.1.call-start = ((), (), s32[]{:S(2)}) async-start(), calls=%async_computation.1 | async-start | bytes 1548288 | tf_op jit(solution)/shard_map/all_gather | solution.py:737
  9.0 7.6 %collective-permute-start.1 = (bf16[96,768]{1,0:T(8,128)(2,1)S(1)}, bf16[96,768]{1,0:T(8,128)(2,1)S(1)}, u32[]{:S(2)}, u32[]{:S(2)}) collective-permute-start(bf16[96,768]{1,0:T(8,128)(2,1)S(1)} %shard_map.298.refs_0_), channel_id=1, source_target_pairs={{8,0},{16,8},{24,16},{28,24},{20,28},{12,20},{4,12},{0,4},{9,1},{1... | collective-permute-start | bytes 442376 | tf_op jit(solution)/shard_map/ppermute | solution.py:611
  12.2 16.6 %collective-permute-start.8 = (bf16[128,768]{1,0:T(8,128)(2,1)}, bf16[128,768]{1,0:T(8,128)(2,1)S(1)}, u32[]{:S(2)}, u32[]{:S(2)}) collective-permute-start(bf16[128,768]{1,0:T(8,128)(2,1)} %refs_9_.1), channel_id=1, source_target_pairs={{0,1},{1,0},{2,3},{3,2},{4,5},{5,4},{6,7},{7,6},{8,9},{9,8},{10,11... | collective-permute-start | bytes 589832 | tf_op jit(solution)/shard_map/ppermute | solution.py:666
  12.2 20.2 %collective-permute-start.9 = (bf16[128,768]{1,0:T(8,128)(2,1)}, bf16[128,768]{1,0:T(8,128)(2,1)S(1)}, u32[]{:S(2)}, u32[]{:S(2)}) collective-permute-start(bf16[128,768]{1,0:T(8,128)(2,1)} %refs_9_.1), channel_id=1, source_target_pairs={{0,2},{1,3},{2,0},{3,1},{4,6},{5,7},{6,4},{7,5},{8,10},{9,11},{10,... | collective-permute-start | bytes 589832 | tf_op jit(solution)/shard_map/ppermute | solution.py:669
  21.2 221.6 %reduce-scatter.2.cloned.1.call-start = ((), (), s32[]{:S(2)}) async-start(), calls=%async_computation.3 | async-start | bytes 2654208 | tf_op jit(solution)/shard_map/reduce_scatter | solution.py:829
  22.7 7.4 %collective-permute-start.5 = (bf16[96,768]{1,0:T(8,128)(2,1)S(1)}, bf16[96,768]{1,0:T(8,128)(2,1)S(1)}, u32[]{:S(2)}, u32[]{:S(2)}) collective-permute-start(bf16[96,768]{1,0:T(8,128)(2,1)S(1)} %collective-permute-done.3.refs_4_), channel_id=1, source_target_pairs={{8,0},{16,8},{24,16},{28,24},{20,28},{12,20},{4,12},{0,4},{9,1},{1... | collective-permute-start | bytes 442376 | tf_op jit(solution)/shard_map/ppermute | solution.py:611
  39.3 16.9 %collective-permute-start.12 = (bf16[2,192,512]{2,1,0:T(8,128)(2,1)S(1)}, bf16[2,192,512]{2,1,0:T(8,128)(2,1)S(1)}, u32[]{:S(2)}, u32[]{:S(2)}) collective-permute-start(bf16[2,192,512]{2,1,0:T(8,128)(2,1)S(1)} %get-tuple-element.131.refs_3_.refs_7_), channel_id=1, source_target_pairs={{8,0},{16,8},{24,16},{28,24},{20,28},{12,20},{4,12},{0,4},{9,1},{1... | collective-permute-start | bytes 1179656 | tf_op jit(solution)/shard_map/ppermute | solution.py:611
  41.4 14.8 %collective-permute-start.11 = (bf16[2,192,512]{2,1,0:T(8,128)(2,1)S(1)}, bf16[2,192,512]{2,1,0:T(8,128)(2,1)S(1)}, u32[]{:S(2)}, u32[]{:S(2)}) collective-permute-start(bf16[2,192,512]{2,1,0:T(8,128)(2,1)S(1)} %get-tuple-element.131.refs_3_.refs_7_), channel_id=1, source_target_pairs={{0,8},{8,16},{16,24},{24,28},{28,20},{20,12},{12,4},{4,0},{1,9},{9... | collective-permute-start | bytes 1179656 | tf_op jit(solution)/shard_map/ppermute | solution.py:608
  56.3 12.5 %collective-permute-start.14 = (bf16[2,192,512]{2,1,0:T(8,128)(2,1)S(1)}, bf16[2,192,512]{2,1,0:T(8,128)(2,1)S(1)}, u32[]{:S(2)}, u32[]{:S(2)}) collective-permute-start(bf16[2,192,512]{2,1,0:T(8,128)(2,1)S(1)} %collective-permute-done.11.refs_3_.refs_7_), channel_id=1, source_target_pairs={{0,8},{8,16},{16,24},{24,28},{28,20},{20,12},{12,4},{4,0},{1,9},{9... | collective-permute-start | bytes 1179656 | tf_op jit(solution)/shard_map/ppermute | solution.py:608
  57.4 11.4 %collective-permute-start.15 = (bf16[2,192,512]{2,1,0:T(8,128)(2,1)S(1)}, bf16[2,192,512]{2,1,0:T(8,128)(2,1)S(1)}, u32[]{:S(2)}, u32[]{:S(2)}) collective-permute-start(bf16[2,192,512]{2,1,0:T(8,128)(2,1)S(1)} %collective-permute-done.12.refs_4_.refs_8_), channel_id=1, source_target_pairs={{8,0},{16,8},{24,16},{28,24},{20,28},{12,20},{4,12},{0,4},{9,1},{1... | collective-permute-start | bytes 1179656 | tf_op jit(solution)/shard_map/ppermute | solution.py:611
  68.8 11.9 %collective-permute-start.16 = (bf16[2,192,512]{2,1,0:T(8,128)(2,1)S(1)}, bf16[2,192,512]{2,1,0:T(8,128)(2,1)S(1)}, u32[]{:S(2)}, u32[]{:S(2)}) collective-permute-start(bf16[2,192,512]{2,1,0:T(8,128)(2,1)S(1)} %collective-permute-done.14.refs_3_.refs_7_), channel_id=1, source_target_pairs={{0,8},{8,16},{16,24},{24,28},{28,20},{20,12},{12,4},{4,0},{1,9},{9... | collective-permute-start | bytes 1179656 | tf_op jit(solution)/shard_map/ppermute | solution.py:608
  68.9 13.3 %collective-permute-start.17 = (bf16[2,192,512]{2,1,0:T(8,128)(2,1)S(1)}, bf16[2,192,512]{2,1,0:T(8,128)(2,1)S(1)}, u32[]{:S(2)}, u32[]{:S(2)}) collective-permute-start(bf16[2,192,512]{2,1,0:T(8,128)(2,1)S(1)} %collective-permute-done.15.refs_4_.refs_8_), channel_id=1, source_target_pairs={{8,0},{16,8},{24,16},{28,24},{20,28},{12,20},{4,12},{0,4},{9,1},{1... | collective-permute-start | bytes 1179656 | tf_op jit(solution)/shard_map/ppermute | solution.py:611
  72.6 25.2 %collective-permute-start.22 = (bf16[192,768]{1,0:T(8,128)(2,1)S(1)}, bf16[192,768]{1,0:T(8,128)(2,1)S(1)}, u32[]{:S(2)}, u32[]{:S(2)}) collective-permute-start(bf16[192,768]{1,0:T(8,128)(2,1)S(1)} %collective-permute-done.20.o1), channel_id=1, source_target_pairs={{0,2},{1,3},{2,0},{3,1},{4,6},{5,7},{6,4},{7,5},{8,10},{9,11},{10,... | collective-permute-start | bytes 884744 | tf_op jit(solution)/shard_map/ppermute | solution.py:669
  73.7 24.9 %collective-permute-start.21 = (bf16[192,768]{1,0:T(8,128)(2,1)S(1)}, bf16[192,768]{1,0:T(8,128)(2,1)}, u32[]{:S(2)}, u32[]{:S(2)}) collective-permute-start(bf16[192,768]{1,0:T(8,128)(2,1)S(1)} %slice.44.o0.o_ref), channel_id=1, source_target_pairs={{0,2},{1,3},{2,0},{3,1},{4,6},{5,7},{6,4},{7,5},{8,10},{9,11},{10,... | collective-permute-start | bytes 884744 | tf_op jit(solution)/shard_map/ppermute | solution.py:669
  82.2 6.7 %collective-permute-start.19 = (bf16[1,192,512]{2,1,0:T(8,128)(2,1)S(1)}, bf16[1,192,512]{2,1,0:T(8,128)(2,1)S(1)}, u32[]{:S(2)}, u32[]{:S(2)}) collective-permute-start(bf16[1,192,512]{2,1,0:T(8,128)(2,1)S(1)} %slice.43), channel_id=1, source_target_pairs={{8,0},{16,8},{24,16},{28,24},{20,28},{12,20},{4,12},{0,4},{9,1},{1... | collective-permute-start | bytes 589832 | tf_op jit(solution)/shard_map/ppermute | solution.py:611
  85.4 8.0 %collective-permute-start.18 = (bf16[1,192,512]{2,1,0:T(8,128)(2,1)S(1)}, bf16[1,192,512]{2,1,0:T(8,128)(2,1)S(1)}, u32[]{:S(2)}, u32[]{:S(2)}) collective-permute-start(bf16[1,192,512]{2,1,0:T(8,128)(2,1)S(1)} %slice.42), channel_id=1, source_target_pairs={{0,8},{8,16},{16,24},{24,28},{28,20},{20,12},{12,4},{4,0},{1,9},{9... | collective-permute-start | bytes 589832 | tf_op jit(solution)/shard_map/ppermute | solution.py:608
  113.6 11.6 %collective-permute-start.24 = (bf16[256,768]{1,0:T(8,128)(2,1)S(1)}, bf16[256,768]{1,0:T(8,128)(2,1)S(1)}, u32[]{:S(2)}, u32[]{:S(2)}) collective-permute-start(bf16[256,768]{1,0:T(8,128)(2,1)S(1)} %add_convert_fusion.2.a_ref), channel_id=1, source_target_pairs={{0,2},{1,3},{2,0},{3,1},{4,6},{5,7},{6,4},{7,5},{8,10},{9,11},{10,... | collective-permute-start | bytes 1179656 | tf_op jit(solution)/shard_map/ppermute | solution.py:669
  138.6 11.2 %collective-permute-start.27 = (bf16[256,768]{1,0:T(8,128)(2,1)S(1)}, bf16[256,768]{1,0:T(8,128)(2,1)S(1)}, u32[]{:S(2)}, u32[]{:S(2)}) collective-permute-start(bf16[256,768]{1,0:T(8,128)(2,1)S(1)} %add_convert_fusion.1.a_ref), channel_id=1, source_target_pairs={{0,2},{1,3},{2,0},{3,1},{4,6},{5,7},{6,4},{7,5},{8,10},{9,11},{10,... | collective-permute-start | bytes 1179656 | tf_op jit(solution)/shard_map/ppermute | solution.py:669
  158.3 12.3 %collective-permute-start.32 = (bf16[1,192,512]{2,1,0:T(8,128)(2,1)S(1)}, bf16[1,192,512]{2,1,0:T(8,128)(2,1)S(1)}, u32[]{:S(2)}, u32[]{:S(2)}) collective-permute-start(bf16[1,192,512]{2,1,0:T(8,128)(2,1)S(1)} %get-tuple-element.203), channel_id=1, source_target_pairs={{0,8},{8,16},{16,24},{24,28},{28,20},{20,12},{12,4},{4,0},{1,9},{9... | collective-permute-start | bytes 589832 | tf_op jit(solution)/shard_map/ppermute | solution.py:608
  158.9 18.8 %collective-permute-start.33 = (bf16[1,192,512]{2,1,0:T(8,128)(2,1)S(1)}, bf16[1,192,512]{2,1,0:T(8,128)(2,1)S(1)}, u32[]{:S(2)}, u32[]{:S(2)}) collective-permute-start(bf16[1,192,512]{2,1,0:T(8,128)(2,1)S(1)} %get-tuple-element.204), channel_id=1, source_target_pairs={{8,0},{16,8},{24,16},{28,24},{20,28},{12,20},{4,12},{0,4},{9,1},{1... | collective-permute-start | bytes 589832 | tf_op jit(solution)/shard_map/ppermute | solution.py:611
  178.4 13.8 %collective-permute-start.34 = (bf16[2,192,512]{2,1,0:T(8,128)(2,1)S(1)}, bf16[2,192,512]{2,1,0:T(8,128)(2,1)S(1)}, u32[]{:S(2)}, u32[]{:S(2)}) collective-permute-start(bf16[2,192,512]{2,1,0:T(8,128)(2,1)S(1)} %get-tuple-element.205), channel_id=1, source_target_pairs={{0,8},{8,16},{16,24},{24,28},{28,20},{20,12},{12,4},{4,0},{1,9},{9... | collective-permute-start | bytes 1179656 | tf_op jit(solution)/shard_map/ppermute | solution.py:608
  179.2 13.0 %collective-permute-start.35 = (bf16[2,192,512]{2,1,0:T(8,128)(2,1)S(1)}, bf16[2,192,512]{2,1,0:T(8,128)(2,1)S(1)}, u32[]{:S(2)}, u32[]{:S(2)}) collective-permute-start(bf16[2,192,512]{2,1,0:T(8,128)(2,1)S(1)} %get-tuple-element.206), channel_id=1, source_target_pairs={{8,0},{16,8},{24,16},{28,24},{20,28},{12,20},{4,12},{0,4},{9,1},{1... | collective-permute-start | bytes 1179656 | tf_op jit(solution)/shard_map/ppermute | solution.py:611
  180.7 11.1 %collective-permute-start.30 = (f32[8,768]{1,0:T(8,128)S(1)}, f32[8,768]{1,0:T(8,128)S(1)}, u32[]{:S(2)}, u32[]{:S(2)}) collective-permute-start(f32[8,768]{1,0:T(8,128)S(1)} %add.98), channel_id=1, source_target_pairs={{0,8},{4,12},{8,0},{12,4},{16,24},{20,28},{24,16},{28,20},{1,9},{5... | collective-permute-start | bytes 73736 | tf_op jit(solution)/shard_map/ppermute | solution.py:869
  192.9 17.0 %collective-permute-start.36 = (bf16[2,192,512]{2,1,0:T(8,128)(2,1)S(1)}, bf16[2,192,512]{2,1,0:T(8,128)(2,1)S(1)}, u32[]{:S(2)}, u32[]{:S(2)}) collective-permute-start(bf16[2,192,512]{2,1,0:T(8,128)(2,1)S(1)} %get-tuple-element.207), channel_id=1, source_target_pairs={{0,8},{8,16},{16,24},{24,28},{28,20},{20,12},{12,4},{4,0},{1,9},{9... | collective-permute-start | bytes 1179656 | tf_op jit(solution)/shard_map/ppermute | solution.py:608
  193.8 16.1 %collective-permute-start.37 = (bf16[2,192,512]{2,1,0:T(8,128)(2,1)S(1)}, bf16[2,192,512]{2,1,0:T(8,128)(2,1)S(1)}, u32[]{:S(2)}, u32[]{:S(2)}) collective-permute-start(bf16[2,192,512]{2,1,0:T(8,128)(2,1)S(1)} %get-tuple-element.208), channel_id=1, source_target_pairs={{8,0},{16,8},{24,16},{28,24},{20,28},{12,20},{4,12},{0,4},{9,1},{1... | collective-permute-start | bytes 1179656 | tf_op jit(solution)/shard_map/ppermute | solution.py:611
  195.0 14.9 %collective-permute-start.31 = (f32[8,768]{1,0:T(8,128)S(1)}, f32[8,768]{1,0:T(8,128)S(1)}, u32[]{:S(2)}, u32[]{:S(2)}) collective-permute-start(f32[8,768]{1,0:T(8,128)S(1)} %add.99), channel_id=1, source_target_pairs={{0,16},{4,20},{8,24},{12,28},{16,0},{20,4},{24,8},{28,12},{1,17},{... | collective-permute-start | bytes 73736 | tf_op jit(solution)/shard_map/ppermute | solution.py:869
  210.6 9.9 %collective-permute-start.38 = (bf16[2,192,512]{2,1,0:T(8,128)(2,1)S(1)}, bf16[2,192,512]{2,1,0:T(8,128)(2,1)S(1)}, u32[]{:S(2)}, u32[]{:S(2)}) collective-permute-start(bf16[2,192,512]{2,1,0:T(8,128)(2,1)S(1)} %get-tuple-element.209), channel_id=1, source_target_pairs={{0,8},{8,16},{16,24},{24,28},{28,20},{20,12},{12,4},{4,0},{1,9},{9... | collective-permute-start | bytes 1179656 | tf_op jit(solution)/shard_map/ppermute | solution.py:608
  210.7 12.2 %collective-permute-start.39 = (bf16[2,192,512]{2,1,0:T(8,128)(2,1)S(1)}, bf16[2,192,512]{2,1,0:T(8,128)(2,1)S(1)}, u32[]{:S(2)}, u32[]{:S(2)}) collective-permute-start(bf16[2,192,512]{2,1,0:T(8,128)(2,1)S(1)} %get-tuple-element.210), channel_id=1, source_target_pairs={{8,0},{16,8},{24,16},{28,24},{20,28},{12,20},{4,12},{0,4},{9,1},{1... | collective-permute-start | bytes 1179656 | tf_op jit(solution)/shard_map/ppermute | solution.py:611
  225.7 8.5 %collective-permute-start.40 = (bf16[256,768]{1,0:T(8,128)(2,1)S(1)}, bf16[256,768]{1,0:T(8,128)(2,1)S(1)}, u32[]{:S(2)}, u32[]{:S(2)}) collective-permute-start(bf16[256,768]{1,0:T(8,128)(2,1)S(1)} %get-tuple-element.214), channel_id=1, source_target_pairs={{0,1},{1,0},{2,3},{3,2},{4,5},{5,4},{6,7},{7,6},{8,9},{9,8},{10,11... | collective-permute-start | bytes 1179656 | tf_op jit(solution)/shard_map/ppermute | solution.py:666
  232.1 8.0 %collective-permute-start.44 = (bf16[96,768]{1,0:T(8,128)(2,1)S(1)}, bf16[96,768]{1,0:T(8,128)(2,1)S(1)}, u32[]{:S(2)}, u32[]{:S(2)}) collective-permute-start(bf16[96,768]{1,0:T(8,128)(2,1)S(1)} %get-tuple-element.227), channel_id=1, source_target_pairs={{0,8},{8,16},{16,24},{24,28},{28,20},{20,12},{12,4},{4,0},{1,9},{9... | collective-permute-start | bytes 442376 | tf_op jit(solution)/shard_map/ppermute | solution.py:608
  233.4 6.7 %collective-permute-start.45 = (bf16[96,768]{1,0:T(8,128)(2,1)S(1)}, bf16[96,768]{1,0:T(8,128)(2,1)S(1)}, u32[]{:S(2)}, u32[]{:S(2)}) collective-permute-start(bf16[96,768]{1,0:T(8,128)(2,1)S(1)} %get-tuple-element.228), channel_id=1, source_target_pairs={{8,0},{16,8},{24,16},{28,24},{20,28},{12,20},{4,12},{0,4},{9,1},{1... | collective-permute-start | bytes 442376 | tf_op jit(solution)/shard_map/ppermute | solution.py:611
  (51 other events, 471.5 us)
Sparse Core Ops, SparseCore 0:
  10.2 48.7 all-gather.4
  61.2 44.1 all-gather.2
  136.8 82.0 reduce-scatter.1

commit v4 on v3

--- a/solution.py
+++ b/solution.py
@@ -928,7 +928,7 @@
     grad_inputs = grad_first + (kept.astype(F32) + far.astype(F32))
     if by_ring:
         for i in range(2, nd, 2):
-            scalars = after(place, *((far,) if i == 4 else (grad_w_out, grad_w_in) if i == 6 else ()))
+            scalars = after(place, *((far, grad_w_out, grad_w_in) if i == 6 else ()))
             last_sum.step(scalars, parts[i + 1], parts[i])
         grads = fused(
             finish_kernel,

time: 262 us -> 262 us (level)
    ppermute x16, starting transfers between devices: 11.2 us -> 15 us  [send_up(): return lax.ppermute(x, self.axis, self.up)]
    ppermute x16, starting transfers between devices: 31.4 us -> 27.9 us  [send_down(): return lax.ppermute(x, self.axis, self.down)]
where the time goes in v4:
time: 262 us
  Pallas kernels  85.2 us (33%)
  waiting for transfers between devices  79.1 us (30%)
  starting transfers between devices  60.2 us (23%)
  between operations  14.4 us (5%)
  local copies, waits for them, and re-layouts  8.18 us (3%)
  blocking collectives  7.41 us (3%)
  other arithmetic  7.08 us (3%)
    pallas_call x16, Pallas kernels, fused(): pl.pallas_call(body, out_shape=shapes, in_specs=[pl.BlockSpec(memory_spac...  31 us
    pallas_call x5, Pallas kernels, attend_backward(): pl.pallas_call(functools.partial(backward_kernel, first, last, pieces, pa...  28.5 us
    ppermute x16, starting transfers between devices, send_down(): return lax.ppermute(x, self.axis, self.down)  27.9 us
    pallas_call x5, Pallas kernels, attend_forward(): pl.pallas_call(functools.partial(forward_kernel, first, last, pieces, par...  25.6 us
    ppermute x8, waiting for transfers between devices, send_far(): return lax.ppermute(x, self.axis, self.flip_far)  24.9 us
    ppermute x16, waiting for transfers between devices, send_down(): return lax.ppermute(x, self.axis, self.down)  23.7 us
    ppermute x16, starting transfers between devices, send_up(): return lax.ppermute(x, self.axis, self.up)  15 us
    ppermute x16, waiting for transfers between devices, send_up(): return lax.ppermute(x, self.axis, self.up)  13.8 us
  transfers between devices with their start and end apart: 53, of which 30 were waited for; matrix products, arithmetic and copies ran while one was open for 5% of the time, Pallas kernels for 26%

profile of v4, /device:TPU:0, one launch (start us, length us, event | category | flops | bytes accessed | tf_op | source)
XLA Modules:
  0.0 261.6 jit_solution(11134201547560667485)
XLA Ops:
  9.0 3.0 %collective-permute-start.1 = (bf16[96,768]{1,0:T(8,128)(2,1)S(1)}, bf16[96,768]{1,0:T(8,128)(2,1)S(1)}, u32[]{:S(2)}, u32[]{:S(2)}) collective-permute-start(bf16[96,768]{1,0:T(8,128)(2,1)S(1)} %shard_map.298.refs_0_), channel_id=1, source_target_pairs={{8,0},{16,8},{24,16},{28,24},{20,28},{12,20},{4,12},{0,4},{9,1},{1... | collective-permute-start | bytes 442376 | tf_op jit(solution)/shard_map/ppermute | solution.py:611
  36.9 2.5 shard_map.299
  42.1 5.4 %shard_map.300 = (bf16[3,512,4096]{2,1,0:T(8,128)(2,1)}, f32[3,512,128]{2,1,0:T(8,128)S(1)}) custom-call(s32[8]{0:T(128)S(1)} %get-tuple-element.126.refs_0_, s32[128]{0:T(128)S(1)} %reshape.59.refs_1_, bf16[3,512,64]{2,1,0:T(8,128)(2,1)S(1)} %get-tuple-element.129.refs_2_.refs_4_, bf16[2,192,512]{2,1,0:T(8,128)(2,1)S(1)} %get-tuple-element.130.refs_3_.refs_7_, ...), custom_call_target="tpu_custom_call" | custom-call | flops 201326592 | bytes 3145728 | tf_op jit(solution)/shard_map/pallas_call | solution.py:175
  47.6 8.7 %collective-permute-done.12.refs_4_.refs_8_ = bf16[2,192,512]{2,1,0:T(8,128)(2,1)S(1)} collective-permute-done((bf16[2,192,512]{2,1,0:T(8,128)(2,1)S(1)}, bf16[2,192,512]{2,1,0:T(8,128)(2,1)S(1)}, u32[]{:S(2)}, u32[]{:S(2)}) %collective-permute-start.12) | collective-permute-done | bytes 393248 | tf_op jit(solution)/shard_map/ppermute | solution.py:611
  57.4 2.8 %collective-permute-start.15 = (bf16[2,192,512]{2,1,0:T(8,128)(2,1)S(1)}, bf16[2,192,512]{2,1,0:T(8,128)(2,1)S(1)}, u32[]{:S(2)}, u32[]{:S(2)}) collective-permute-start(bf16[2,192,512]{2,1,0:T(8,128)(2,1)S(1)} %collective-permute-done.12.refs_4_.refs_8_), channel_id=1, source_target_pairs={{8,0},{16,8},{24,16},{28,24},{20,28},{12,20},{4,12},{0,4},{9,1},{1... | collective-permute-start | bytes 1179656 | tf_op jit(solution)/shard_map/ppermute | solution.py:611
  60.2 8.5 %shard_map.301 = (bf16[3,512,4096]{2,1,0:T(8,128)(2,1)}, f32[3,512,128]{2,1,0:T(8,128)S(1)}) custom-call(s32[8]{0:T(128)S(1)} %get-tuple-element.126.refs_0_, s32[128]{0:T(128)S(1)} %reshape.59.refs_1_, bf16[3,512,64]{2,1,0:T(8,128)(2,1)S(1)} %get-tuple-element.129.refs_2_.refs_4_, ...), custom_call_target="tpu_custom_call", output_to_operand_aliasing={{0}: (6, {})} | custom-call | flops 402653184 | bytes 6291456 | tf_op jit(solution)/shard_map/pallas_call | solution.py:175
  74.7 6.0 %shard_map.302 = (bf16[3,512,4096]{2,1,0:T(8,128)(2,1)}, f32[3,512,128]{2,1,0:T(8,128)S(1)}) custom-call(s32[8]{0:T(128)S(1)} %get-tuple-element.126.refs_0_, s32[128]{0:T(128)S(1)} %reshape.59.refs_1_, bf16[3,512,64]{2,1,0:T(8,128)(2,1)S(1)} %get-tuple-element.129.refs_2_.refs_4_, ...), custom_call_target="tpu_custom_call", output_to_operand_aliasing={{0}: (6, {})} | custom-call | flops 402653184 | bytes 6291456 | tf_op jit(solution)/shard_map/pallas_call | solution.py:175
  82.2 3.2 %collective-permute-start.19 = (bf16[1,192,512]{2,1,0:T(8,128)(2,1)S(1)}, bf16[1,192,512]{2,1,0:T(8,128)(2,1)S(1)}, u32[]{:S(2)}, u32[]{:S(2)}) collective-permute-start(bf16[1,192,512]{2,1,0:T(8,128)(2,1)S(1)} %slice.43), channel_id=1, source_target_pairs={{8,0},{16,8},{24,16},{28,24},{20,28},{12,20},{4,12},{0,4},{9,1},{1... | collective-permute-start | bytes 589832 | tf_op jit(solution)/shard_map/ppermute | solution.py:611
  85.4 3.0 %shard_map.303 = (bf16[3,512,4096]{2,1,0:T(8,128)(2,1)}, f32[3,512,128]{2,1,0:T(8,128)S(1)}) custom-call(s32[8]{0:T(128)S(1)} %get-tuple-element.126.refs_0_, s32[128]{0:T(128)S(1)} %reshape.59.refs_1_, bf16[3,512,64]{2,1,0:T(8,128)(2,1)S(1)} %get-tuple-element.129.refs_2_.refs_4_, ...), custom_call_target="tpu_custom_call", output_to_operand_aliasing={{0}: (6, {})} | custom-call | flops 402653184 | bytes 6291456 | tf_op jit(solution)/shard_map/pallas_call | solution.py:175
  88.9 4.6 %collective-permute-done.18.refs_3_.refs_7_ = bf16[1,192,512]{2,1,0:T(8,128)(2,1)S(1)} collective-permute-done((bf16[1,192,512]{2,1,0:T(8,128)(2,1)S(1)}, bf16[1,192,512]{2,1,0:T(8,128)(2,1)S(1)}, u32[]{:S(2)}, u32[]{:S(2)}) %collective-permute-start.18) | collective-permute-done | bytes 196640 | tf_op jit(solution)/shard_map/ppermute | solution.py:608
  94.2 2.7 %shard_map.304 = (bf16[3,512,4096]{2,1,0:T(8,128)(2,1)}, bf16[192,512]{1,0:T(8,128)(2,1)S(1)}, f32[3,512,128]{2,1,0:T(8,128)S(1)}) custom-call(s32[8]{0:T(128)S(1)} %get-tuple-element.126.refs_0_, s32[128]{0:T(128)S(1)} %reshape.59.refs_1_, bf16[3,512,64]{2,1,0:T(8,128)(2,1)S(1)} %get-tuple-element.129.refs_2_.refs_4_, ...), custom_call_target="tpu_custom_call", output_to_operand_aliasing={{0}: (6, {})} | custom-call | flops 201326592 | bytes 3145728 | tf_op jit(solution)/shard_map/pallas_call | solution.py:175
  97.9 7.4 %all_gather.9.mixed_ref = bf16[768,512]{1,0:T(8,128)(2,1)S(1)} all-gather(bf16[192,512]{1,0:T(8,128)(2,1)S(1)} %get-tuple-element.148.mixed_ref), channel_id=1, replica_groups=mesh['dp'=8,'tensor'=4] {'tensor'}, dimensions={0}, use_global_device_ids=true | all-gather | bytes 983040 | tf_op jit(solution)/shard_map/all_gather | solution.py:780
  105.5 5.7 %shard_map.305 = (bf16[512,768]{1,0:T(8,128)(2,1)S(1)}, bf16[512,768]{1,0:T(8,128)(2,1)S(1)}, f32[512,768]{1,0:T(8,128)S(1)}, f32[256,768]{1,0:T(8,128)S(1)}, f3...) custom-call(s32[9]{0:T(128)S(1)} %pad_add_fusion.s_ref, ...), custom_call_target="tpu_custom_call" | custom-call | bytes 1048576 | tf_op jit(solution)/shard_map/pallas_call | solution.py:339
  115.0 9.6 %collective-permute-done.24.b_ref = bf16[256,768]{1,0:T(8,128)(2,1)S(1)} collective-permute-done((bf16[256,768]{1,0:T(8,128)(2,1)S(1)}, bf16[256,768]{1,0:T(8,128)(2,1)S(1)}, u32[]{:S(2)}, u32[]{:S(2)}) %collective-permute-start.24) | collective-permute-done | bytes 393248 | tf_op jit(solution)/shard_map/ppermute | solution.py:669
  124.6 2.7 %shard_map.306 = (bf16[128,768]{1,0:T(8,128)(2,1)}, f32[256,768]{1,0:T(8,128)S(1)}, bf16[256,768]{1,0:T(8,128)(2,1)S(1)}, f32[2,768]{1,0:T(2,128)S(1)}) custom-call(s32[9]{0:T(128)S(1)} %pad_add_fusion.s_ref, bf16[256,768]{1,0:T(8,128)(2,1)S(1)} %add_convert_fusion.2.a_ref, bf16[256,768]{1,0:T(8,128)(2,1)S(1)} %collective-permute-done.24.b_ref, ...), custom_call_target="tpu_custom_call" | custom-call | bytes 1048576 | tf_op jit(solution)/shard_map/pallas_call | solution.py:339
  129.0 3.5 %shard_map.307 = (bf16[512,768]{1,0:T(8,128)(2,1)S(1)}, bf16[512,768]{1,0:T(8,128)(2,1)S(1)}, f32[1,768]{1,0:T(1,128)S(1)}, bf16[256,768]{1,0:T(8,128)(2,1)S(1)}, bf16[256,768]{1,0:T(8,128)(2,1)S(1)}) custom-call(s32[9]{0:T(128)S(1)} %pad_add_fusion.s_ref, bf16[256,768]{1,0:T(8,128)(2,1)S(1)} %get-tuple-element.164.low_ref, ...), custom_call_target="tpu_custom_call" | custom-call | bytes 1048576 | tf_op jit(solution)/shard_map/pallas_call | solution.py:339
  132.5 3.5 %shard_map.308 = bf16[768,1536]{1,0:T(8,128)(2,1)} custom-call(s32[9]{0:T(128)S(1)} %pad_add_fusion.s_ref, bf16[512,768]{1,0:T(8,128)(2,1)S(1)} %get-tuple-element.168.active_ref, bf16[512,768]{1,0:T(8,128)(2,1)S(1)} %get-tuple-element.169.second_ref, bf16[512,768]{1,0:T(8,128)(2,1)S(1)} %get-tuple-element.170.low_ref, ...), custom_call_target="tpu_custom_call" | custom-call | bytes 1048576 | tf_op jit(solution)/shard_map/pallas_call | solution.py:339
  139.7 9.4 %collective-permute-done.27.b_ref = bf16[256,768]{1,0:T(8,128)(2,1)S(1)} collective-permute-done((bf16[256,768]{1,0:T(8,128)(2,1)S(1)}, bf16[256,768]{1,0:T(8,128)(2,1)S(1)}, u32[]{:S(2)}, u32[]{:S(2)}) %collective-permute-start.27) | collective-permute-done | bytes 393248 | tf_op jit(solution)/shard_map/ppermute | solution.py:669
  155.0 2.6 shard_map.311
  158.8 5.4 %collective-permute-start.33 = (bf16[1,192,512]{2,1,0:T(8,128)(2,1)S(1)}, bf16[1,192,512]{2,1,0:T(8,128)(2,1)S(1)}, u32[]{:S(2)}, u32[]{:S(2)}) collective-permute-start(bf16[1,192,512]{2,1,0:T(8,128)(2,1)S(1)} %get-tuple-element.203), channel_id=1, source_target_pairs={{8,0},{16,8},{24,16},{28,24},{20,28},{12,20},{4,12},{0,4},{9,1},{1... | collective-permute-start | bytes 589832 | tf_op jit(solution)/shard_map/ppermute | solution.py:611
  166.2 3.4 %shard_map.312 = (bf16[3,512,4096]{2,1,0:T(8,128)(2,1)}, bf16[2,192,512]{2,1,0:T(8,128)(2,1)S(1)}, bf16[2,192,512]{2,1,0:T(8,128)(2,1)S(1)}, f32[3,512,64]{2,1,0:T(8,128)S(1)}) custom-call(s32[8]{0:T(128)S(1)} %get-tuple-element.126.refs_0_, s32[128]{0:T(128)S(1)} %reshape.59.refs_1_, ...), custom_call_target="tpu_custom_call", output_to_operand_aliasing={{0}: (11, {})} | custom-call | flops 1006632960 | bytes 9437184 | tf_op jit(solution)/shard_map/pallas_call | solution.py:311
  169.9 5.2 %collective-permute-done.33.down_ref = bf16[1,192,512]{2,1,0:T(8,128)(2,1)S(1)} collective-permute-done((bf16[1,192,512]{2,1,0:T(8,128)(2,1)S(1)}, bf16[1,192,512]{2,1,0:T(8,128)(2,1)S(1)}, u32[]{:S(2)}, u32[]{:S(2)}) %collective-permute-start.33) | collective-permute-done | bytes 196640 | tf_op jit(solution)/shard_map/ppermute | solution.py:611
  175.8 2.5 collective-permute-start.34
  180.2 6.9 %shard_map.313 = (bf16[3,512,4096]{2,1,0:T(8,128)(2,1)}, bf16[2,192,512]{2,1,0:T(8,128)(2,1)S(1)}, bf16[2,192,512]{2,1,0:T(8,128)(2,1)S(1)}, f32[3,512,64]{2,1,0:T(8,128)S(1)}) custom-call(s32[8]{0:T(128)S(1)} %get-tuple-element.126.refs_0_, s32[128]{0:T(128)S(1)} %reshape.59.refs_1_, ...), custom_call_target="tpu_custom_call", output_to_operand_aliasing={{0}: (11, {})} | custom-call | flops 1006632960 | bytes 9437184 | tf_op jit(solution)/shard_map/pallas_call | solution.py:311
  193.1 4.3 %collective-permute-start.31 = (f32[8,768]{1,0:T(8,128)S(1)}, f32[8,768]{1,0:T(8,128)S(1)}, u32[]{:S(2)}, u32[]{:S(2)}) collective-permute-start(f32[8,768]{1,0:T(8,128)S(1)} %add.99), channel_id=1, source_target_pairs={{0,16},{4,20},{8,24},{12,28},{16,0},{20,4},{24,8},{28,12},{1,17},{... | collective-permute-start | bytes 73736 | tf_op jit(solution)/shard_map/ppermute | solution.py:869
  197.4 9.4 %shard_map.314 = (bf16[3,512,4096]{2,1,0:T(8,128)(2,1)}, bf16[2,192,512]{2,1,0:T(8,128)(2,1)S(1)}, bf16[2,192,512]{2,1,0:T(8,128)(2,1)S(1)}, f32[3,512,64]{2,1,0:T(8,128)S(1)}) custom-call(s32[8]{0:T(128)S(1)} %get-tuple-element.126.refs_0_, s32[128]{0:T(128)S(1)} %reshape.59.refs_1_, ...), custom_call_target="tpu_custom_call", output_to_operand_aliasing={{0}: (11, {})} | custom-call | flops 1006632960 | bytes 9437184 | tf_op jit(solution)/shard_map/pallas_call | solution.py:311
  206.9 5.6 %collective-permute-done.31 = f32[8,768]{1,0:T(8,128)S(1)} collective-permute-done((f32[8,768]{1,0:T(8,128)S(1)}, f32[8,768]{1,0:T(8,128)S(1)}, u32[]{:S(2)}, u32[]{:S(2)}) %collective-permute-start.31) | collective-permute-done | bytes 24608 | tf_op jit(solution)/shard_map/ppermute | solution.py:869
  215.3 6.2 %shard_map.315 = (bf16[3,512,4096]{2,1,0:T(8,128)(2,1)}, bf16[2,192,512]{2,1,0:T(8,128)(2,1)S(1)}, bf16[192,512]{1,0:T(8,128)(2,1)S(1)}) custom-call(s32[8]{0:T(128)S(1)} %get-tuple-element.126.refs_0_, s32[128]{0:T(128)S(1)} %reshape.59.refs_1_, bf16[192,512]{1,0:T(8,128)(2,1)S(1)} %get-tuple-element.132.refs_2_, ...), custom_call_target="tpu_custom_call", output_to_operand_aliasing={{0}: (10, {})} | custom-call | flops 503316480 | bytes 4718592 | tf_op jit(solution)/shard_map/pallas_call | solution.py:311
  222.7 2.8 %shard_map.319 = (bf16[48,768]{1,0:T(8,128)(2,1)S(1)}, bf16[48,768]{1,0:T(8,128)(2,1)S(1)}, bf16[96,768]{1,0:T(8,128)(2,1)S(1)}, bf16[96,768]{1,0:T(8,128)(2,1)S...) custom-call(s32[9]{0:T(128)S(1)} %pad_add_fusion.s_ref, ...), custom_call_target="tpu_custom_call" | custom-call | bytes 1048576 | tf_op jit(solution)/shard_map/pallas_call | solution.py:339
  227.6 2.3 collective-permute-done.42.up_ref
  243.9 3.8 %collective-permute-done.41 = bf16[128,768]{1,0:T(8,128)(2,1)S(1)} collective-permute-done((bf16[128,768]{1,0:T(8,128)(2,1)S(1)}, bf16[128,768]{1,0:T(8,128)(2,1)S(1)}, u32[]{:S(2)}, u32[]{:S(2)}) %collective-permute-start.41) | collective-permute-done | bytes 196640 | tf_op jit(solution)/shard_map/ppermute | solution.py:669
  251.3 2.3 collective-permute-done.48.up_ref
  (195 shorter events, 92.2 us)
Async XLA Ops:
  7.2 98.1 %all-gather.5.cloned.1.call-start = ((), (), s32[]{:S(2)}) async-start(), calls=%async_computation.2 | async-start | bytes 1327104 | tf_op jit(solution)/shard_map/all_gather | solution.py:723
  7.9 97.6 %all-gather.3.cloned.1.call-start = ((), (), s32[]{:S(2)}) async-start(), calls=%async_computation.1 | async-start | bytes 1548288 | tf_op jit(solution)/shard_map/all_gather | solution.py:737
  9.0 7.6 %collective-permute-start.1 = (bf16[96,768]{1,0:T(8,128)(2,1)S(1)}, bf16[96,768]{1,0:T(8,128)(2,1)S(1)}, u32[]{:S(2)}, u32[]{:S(2)}) collective-permute-start(bf16[96,768]{1,0:T(8,128)(2,1)S(1)} %shard_map.298.refs_0_), channel_id=1, source_target_pairs={{8,0},{16,8},{24,16},{28,24},{20,28},{12,20},{4,12},{0,4},{9,1},{1... | collective-permute-start | bytes 442376 | tf_op jit(solution)/shard_map/ppermute | solution.py:611
  12.2 16.6 %collective-permute-start.8 = (bf16[128,768]{1,0:T(8,128)(2,1)}, bf16[128,768]{1,0:T(8,128)(2,1)S(1)}, u32[]{:S(2)}, u32[]{:S(2)}) collective-permute-start(bf16[128,768]{1,0:T(8,128)(2,1)} %refs_9_.1), channel_id=1, source_target_pairs={{0,1},{1,0},{2,3},{3,2},{4,5},{5,4},{6,7},{7,6},{8,9},{9,8},{10,11... | collective-permute-start | bytes 589832 | tf_op jit(solution)/shard_map/ppermute | solution.py:666
  12.2 20.2 %collective-permute-start.9 = (bf16[128,768]{1,0:T(8,128)(2,1)}, bf16[128,768]{1,0:T(8,128)(2,1)S(1)}, u32[]{:S(2)}, u32[]{:S(2)}) collective-permute-start(bf16[128,768]{1,0:T(8,128)(2,1)} %refs_9_.1), channel_id=1, source_target_pairs={{0,2},{1,3},{2,0},{3,1},{4,6},{5,7},{6,4},{7,5},{8,10},{9,11},{10,... | collective-permute-start | bytes 589832 | tf_op jit(solution)/shard_map/ppermute | solution.py:669
  21.2 220.9 %reduce-scatter.2.cloned.1.call-start = ((), (), s32[]{:S(2)}) async-start(), calls=%async_computation.3 | async-start | bytes 2654208 | tf_op jit(solution)/shard_map/reduce_scatter | solution.py:829
  22.7 7.4 %collective-permute-start.5 = (bf16[96,768]{1,0:T(8,128)(2,1)S(1)}, bf16[96,768]{1,0:T(8,128)(2,1)S(1)}, u32[]{:S(2)}, u32[]{:S(2)}) collective-permute-start(bf16[96,768]{1,0:T(8,128)(2,1)S(1)} %collective-permute-done.3.refs_4_), channel_id=1, source_target_pairs={{8,0},{16,8},{24,16},{28,24},{20,28},{12,20},{4,12},{0,4},{9,1},{1... | collective-permute-start | bytes 442376 | tf_op jit(solution)/shard_map/ppermute | solution.py:611
  39.3 16.9 %collective-permute-start.12 = (bf16[2,192,512]{2,1,0:T(8,128)(2,1)S(1)}, bf16[2,192,512]{2,1,0:T(8,128)(2,1)S(1)}, u32[]{:S(2)}, u32[]{:S(2)}) collective-permute-start(bf16[2,192,512]{2,1,0:T(8,128)(2,1)S(1)} %get-tuple-element.130.refs_3_.refs_7_), channel_id=1, source_target_pairs={{8,0},{16,8},{24,16},{28,24},{20,28},{12,20},{4,12},{0,4},{9,1},{1... | collective-permute-start | bytes 1179656 | tf_op jit(solution)/shard_map/ppermute | solution.py:611
  41.4 14.8 %collective-permute-start.11 = (bf16[2,192,512]{2,1,0:T(8,128)(2,1)S(1)}, bf16[2,192,512]{2,1,0:T(8,128)(2,1)S(1)}, u32[]{:S(2)}, u32[]{:S(2)}) collective-permute-start(bf16[2,192,512]{2,1,0:T(8,128)(2,1)S(1)} %get-tuple-element.130.refs_3_.refs_7_), channel_id=1, source_target_pairs={{0,8},{8,16},{16,24},{24,28},{28,20},{20,12},{12,4},{4,0},{1,9},{9... | collective-permute-start | bytes 1179656 | tf_op jit(solution)/shard_map/ppermute | solution.py:608
  56.3 12.5 %collective-permute-start.14 = (bf16[2,192,512]{2,1,0:T(8,128)(2,1)S(1)}, bf16[2,192,512]{2,1,0:T(8,128)(2,1)S(1)}, u32[]{:S(2)}, u32[]{:S(2)}) collective-permute-start(bf16[2,192,512]{2,1,0:T(8,128)(2,1)S(1)} %collective-permute-done.11.refs_3_.refs_7_), channel_id=1, source_target_pairs={{0,8},{8,16},{16,24},{24,28},{28,20},{20,12},{12,4},{4,0},{1,9},{9... | collective-permute-start | bytes 1179656 | tf_op jit(solution)/shard_map/ppermute | solution.py:608
  57.4 11.4 %collective-permute-start.15 = (bf16[2,192,512]{2,1,0:T(8,128)(2,1)S(1)}, bf16[2,192,512]{2,1,0:T(8,128)(2,1)S(1)}, u32[]{:S(2)}, u32[]{:S(2)}) collective-permute-start(bf16[2,192,512]{2,1,0:T(8,128)(2,1)S(1)} %collective-permute-done.12.refs_4_.refs_8_), channel_id=1, source_target_pairs={{8,0},{16,8},{24,16},{28,24},{20,28},{12,20},{4,12},{0,4},{9,1},{1... | collective-permute-start | bytes 1179656 | tf_op jit(solution)/shard_map/ppermute | solution.py:611
  68.8 11.9 %collective-permute-start.16 = (bf16[2,192,512]{2,1,0:T(8,128)(2,1)S(1)}, bf16[2,192,512]{2,1,0:T(8,128)(2,1)S(1)}, u32[]{:S(2)}, u32[]{:S(2)}) collective-permute-start(bf16[2,192,512]{2,1,0:T(8,128)(2,1)S(1)} %collective-permute-done.14.refs_3_.refs_7_), channel_id=1, source_target_pairs={{0,8},{8,16},{16,24},{24,28},{28,20},{20,12},{12,4},{4,0},{1,9},{9... | collective-permute-start | bytes 1179656 | tf_op jit(solution)/shard_map/ppermute | solution.py:608
  68.9 13.3 %collective-permute-start.17 = (bf16[2,192,512]{2,1,0:T(8,128)(2,1)S(1)}, bf16[2,192,512]{2,1,0:T(8,128)(2,1)S(1)}, u32[]{:S(2)}, u32[]{:S(2)}) collective-permute-start(bf16[2,192,512]{2,1,0:T(8,128)(2,1)S(1)} %collective-permute-done.15.refs_4_.refs_8_), channel_id=1, source_target_pairs={{8,0},{16,8},{24,16},{28,24},{20,28},{12,20},{4,12},{0,4},{9,1},{1... | collective-permute-start | bytes 1179656 | tf_op jit(solution)/shard_map/ppermute | solution.py:611
  72.6 25.3 %collective-permute-start.22 = (bf16[192,768]{1,0:T(8,128)(2,1)S(1)}, bf16[192,768]{1,0:T(8,128)(2,1)S(1)}, u32[]{:S(2)}, u32[]{:S(2)}) collective-permute-start(bf16[192,768]{1,0:T(8,128)(2,1)S(1)} %collective-permute-done.20.o1), channel_id=1, source_target_pairs={{0,2},{1,3},{2,0},{3,1},{4,6},{5,7},{6,4},{7,5},{8,10},{9,11},{10,... | collective-permute-start | bytes 884744 | tf_op jit(solution)/shard_map/ppermute | solution.py:669
  73.7 24.2 %collective-permute-start.21 = (bf16[192,768]{1,0:T(8,128)(2,1)S(1)}, bf16[192,768]{1,0:T(8,128)(2,1)}, u32[]{:S(2)}, u32[]{:S(2)}) collective-permute-start(bf16[192,768]{1,0:T(8,128)(2,1)S(1)} %slice.44.o0.o_ref), channel_id=1, source_target_pairs={{0,2},{1,3},{2,0},{3,1},{4,6},{5,7},{6,4},{7,5},{8,10},{9,11},{10,... | collective-permute-start | bytes 884744 | tf_op jit(solution)/shard_map/ppermute | solution.py:669
  82.2 6.7 %collective-permute-start.19 = (bf16[1,192,512]{2,1,0:T(8,128)(2,1)S(1)}, bf16[1,192,512]{2,1,0:T(8,128)(2,1)S(1)}, u32[]{:S(2)}, u32[]{:S(2)}) collective-permute-start(bf16[1,192,512]{2,1,0:T(8,128)(2,1)S(1)} %slice.43), channel_id=1, source_target_pairs={{8,0},{16,8},{24,16},{28,24},{20,28},{12,20},{4,12},{0,4},{9,1},{1... | collective-permute-start | bytes 589832 | tf_op jit(solution)/shard_map/ppermute | solution.py:611
  85.4 8.1 %collective-permute-start.18 = (bf16[1,192,512]{2,1,0:T(8,128)(2,1)S(1)}, bf16[1,192,512]{2,1,0:T(8,128)(2,1)S(1)}, u32[]{:S(2)}, u32[]{:S(2)}) collective-permute-start(bf16[1,192,512]{2,1,0:T(8,128)(2,1)S(1)} %slice.42), channel_id=1, source_target_pairs={{0,8},{8,16},{16,24},{24,28},{28,20},{20,12},{12,4},{4,0},{1,9},{9... | collective-permute-start | bytes 589832 | tf_op jit(solution)/shard_map/ppermute | solution.py:608
  113.1 11.4 %collective-permute-start.24 = (bf16[256,768]{1,0:T(8,128)(2,1)S(1)}, bf16[256,768]{1,0:T(8,128)(2,1)S(1)}, u32[]{:S(2)}, u32[]{:S(2)}) collective-permute-start(bf16[256,768]{1,0:T(8,128)(2,1)S(1)} %add_convert_fusion.2.a_ref), channel_id=1, source_target_pairs={{0,2},{1,3},{2,0},{3,1},{4,6},{5,7},{6,4},{7,5},{8,10},{9,11},{10,... | collective-permute-start | bytes 1179656 | tf_op jit(solution)/shard_map/ppermute | solution.py:669
  137.9 11.2 %collective-permute-start.27 = (bf16[256,768]{1,0:T(8,128)(2,1)S(1)}, bf16[256,768]{1,0:T(8,128)(2,1)S(1)}, u32[]{:S(2)}, u32[]{:S(2)}) collective-permute-start(bf16[256,768]{1,0:T(8,128)(2,1)S(1)} %add_convert_fusion.1.a_ref), channel_id=1, source_target_pairs={{0,2},{1,3},{2,0},{3,1},{4,6},{5,7},{6,4},{7,5},{8,10},{9,11},{10,... | collective-permute-start | bytes 1179656 | tf_op jit(solution)/shard_map/ppermute | solution.py:669
  157.6 12.3 %collective-permute-start.32 = (bf16[1,192,512]{2,1,0:T(8,128)(2,1)S(1)}, bf16[1,192,512]{2,1,0:T(8,128)(2,1)S(1)}, u32[]{:S(2)}, u32[]{:S(2)}) collective-permute-start(bf16[1,192,512]{2,1,0:T(8,128)(2,1)S(1)} %get-tuple-element.202), channel_id=1, source_target_pairs={{0,8},{8,16},{16,24},{24,28},{28,20},{20,12},{12,4},{4,0},{1,9},{9... | collective-permute-start | bytes 589832 | tf_op jit(solution)/shard_map/ppermute | solution.py:608
  158.8 16.3 %collective-permute-start.33 = (bf16[1,192,512]{2,1,0:T(8,128)(2,1)S(1)}, bf16[1,192,512]{2,1,0:T(8,128)(2,1)S(1)}, u32[]{:S(2)}, u32[]{:S(2)}) collective-permute-start(bf16[1,192,512]{2,1,0:T(8,128)(2,1)S(1)} %get-tuple-element.203), channel_id=1, source_target_pairs={{8,0},{16,8},{24,16},{28,24},{20,28},{12,20},{4,12},{0,4},{9,1},{1... | collective-permute-start | bytes 589832 | tf_op jit(solution)/shard_map/ppermute | solution.py:611
  175.8 14.4 %collective-permute-start.34 = (bf16[2,192,512]{2,1,0:T(8,128)(2,1)S(1)}, bf16[2,192,512]{2,1,0:T(8,128)(2,1)S(1)}, u32[]{:S(2)}, u32[]{:S(2)}) collective-permute-start(bf16[2,192,512]{2,1,0:T(8,128)(2,1)S(1)} %get-tuple-element.204), channel_id=1, source_target_pairs={{0,8},{8,16},{16,24},{24,28},{28,20},{20,12},{12,4},{4,0},{1,9},{9... | collective-permute-start | bytes 1179656 | tf_op jit(solution)/shard_map/ppermute | solution.py:608
  178.2 11.9 %collective-permute-start.35 = (bf16[2,192,512]{2,1,0:T(8,128)(2,1)S(1)}, bf16[2,192,512]{2,1,0:T(8,128)(2,1)S(1)}, u32[]{:S(2)}, u32[]{:S(2)}) collective-permute-start(bf16[2,192,512]{2,1,0:T(8,128)(2,1)S(1)} %get-tuple-element.205), channel_id=1, source_target_pairs={{8,0},{16,8},{24,16},{28,24},{20,28},{12,20},{4,12},{0,4},{9,1},{1... | collective-permute-start | bytes 1179656 | tf_op jit(solution)/shard_map/ppermute | solution.py:611
  178.2 10.7 %collective-permute-start.30 = (f32[8,768]{1,0:T(8,128)S(1)}, f32[8,768]{1,0:T(8,128)S(1)}, u32[]{:S(2)}, u32[]{:S(2)}) collective-permute-start(f32[8,768]{1,0:T(8,128)S(1)} %add.98), channel_id=1, source_target_pairs={{0,8},{4,12},{8,0},{12,4},{16,24},{20,28},{24,16},{28,20},{1,9},{5... | collective-permute-start | bytes 73736 | tf_op jit(solution)/shard_map/ppermute | solution.py:869
  190.9 21.6 %collective-permute-start.36 = (bf16[2,192,512]{2,1,0:T(8,128)(2,1)S(1)}, bf16[2,192,512]{2,1,0:T(8,128)(2,1)S(1)}, u32[]{:S(2)}, u32[]{:S(2)}) collective-permute-start(bf16[2,192,512]{2,1,0:T(8,128)(2,1)S(1)} %get-tuple-element.206), channel_id=1, source_target_pairs={{0,8},{8,16},{16,24},{24,28},{28,20},{20,12},{12,4},{4,0},{1,9},{9... | collective-permute-start | bytes 1179656 | tf_op jit(solution)/shard_map/ppermute | solution.py:608
  192.7 19.8 %collective-permute-start.37 = (bf16[2,192,512]{2,1,0:T(8,128)(2,1)S(1)}, bf16[2,192,512]{2,1,0:T(8,128)(2,1)S(1)}, u32[]{:S(2)}, u32[]{:S(2)}) collective-permute-start(bf16[2,192,512]{2,1,0:T(8,128)(2,1)S(1)} %get-tuple-element.207), channel_id=1, source_target_pairs={{8,0},{16,8},{24,16},{28,24},{20,28},{12,20},{4,12},{0,4},{9,1},{1... | collective-permute-start | bytes 1179656 | tf_op jit(solution)/shard_map/ppermute | solution.py:611
  193.1 19.3 %collective-permute-start.31 = (f32[8,768]{1,0:T(8,128)S(1)}, f32[8,768]{1,0:T(8,128)S(1)}, u32[]{:S(2)}, u32[]{:S(2)}) collective-permute-start(f32[8,768]{1,0:T(8,128)S(1)} %add.99), channel_id=1, source_target_pairs={{0,16},{4,20},{8,24},{12,28},{16,0},{20,4},{24,8},{28,12},{1,17},{... | collective-permute-start | bytes 73736 | tf_op jit(solution)/shard_map/ppermute | solution.py:869
  213.2 8.3 %collective-permute-start.38 = (bf16[2,192,512]{2,1,0:T(8,128)(2,1)S(1)}, bf16[2,192,512]{2,1,0:T(8,128)(2,1)S(1)}, u32[]{:S(2)}, u32[]{:S(2)}) collective-permute-start(bf16[2,192,512]{2,1,0:T(8,128)(2,1)S(1)} %get-tuple-element.208), channel_id=1, source_target_pairs={{0,8},{8,16},{16,24},{24,28},{28,20},{20,12},{12,4},{4,0},{1,9},{9... | collective-permute-start | bytes 1179656 | tf_op jit(solution)/shard_map/ppermute | solution.py:608
  214.7 7.9 %collective-permute-start.39 = (bf16[2,192,512]{2,1,0:T(8,128)(2,1)S(1)}, bf16[2,192,512]{2,1,0:T(8,128)(2,1)S(1)}, u32[]{:S(2)}, u32[]{:S(2)}) collective-permute-start(bf16[2,192,512]{2,1,0:T(8,128)(2,1)S(1)} %get-tuple-element.209), channel_id=1, source_target_pairs={{8,0},{16,8},{24,16},{28,24},{20,28},{12,20},{4,12},{0,4},{9,1},{1... | collective-permute-start | bytes 1179656 | tf_op jit(solution)/shard_map/ppermute | solution.py:611
  227.6 14.2 %collective-permute-start.40 = (bf16[256,768]{1,0:T(8,128)(2,1)S(1)}, bf16[256,768]{1,0:T(8,128)(2,1)S(1)}, u32[]{:S(2)}, u32[]{:S(2)}) collective-permute-start(bf16[256,768]{1,0:T(8,128)(2,1)S(1)} %get-tuple-element.213), channel_id=1, source_target_pairs={{0,1},{1,0},{2,3},{3,2},{4,5},{5,4},{6,7},{7,6},{8,9},{9,8},{10,11... | collective-permute-start | bytes 1179656 | tf_op jit(solution)/shard_map/ppermute | solution.py:666
  239.8 8.0 %collective-permute-start.46 = (bf16[96,768]{1,0:T(8,128)(2,1)S(1)}, bf16[96,768]{1,0:T(8,128)(2,1)S(1)}, u32[]{:S(2)}, u32[]{:S(2)}) collective-permute-start(bf16[96,768]{1,0:T(8,128)(2,1)S(1)} %get-tuple-element.227), channel_id=1, source_target_pairs={{0,8},{8,16},{16,24},{24,28},{28,20},{20,12},{12,4},{4,0},{1,9},{9... | collective-permute-start | bytes 442376 | tf_op jit(solution)/shard_map/ppermute | solution.py:608
  240.0 7.7 %collective-permute-start.47 = (bf16[96,768]{1,0:T(8,128)(2,1)S(1)}, bf16[96,768]{1,0:T(8,128)(2,1)S(1)}, u32[]{:S(2)}, u32[]{:S(2)}) collective-permute-start(bf16[96,768]{1,0:T(8,128)(2,1)S(1)} %get-tuple-element.228), channel_id=1, source_target_pairs={{8,0},{16,8},{24,16},{28,24},{20,28},{12,20},{4,12},{0,4},{9,1},{1... | collective-permute-start | bytes 442376 | tf_op jit(solution)/shard_map/ppermute | solution.py:611
  (51 other events, 477.2 us)
Sparse Core Ops, SparseCore 0:
  10.2 48.7 all-gather.4
  61.2 44.2 all-gather.2
  136.1 82.9 reduce-scatter.1
